TPU v7x, 256 devices: a whole 4x4x8 slice. The times are simulated.
256 devices in a mesh: tm: 32 (over x, y, core), space: 8 (over z).
Axes of the slice: x: 4, y: 4, z: 8, core: 2. Of those that a mesh axis runs over, the one named last changes fastest.
Arguments:
- snapshots: bfloat16 [512, 524288], P('tm', 'space'), may hold values from -6 to 6
- block_lists: int32 [8192, 2], P(('tm', 'space')), may hold values from 0 to 8191
- tile_counts: int32 [8192], P(('tm', 'space')), may hold values from 1 to 2
- remap_weights: bfloat16 [8192, 64, 128], P(('tm', 'space')), may hold values from -0.5 to 0.5
- basis: bfloat16 [524288, 1024], P(('tm', 'space')), may hold values from -6 to 6
- variances: float32 [1024], replicated, may hold values from 0.3 to 3
Outputs:
- coeffs: float32 [1024, 512], P('space')
- rotated: bfloat16 [524288, 1024], P(('tm', 'space'))
Inputs may be any that keep to these rules, and one draw needn't show every extreme that they name: `block_lists`: slots at or beyond a tile's count carry no weight.
All inputs are finite; a program needn't handle non-finite values.
Results may differ from a plain program's by a relative error of at most 0.0043.
Values may be sent and summed in bfloat16 or wider, within the bound.
No kernel may reach another device: no remote copies, remote signals or barrier semaphores. Data moves between devices by JAX's collectives and lax.ppermute only.
A program may use at most 192 MiB of HBM per device.

v0:
```python
import math

import jax
import jax.numpy as jnp
from jax import lax
from jax.sharding import PartitionSpec as P

TILE = 64
MAXB = 2


def per_device(snapshots, block_lists, tile_counts, remap_weights, basis, variances):
    local_tiles = block_lists.shape[0]
    time_rows = snapshots.shape[0]
    tm_size = lax.axis_size("tm")
    list_column, count_column = (
        lax.all_gather(block_lists, "tm", axis=0, tiled=True),
        lax.all_gather(tile_counts, "tm", axis=0, tiled=True),
    )
    gathered = lax.all_gather(snapshots, "space", axis=1, tiled=True)
    cell_total = gathered.shape[1]
    blocks = gathered.reshape(time_rows, cell_total // TILE, TILE)
    picked = blocks[:, list_column.reshape(-1), :].reshape(
        time_rows, tm_size * local_tiles, MAXB * TILE
    )
    slot_index = jnp.arange(MAXB * TILE, dtype=jnp.int32) // TILE
    weight_column = lax.all_gather(remap_weights, "tm", axis=0, tiled=True)
    keep = slot_index[None, :] < count_column[:, None]
    masked = jnp.where(keep[:, None, :], weight_column, jnp.zeros_like(weight_column))
    remap_part = jnp.einsum("kip,tkp->kit", masked, picked, preferred_element_type=jnp.float32)
    remap_part = remap_part.astype(jnp.bfloat16).reshape(tm_size, local_tiles * TILE, time_rows)
    arrived = lax.all_to_all(remap_part, "tm", split_axis=0, concat_axis=2, tiled=True)
    remapped = arrived.reshape(local_tiles * TILE, tm_size * time_rows)
    snap_total = remapped.shape[1]
    partial_coeffs = lax.dot_general(
        basis, remapped, (((0,), (0,)), ((), ())), preferred_element_type=jnp.float32
    )
    coeffs = lax.psum(partial_coeffs, ("tm", "space")) / math.sqrt(cell_total)
    coeff_half = coeffs.astype(jnp.bfloat16)
    coeff_rows = coeffs.shape[0] // lax.axis_size("space")
    own_coeffs = lax.dynamic_slice_in_dim(
        coeffs, lax.axis_index("space") * coeff_rows, coeff_rows, 0
    )
    update = lax.dot_general(
        remapped, coeff_half, (((1,), (1,)), ((), ())), preferred_element_type=jnp.float32
    ) / math.sqrt(snap_total)
    rotated = (basis.astype(jnp.float32) * variances[None, :] + update).astype(jnp.bfloat16)
    return (own_coeffs, rotated)


def solution(mesh):
    return jax.shard_map(
        per_device,
        mesh=mesh,
        in_specs=(
            P("tm", "space"),
            P(("tm", "space"), None),
            P(("tm", "space")),
            P(("tm", "space"), None, None),
            P(("tm", "space"), None),
            P(),
        ),
        out_specs=(P("space", None), P(("tm", "space"), None)),
        check_vma=False,
    )
```

profile of v0, /device:TPU:1, one launch (start us, length us, event | category | flops | bytes accessed | tf_op | source)
XLA Modules:
  0.0 670.7 jit_solution(16009837492111305055)
XLA Ops:
  7.2 0.0 all-gather.6.cloned.1.call-start
  7.2 0.7 all-gather.6.cloned.1.call-update
  7.9 0.0 all-gather.4.cloned.1.call-start
  7.9 0.7 all-gather.4.cloned.1.call-update
  8.6 0.0 all-reduce.3.cloned.1.call-start
  8.7 25.9 %all-gather = s32[32,32,2]{1,2,0:T(2,128)S(1)} all-gather(s32[1,32,2]{1,2,0:T(2,128)} %bitcast.20), channel_id=1, replica_groups=mesh['tm'=32,'space'=8] {'tm'}, dimensions={0}, use_global_device_ids=true | all-gather | bytes 8448 | tf_op jit(solution)/shard_map/all_gather | solution.py:17
  34.6 0.3 copy.16
  34.9 0.3 reshape.86
  35.2 1.3 dynamic-slice
  37.1 0.9 dynamic-update-slice
  38.0 11.8 %all-reduce = s32[1024]{0:T(1024)S(1)} all-reduce(s32[1024]{0:T(1024)S(1)} %dynamic-update-slice), channel_id=1, replica_groups=mesh['tm'=32,'space'=8] {'tm'}, use_global_device_ids=true, to_apply=%add | all-reduce | flops 1024 | bytes 8192
  49.8 0.2 broadcast_compare_fusion
  50.0 136.1 %all-gather.6.cloned.1.call-done = bf16[16,524288]{1,0:T(8,128)(2,1)} async-done(((bf16[16,65536]{1,0:T(8,128)(2,1)}), bf16[16,524288]{1,0:T(8,128)(2,1)}) %all-gather.6.cloned.1.call-update) | async-done | bytes 16777232 | tf_op jit(solution)/shard_map/all_gather | solution.py:20
  186.1 60.6 %reshape.85 = bf16[16,8192,64]{2,1,0:T(8,128)(2,1)} reshape(bf16[16,524288]{1,0:T(8,128)(2,1)} %all-gather.6.cloned.1.call-done) | data formatting | bytes 33554432 | tf_op jit(solution)/shard_map/reshape | solution.py:22
  246.8 29.5 %copy.17 = bf16[16,8192,64]{2,0,1:T(8,128)(2,1)} copy(bf16[16,8192,64]{2,1,0:T(8,128)(2,1)} %reshape.85) | data formatting | bytes 33554432 | tf_op jit(solution)/shard_map/reshape | solution.py:22
  276.2 33.4 %gather_fusion = bf16[2048,16,64]{2,1,0:T(8,128)(2,1)} fusion(bf16[16,8192,64]{2,0,1:T(8,128)(2,1)} %copy.17, s32[2048]{0:T(1024)S(1)} %broadcast_clamp_fusion), kind=kCustom, calls=%fused_computation | custom fusion | bytes 8396800 | tf_op jit(solution)/shard_map/gather | solution.py:23
  309.7 8.8 %copy.18 = bf16[16,2048,64]{2,1,0:T(8,128)(2,1)} copy(bf16[16,2048,64]{2,0,1:T(8,128)(2,1)} %bitcast.16) | data formatting | bytes 8388608 | tf_op jit(solution)/shard_map/gather | solution.py:23
  318.4 11.3 %reshape.87 = bf16[16,1024,128]{2,1,0:T(8,128)(2,1)} reshape(bf16[16,2048,64]{2,1,0:T(8,128)(2,1)} %copy.18) | data formatting | bytes 8388608 | tf_op jit(solution)/shard_map/reshape | solution.py:23
  329.7 0.0 all-gather.4.cloned.1.call-done
  329.7 14.3 %fusion.5 = bf16[1024,64,16]{1,2,0:T(8,128)(2,1)} fusion(bf16[16,1024,128]{2,1,0:T(8,128)(2,1)} %reshape.87, bf16[1024,64,128]{2,1,0:T(8,128)(2,1)} %all-gather.4.cloned.1.call-done, pred[1024,128]{1,0:T(8,128)(4,1)S(1)} %broadcast_compare_fusion), kind=kOutput, calls=%fused_computation.7 | convolution fusion | flops 277872640 | bytes 23199744 | tf_op jit(solution)/shard_map/kip,tkp->kit/dot_general | solution.py:30
  344.0 5.3 copy.20
  349.3 5.8 reshape.88
  355.0 0.0 copy-start
  355.0 1.2 copy.21
  356.2 35.4 %all_to_all.15 = bf16[32,2048,16]{1,2,0:T(8,128)(2,1)S(1)} all-to-all(bf16[32,2048,16]{1,2,0:T(8,128)(2,1)S(1)} %copy.21), channel_id=1, replica_groups=mesh['tm'=32,'space'=8] {'tm'}, dimensions={0} | all-to-all | bytes 4194304 | tf_op jit(solution)/shard_map/all_to_all | solution.py:32
  391.6 0.0 copy-done
  391.6 3.7 convolution_bitcast_fusion
  395.3 0.0 copy-start.1
  395.3 0.0 all-reduce.3.cloned.1.call-update
  395.4 258.5 %all-reduce.3.cloned.1.call-done = f32[1024,512]{0,1:T(8,128)} async-done(((f32[1024,512]{0,1:T(8,128)}), f32[1024,512]{0,1:T(8,128)}) %all-reduce.3.cloned.1.call-update) | async-done | bytes 2097168 | tf_op jit(solution)/shard_map/psum | solution.py:38
  653.8 1.8 broadcast_multiply_fusion
  655.7 0.8 copy.22
  656.5 0.0 copy-done.1
  656.5 7.7 %add_convert_fusion = bf16[2048,1024]{1,0:T(8,128)(2,1)} fusion(bf16[2048,1024]{1,0:T(8,128)(2,1)} %param.10, bf16[2048,512]{0,1:T(8,128)(2,1)S(1)} %bitcast.18, f32[1024]{0:T(1024)S(1)} %copy-done.1, f32[1024,512]{0,1:T(8,128)} %all-reduce.3.cloned.1.call-done), kind=kOutput, calls=%fused_computation.4 | convolution fusion | flops 2159017984 | bytes 12587008 | tf_op jit(solution)/shard_map/dot_general | solution.py:44
  (5 shorter events, 0.1 us)
Async XLA Ops:
  7.2 179.0 %all-gather.6.cloned.1.call-start = ((), (), s32[]{:S(2)}) async-start(), calls=%async_computation.2 | async-start | bytes 18874368 | tf_op jit(solution)/shard_map/all_gather | solution.py:20
  7.9 321.8 %all-gather.4.cloned.1.call-start = ((), (), s32[]{:S(2)}) async-start(), calls=%async_computation.1 | async-start | bytes 17301504 | tf_op jit(solution)/shard_map/all_gather | solution.py:27
  8.6 645.2 %all-reduce.3.cloned.1.call-start = ((), (), s32[]{:S(2)}) async-start(), calls=%async_computation.3 | async-start | bytes 4194304 | tf_op jit(solution)/shard_map/psum | solution.py:38
  355.0 36.6 %copy-start = (bf16[2048,1024]{1,0:T(8,128)(2,1)S(1)}, bf16[2048,1024]{1,0:T(8,128)(2,1)}, u32[]{:S(2)}) copy-start(bf16[2048,1024]{1,0:T(8,128)(2,1)} %param.10) | copy-start | bytes 12582916
  395.3 261.2 %copy-start.1 = (f32[1024]{0:T(1024)S(1)}, f32[1024]{0:T(1024)}, u32[]{:S(2)}) copy-start(f32[1024]{0:T(1024)} %param.11) | copy-start | bytes 12292
Sparse Core Ops, SparseCore 0:
  9.8 176.3 all-gather.5
  188.7 76.7 all-gather.3
  395.5 258.3 all-reduce.2
where the time goes:
time: 673 us; the launch traced here: 671 us
  waiting for transfers between devices  396 us (59%)
  local copies, waits for them, and re-layouts  159 us (24%)
  blocking collectives  73.1 us (11%)
  matrix products  25.6 us (4%)
  between operations  14.5 us (2%)
    psum x1, waiting for transfers between devices, per_device(): coeffs = lax.psum(partial_coeffs, ('tm', 'space')) / math.sqrt(cell_total)  258 us
    all_gather x1, waiting for transfers between devices, per_device(): gathered = lax.all_gather(snapshots, 'space', axis=1, tiled=True)  136 us
    reshape x2, local copies, waits for them, and re-layouts, per_device(): blocks = gathered.reshape(time_rows, cell_total // TILE, TILE)  90.1 us
    gather x2, local copies, waits for them, and re-layouts, per_device(): blocks[:, list_column.reshape(-1), :]  42.2 us
    all_to_all x1, blocking collectives, per_device(): lax.all_to_all(remap_part, 'tm', split_axis=0, concat_axis=2, tiled=True)  35.4 us
    all_gather x1, blocking collectives, per_device(): lax.all_gather(block_lists, 'tm', axis=0, tiled=True)  25.9 us
    dot_general x1, matrix products, per_device(): jnp.einsum('kip,tkp->kit', masked, picked, preferred_element_type=jnp.flo...  14.3 us
  transfers between devices with their start and end apart: 3, of which 2 were waited for; matrix products, arithmetic and copies ran while one was open for 22% of the time, Pallas kernels for 0%

commit v1 on v0

v1 whole, which is shorter than its diff:
```python
import functools
import math

import jax
import jax.numpy as jnp
from jax import lax
from jax.experimental import pallas as pl
from jax.experimental.pallas import tpu as pltpu
from jax.sharding import PartitionSpec as P

TILE = 64
MAXB = 2
PAIR = MAXB * TILE
ROWS = 8
BF16 = jnp.bfloat16
F32 = jnp.float32


def pick_kernel(tiles, per_space, sel_ref, source_ref, out_ref):
    group = pl.program_id(0) * out_ref.shape[0]
    low = lax.broadcasted_iota(jnp.int32, (ROWS, PAIR), 1) < TILE

    def fetch(slot):
        block = sel_ref[slot]
        within = lax.rem(block, per_space)
        lanes = pl.ds(pl.multiple_of(lax.div(within, 2) * PAIR, PAIR), PAIR)
        found = source_ref[lax.div(block, per_space), :, lanes]
        swapped = jnp.concatenate([found[:, TILE:], found[:, :TILE]], axis=1)
        return found, swapped, lax.rem(within, 2) == 1

    for owner in range(out_ref.shape[0]):
        def tile(k, carry):
            slot = ((group + owner) * tiles + k) * MAXB
            a, a_swapped, a_odd = fetch(slot)
            b, b_swapped, b_odd = fetch(slot + 1)
            first = jnp.where(a_odd, a_swapped, a)
            second = jnp.where(b_odd, b, b_swapped)
            lanes = pl.ds(pl.multiple_of(k * PAIR, PAIR), PAIR)
            out_ref[owner, :, lanes] = jnp.where(low, first, second)
            return carry

        lax.fori_loop(0, tiles, tile, 0, unroll=8)


def pick(sel, source, owners, tiles, interpret=False):
    spaces, rows, cells = source.shape
    step = min(8, owners)
    return pl.pallas_call(
        functools.partial(pick_kernel, tiles, cells // TILE),
        out_shape=jax.ShapeDtypeStruct((owners, rows, tiles * PAIR), BF16),
        grid_spec=pltpu.PrefetchScalarGridSpec(
            num_scalar_prefetch=1,
            grid=(owners // step,),
            in_specs=[
                pl.BlockSpec((spaces, rows, cells), lambda i, sel: (0, 0, 0), pipeline_mode=pl.Buffered(1)),
            ],
            out_specs=pl.BlockSpec((step, rows, tiles * PAIR), lambda i, sel: (i, 0, 0)),
        ),
        compiler_params=pltpu.CompilerParams(vmem_limit_bytes=40 << 20),
        name="pick",
        interpret=interpret,
    )(sel, source)


def project_kernel(group, counts_ref, picked_ref, weights_ref, basis_ref, remapped_ref, partial_ref):
    step = pl.program_id(0)

    @pl.when(step == 0)
    def _():
        partial_ref[...] = jnp.zeros_like(partial_ref)

    low = lax.broadcasted_iota(jnp.int32, (TILE, PAIR), 1) < TILE
    pieces = []
    for k in range(group):
        both = counts_ref[step * group + k] > 1
        weights = jnp.where(jnp.logical_or(low, both), weights_ref[k].astype(F32), 0.0).astype(BF16)
        picked = picked_ref[:, k * PAIR:(k + 1) * PAIR]
        pieces.append(
            lax.dot_general(weights, picked, (((1,), (1,)), ((), ())), preferred_element_type=F32)
        )
    block = jnp.concatenate(pieces, axis=0).astype(BF16)
    remapped_ref[...] = block
    partial_ref[...] += jnp.dot(block.T, basis_ref[...], preferred_element_type=F32)


def project(counts, picked, weights, basis, interpret=False):
    snaps = picked.shape[0]
    tiles = weights.shape[0]
    cells, rank = basis.shape
    group = 4
    return pl.pallas_call(
        functools.partial(project_kernel, group),
        out_shape=(
            jax.ShapeDtypeStruct((cells, snaps), BF16),
            jax.ShapeDtypeStruct((snaps, rank), F32),
        ),
        grid_spec=pltpu.PrefetchScalarGridSpec(
            num_scalar_prefetch=1,
            grid=(tiles // group,),
            in_specs=[
                pl.BlockSpec((snaps, group * PAIR), lambda i, counts: (0, i)),
                pl.BlockSpec((group, TILE, PAIR), lambda i, counts: (i, 0, 0)),
                pl.BlockSpec((group * TILE, rank), lambda i, counts: (i, 0)),
            ],
            out_specs=(
                pl.BlockSpec((group * TILE, snaps), lambda i, counts: (i, 0)),
                pl.BlockSpec((snaps, rank), lambda i, counts: (0, 0)),
            ),
        ),
        compiler_params=pltpu.CompilerParams(vmem_limit_bytes=40 << 20),
        name="project",
        interpret=interpret,
    )(counts, picked, weights, basis)


def rotate_kernel(scale, r0_ref, r1_ref, c0_ref, c1_ref, basis_ref, variances_ref, out_ref):
    update = jnp.dot(r0_ref[...], c0_ref[...], preferred_element_type=F32)
    update += jnp.dot(r1_ref[...], c1_ref[...], preferred_element_type=F32)
    out_ref[...] = (basis_ref[...].astype(F32) * variances_ref[...] + update * scale).astype(BF16)


def rotate(remapped, halves, basis, variances, interpret=False):
    cells, rank = basis.shape
    snaps = remapped[0].shape[1]
    rows = min(256, cells)
    resident = lambda i: (0, 0)
    return pl.pallas_call(
        functools.partial(rotate_kernel, 1.0 / math.sqrt(2 * snaps)),
        out_shape=jax.ShapeDtypeStruct((cells, rank), BF16),
        grid=(cells // rows,),
        in_specs=[
            pl.BlockSpec((rows, snaps), lambda i: (i, 0)),
            pl.BlockSpec((rows, snaps), lambda i: (i, 0)),
            pl.BlockSpec((snaps, rank), resident),
            pl.BlockSpec((snaps, rank), resident),
            pl.BlockSpec((rows, rank), lambda i: (i, 0)),
            pl.BlockSpec((1, rank), resident),
        ],
        out_specs=pl.BlockSpec((rows, rank), lambda i: (i, 0)),
        compiler_params=pltpu.CompilerParams(vmem_limit_bytes=40 << 20),
        name="rotate",
        interpret=interpret,
    )(*remapped, *halves, basis, variances[None, :])


def exchange(array, axis):
    return lax.all_to_all(array, axis, split_axis=0, concat_axis=0, tiled=True)


def per_device(interpret, snapshots, block_lists, tile_counts, remap_weights, basis, variances):
    tiles = block_lists.shape[0]
    owners, spaces = lax.axis_size("tm"), lax.axis_size("space")
    cells, rank = basis.shape
    total = cells * owners * spaces
    own_ranks = rank // spaces
    here = lax.axis_index("space")

    sources = [
        lax.all_gather(snapshots[c * ROWS:(c + 1) * ROWS], "space", axis=0) for c in range(2)
    ]
    sel = lax.all_gather(block_lists, "tm", axis=0, tiled=True).reshape(-1)

    remapped, messages = [], []
    for source in sources:
        if messages:
            source, messages[0] = lax.optimization_barrier((source, messages[0]))
        picked = pick(sel, source, owners, tiles, interpret)
        arrived = exchange(picked, "tm").reshape(owners * ROWS, tiles * PAIR)
        block, partial = project(tile_counts, arrived, remap_weights, basis, interpret)
        parts = exchange(partial.reshape(owners, ROWS, rank), "tm")
        column = jnp.sum(parts, axis=0)
        column = exchange(jnp.broadcast_to(column, (spaces, ROWS, rank)), "space")
        coeffs = jnp.sum(column, axis=0) * (1.0 / math.sqrt(total))
        half = coeffs.astype(BF16)
        rest = lax.dynamic_slice_in_dim(coeffs - half.astype(F32), here * own_ranks, own_ranks, 1)
        messages.append(jnp.concatenate([half, rest.astype(BF16)], axis=1))
        remapped.append(block)

    message = jnp.concatenate(messages, axis=0)
    everyone = exchange(jnp.broadcast_to(message, (owners,) + message.shape), "tm")
    halves = [
        everyone[:, c * ROWS:(c + 1) * ROWS, :rank].reshape(owners * ROWS, rank) for c in range(2)
    ]
    high = lax.dynamic_slice_in_dim(everyone, here * own_ranks, own_ranks, 2)
    own = high.astype(F32) + everyone[:, :, rank:].astype(F32)
    own_coeffs = own.reshape(owners * 2 * ROWS, own_ranks).T
    rotated = rotate(remapped, halves, basis, variances, interpret)
    return (own_coeffs, rotated)


def solution(mesh, interpret=False):
    return jax.shard_map(
        functools.partial(per_device, interpret),
        mesh=mesh,
        in_specs=(
            P("tm", "space"),
            P(("tm", "space"), None),
            P(("tm", "space")),
            P(("tm", "space"), None, None),
            P(("tm", "space"), None),
            P(),
        ),
        out_specs=(P("space", None), P(("tm", "space"), None)),
        check_vma=False,
    )
```

time: 673 us -> 355 us (0.53)
  waiting for transfers between devices: 396 us -> 102 us
  local copies, waits for them, and re-layouts: 159 us -> 16.5 us
  blocking collectives: 73.1 us -> 152 us
  Pallas kernels: 0 us -> 58 us
  matrix products: 25.6 us -> 0 us
  starting transfers between devices: 0.11 us -> 8.77 us
    psum x1 -> x0, waiting for transfers between devices: 258 us -> none  [per_device(): coeffs = lax.psum(partial_coeffs, ('tm', 'space')) / math.sqrt(cell_total)]
    reshape x6 -> x2, local copies, waits for them, and re-layouts: 109 us -> 1.54 us  [the longest x1 1.27 us: per_device(): everyone[:, c * ROWS:(c + 1) * ROWS, :rank].reshape(owners * ROWS, rank)]
    all_to_all x1 -> x5, blocking collectives: 35.4 us -> 127 us  [exchange(): return lax.all_to_all(array, axis, split_axis=0, concat_axis=0, tiled=True)]
    all_gather x2, waiting for transfers between devices: 136 us -> 70.7 us  [per_device(): lax.all_gather(snapshots[c * ROWS:(c + 1) * ROWS], 'space', axis=0)]
    pallas_call x0 -> x5, Pallas kernels: none -> 58 us  [the longest x2 42.2 us: pick(): pl.pallas_call(functools.partial(pick_kernel, tiles, cells // TILE), out_...]
    gather x2 -> x0, local copies, waits for them, and re-layouts: 42.2 us -> none  [per_device(): blocks[:, list_column.reshape(-1), :]]
    all_to_all x0 -> x2, waiting for transfers between devices: none -> 30.8 us  [exchange(): return lax.all_to_all(array, axis, split_axis=0, concat_axis=0, tiled=True)]
    dot_general x3 -> x0, matrix products: 25.6 us -> none  [the longest x1 14.3 us: per_device(): jnp.einsum('kip,tkp->kit', masked, picked, preferred_element_type=jnp.flo...]
  transfers between devices with their start and end apart: 3 -> 4, of which waited for: 2 -> 3; matrix products, arithmetic and copies ran while one was open for 22% -> 0% of each run, Pallas kernels for 0% -> 7%
where the time goes in v1:
time: 355 us
  blocking collectives  152 us (43%)
  waiting for transfers between devices  102 us (29%)
  Pallas kernels  58 us (16%)
  local copies, waits for them, and re-layouts  16.5 us (5%)
  between operations  14.2 us (4%)
  starting transfers between devices  8.77 us (2%)
    all_to_all x5, blocking collectives, exchange(): return lax.all_to_all(array, axis, split_axis=0, concat_axis=0, tiled=True)  127 us
    all_gather x2, waiting for transfers between devices, per_device(): lax.all_gather(snapshots[c * ROWS:(c + 1) * ROWS], 'space', axis=0)  70.7 us
    pallas_call x2, Pallas kernels, pick(): pl.pallas_call(functools.partial(pick_kernel, tiles, cells // TILE), out_...  42.2 us
    all_to_all x2, waiting for transfers between devices, exchange(): return lax.all_to_all(array, axis, split_axis=0, concat_axis=0, tiled=True)  30.8 us
    all_gather x1, blocking collectives, per_device(): sel = lax.all_gather(block_lists, 'tm', axis=0, tiled=True).reshape(-1)  25.9 us
    pallas_call x2, Pallas kernels, project(): pl.pallas_call(functools.partial(project_kernel, group), out_shape=(jax.S...  10.3 us
    unnamed x19, local copies, waits for them, and re-layouts  9.81 us
    all_to_all x2, starting transfers between devices, exchange(): return lax.all_to_all(array, axis, split_axis=0, concat_axis=0, tiled=True)  8.69 us
  transfers between devices with their start and end apart: 4, of which 3 were waited for; matrix products, arithmetic and copies ran while one was open for 0% of the time, Pallas kernels for 7%

profile of v1, /device:TPU:1, one launch (start us, length us, event | category | flops | bytes accessed | tf_op | source)
XLA Modules:
  0.0 354.5 jit_solution(14175063675185518062)
XLA Ops:
  7.2 0.0 all-gather.8.cloned.1.call-start
  7.2 3.0 fusion.4
  10.2 0.0 copy-start.8
  10.2 0.0 all-gather.8.cloned.1.call-update
  10.2 0.0 all-gather.6.cloned.1.call-start
  10.3 0.7 all-gather.6.cloned.1.call-update
  11.0 0.0 copy-done.8
  11.0 25.9 %all-gather.2 = s32[32,32,2]{1,2,0:T(2,128)S(1)} all-gather(s32[1,32,2]{1,2,0:T(2,128)S(1)} %bitcast.23), channel_id=1, replica_groups=mesh['tm'=32,'space'=8] {'tm'}, dimensions={0}, use_global_device_ids=true | all-gather | bytes 8448 | tf_op jit(solution)/shard_map/all_gather | solution.py:161
  36.9 0.3 copy.13
  37.1 0.3 reshape.28.sel_ref
  37.4 70.7 %all-gather.8.cloned.1.call-done = bf16[64,65536]{1,0:T(8,128)(2,1)} async-done(((bf16[8,65536]{1,0:T(8,128)(2,1)}), bf16[64,65536]{1,0:T(8,128)(2,1)}) %all-gather.8.cloned.1.call-update) | async-done | bytes 8388624 | tf_op jit(solution)/shard_map/all_gather | solution.py:159
  108.1 0.0 copy-start.4
  108.1 3.4 copy-done.4
  111.5 21.1 %pick.2 = bf16[32,8,4096]{2,1,0:T(8,128)(2,1)S(1)} custom-call(s32[2048]{0:T(1024)S(1)} %reshape.28.sel_ref, bf16[8,8,65536]{2,1,0:T(8,128)(2,1)S(1)} %bitcast.16), custom_call_target="tpu_custom_call" | custom-call | tf_op jit(solution)/shard_map/pick/pallas_call | solution.py:48
  132.6 0.0 copy-start
  132.6 0.0 copy-start.7
  132.6 35.9 %all_to_all.35 = bf16[32,8,4096]{2,1,0:T(8,128)(2,1)S(1)} all-to-all(bf16[32,8,4096]{2,1,0:T(8,128)(2,1)S(1)} %pick.2), channel_id=1, replica_groups=mesh['tm'=32,'space'=8] {'tm'}, dimensions={0} | all-to-all | bytes 4194304 | tf_op jit(solution)/shard_map/all_to_all | solution.py:147
  168.5 0.0 copy-done.5
  168.5 0.0 copy-done
  168.5 0.0 copy-done.7
  168.5 5.1 %project.2 = (bf16[2048,256]{1,0:T(8,128)(2,1)S(1)}, f32[256,1024]{1,0:T(8,128)S(1)}) custom-call(s32[32]{0:T(128)S(1)} %copy-done.7, bf16[256,4096]{1,0:T(8,128)(2,1)S(1)} %bitcast.17, bf16[32,64,128]{2,1,0:T(8,128)(2,1)S(1)} %copy-done.5, bf16[2048,1024]{1,0:T(8,128)(2,1)S(1)} %copy-done), custom_call_target="tpu_custom_call" | custom-call | tf_op jit(solution)/shard_map/project/pallas_call | solution.py:91
  173.7 20.7 %all_to_all.36 = f32[32,8,1024]{2,1,0:T(8,128)S(1)} all-to-all(f32[32,8,1024]{2,1,0:T(8,128)S(1)} %bitcast.19), channel_id=1, replica_groups=mesh['tm'=32,'space'=8] {'tm'}, dimensions={0} | all-to-all | bytes 2097152 | tf_op jit(solution)/shard_map/all_to_all | solution.py:147
  194.3 0.1 reduce_sum.36
  194.4 0.7 broadcast_in_dim.12
  195.1 4.0 %all-to-all-start.2 = ((f32[8,8,1024]{2,1,0:T(8,128)}), f32[8,8,1024]{2,1,0:T(8,128)S(1)}, u32[]{:S(2)}, u32[]{:S(2)}) async-start(f32[8,8,1024]{2,1,0:T(8,128)} %broadcast_in_dim.12), calls=%async_computation.2 | async-start | bytes 524288 | tf_op jit(solution)/shard_map/all_to_all | solution.py:147
  199.1 12.3 %all-to-all-done.2 = f32[8,8,1024]{2,1,0:T(8,128)S(1)} async-done(((f32[8,8,1024]{2,1,0:T(8,128)}), f32[8,8,1024]{2,1,0:T(8,128)S(1)}, u32[]{:S(2)}, u32[]{:S(2)}) %all-to-all-start.2) | async-done | bytes 262176 | tf_op jit(solution)/shard_map/all_to_all | solution.py:147
  211.5 0.0 all-gather.6.cloned.1.call-done
  211.5 0.0 copy-start.3
  211.5 3.4 copy-done.3
  214.9 21.1 %pick.3 = bf16[32,8,4096]{2,1,0:T(8,128)(2,1)S(1)} custom-call(s32[2048]{0:T(1024)S(1)} %reshape.28.sel_ref, bf16[8,8,65536]{2,1,0:T(8,128)(2,1)S(1)} %bitcast.15), custom_call_target="tpu_custom_call" | custom-call | tf_op jit(solution)/shard_map/pick/pallas_call | solution.py:48
  236.0 0.0 copy-start.1
  236.0 34.5 %all_to_all.37 = bf16[32,8,4096]{2,1,0:T(8,128)(2,1)S(1)} all-to-all(bf16[32,8,4096]{2,1,0:T(8,128)(2,1)S(1)} %pick.3), channel_id=1, replica_groups=mesh['tm'=32,'space'=8] {'tm'}, dimensions={0} | all-to-all | bytes 4194304 | tf_op jit(solution)/shard_map/all_to_all | solution.py:147
  270.6 0.0 copy-done.1
  270.6 5.2 %project.3 = (bf16[2048,256]{1,0:T(8,128)(2,1)S(1)}, f32[256,1024]{1,0:T(8,128)S(1)}) custom-call(s32[32]{0:T(128)S(1)} %copy-done.7, bf16[256,4096]{1,0:T(8,128)(2,1)S(1)} %bitcast.18, bf16[32,64,128]{2,1,0:T(8,128)(2,1)S(1)} %copy-done.5, bf16[2048,1024]{1,0:T(8,128)(2,1)S(1)} %copy-done.1), custom_call_target="tpu_custom_call" | custom-call | tf_op jit(solution)/shard_map/project/pallas_call | solution.py:91
  275.7 20.7 %all_to_all.38 = f32[32,8,1024]{2,1,0:T(8,128)} all-to-all(f32[32,8,1024]{2,1,0:T(8,128)S(1)} %bitcast.20), channel_id=1, replica_groups=mesh['tm'=32,'space'=8] {'tm'}, dimensions={0} | all-to-all | bytes 2097152 | tf_op jit(solution)/shard_map/all_to_all | solution.py:147
  296.4 1.3 reduce_sum.38
  297.7 14.8 %all_to_all.39 = f32[8,8,1024]{2,1,0:T(8,128)S(1)} all-to-all(f32[8,8,1024]{2,1,0:T(8,128)S(1)} %broadcast_in_dim.13), channel_id=1, replica_groups=mesh['tm'=32,'space'=8] {'space'}, dimensions={0} | all-to-all | bytes 524288 | tf_op jit(solution)/shard_map/all_to_all | solution.py:147
  312.6 1.1 broadcast_in_dim.14
  313.7 4.7 %all-to-all-start.6 = ((bf16[32,16,1152]{2,1,0:T(8,128)(2,1)}), bf16[32,16,1152]{2,1,0:T(8,128)(2,1)}, u32[]{:S(2)}, u32[]{:S(2)}) async-start(bf16[32,16,1152]{2,1,0:T(8,128)(2,1)} %broadcast_in_dim.14), calls=%async_computation.6 | async-start | bytes 2359296 | tf_op jit(solution)/shard_map/all_to_all | solution.py:147
  318.4 0.0 copy-start.6
  318.4 18.5 %all-to-all-done.6 = bf16[32,16,1152]{2,1,0:T(8,128)(2,1)} async-done(((bf16[32,16,1152]{2,1,0:T(8,128)(2,1)}), bf16[32,16,1152]{2,1,0:T(8,128)(2,1)}, u32[]{:S(2)}, u32[]{:S(2)}) %all-to-all-start.6) | async-done | bytes 1179680 | tf_op jit(solution)/shard_map/all_to_all | solution.py:147
  336.9 1.0 convert_add_fusion
  337.9 0.8 copy.14
  338.8 1.3 slice_bitcast_fusion
  340.0 0.0 copy-done.6
  340.0 0.0 copy-start.2
  340.1 2.2 copy-done.2
  342.2 5.4 %rotate.1 = bf16[2048,1024]{1,0:T(8,128)(2,1)} custom-call(bf16[2048,256]{1,0:T(8,128)(2,1)S(1)} %get-tuple-element.12.r0_ref, bf16[2048,256]{1,0:T(8,128)(2,1)S(1)} %get-tuple-element.13.r1_ref, bf16[256,1024]{1,0:T(8,128)(2,1)S(1)} %get-tuple-element.23.c0_ref, bf16[256,1024]{1,0:T(8,128)(2,1)S(1)} %get-tuple-element.22.c1_ref, ...), custom_call_target="tpu_custom_call" | custom-call | tf_op jit(solution)/shard_map/rotate/pallas_call | solution.py:127
  (10 shorter events, 0.1 us)
Async XLA Ops:
  7.2 100.9 %all-gather.8.cloned.1.call-start = ((), (), s32[]{:S(2)}) async-start(), calls=%async_computation.8 | async-start | bytes 9437184 | tf_op jit(solution)/shard_map/all_gather | solution.py:159
  10.2 0.8 copy-start.8
  10.2 201.3 %all-gather.6.cloned.1.call-start = ((), (), s32[]{:S(2)}) async-start(), calls=%async_computation.7 | async-start | bytes 9437184 | tf_op jit(solution)/shard_map/all_gather | solution.py:159
  108.1 3.4 copy-start.4
  111.5 57.1 %copy-start.5 = (bf16[32,64,128]{2,1,0:T(8,128)(2,1)S(1)}, bf16[32,64,128]{2,1,0:T(8,128)(2,1)}, u32[]{:S(2)}) copy-start(bf16[32,64,128]{2,1,0:T(8,128)(2,1)} %weights_ref.3) | copy-start | bytes 1572868
  132.6 35.9 %copy-start = (bf16[2048,1024]{1,0:T(8,128)(2,1)S(1)}, bf16[2048,1024]{1,0:T(8,128)(2,1)}, u32[]{:S(2)}) copy-start(bf16[2048,1024]{1,0:T(8,128)(2,1)} %basis_ref.5) | copy-start | bytes 12582916
  132.6 35.9 %copy-start.7 = (s32[32]{0:T(128)S(1)}, s32[32]{0:T(128)}, u32[]{:S(2)}) copy-start(s32[32]{0:T(128)} %counts_ref.3) | copy-start | bytes 388
  195.1 16.3 %all-to-all-start.2 = ((f32[8,8,1024]{2,1,0:T(8,128)}), f32[8,8,1024]{2,1,0:T(8,128)S(1)}, u32[]{:S(2)}, u32[]{:S(2)}) async-start(f32[8,8,1024]{2,1,0:T(8,128)} %broadcast_in_dim.12), calls=%async_computation.2 | async-start | bytes 524288 | tf_op jit(solution)/shard_map/all_to_all | solution.py:147
  211.5 3.4 copy-start.3
  236.0 34.5 %copy-start.1 = (bf16[2048,1024]{1,0:T(8,128)(2,1)S(1)}, bf16[2048,1024]{1,0:T(8,128)(2,1)}, u32[]{:S(2)}) copy-start(bf16[2048,1024]{1,0:T(8,128)(2,1)} %basis_ref.5) | copy-start | bytes 12582916
  313.7 23.2 %all-to-all-start.6 = ((bf16[32,16,1152]{2,1,0:T(8,128)(2,1)}), bf16[32,16,1152]{2,1,0:T(8,128)(2,1)}, u32[]{:S(2)}, u32[]{:S(2)}) async-start(bf16[32,16,1152]{2,1,0:T(8,128)(2,1)} %broadcast_in_dim.14), calls=%async_computation.6 | async-start | bytes 2359296 | tf_op jit(solution)/shard_map/all_to_all | solution.py:147
  318.4 21.6 %copy-start.6 = (f32[1024]{0:T(1024)S(1)}, f32[1024]{0:T(1024)}, u32[]{:S(2)}) copy-start(f32[1024]{0:T(1024)} %param.11) | copy-start | bytes 12292
  340.0 2.2 copy-start.2
Sparse Core Ops, SparseCore 0:
  10.4 97.6 all-gather.7
  109.9 92.6 all-gather.5

commit v2 on v1

--- a/solution.py
+++ b/solution.py
@@ -16,45 +16,42 @@
 F32 = jnp.float32
 
 
-def pick_kernel(tiles, per_space, sel_ref, source_ref, out_ref):
-    group = pl.program_id(0) * out_ref.shape[0]
+def pick_kernel(sel_ref, source_ref, out_ref):
+    count = out_ref.shape[0]
+    start = pl.program_id(0) * count
     low = lax.broadcasted_iota(jnp.int32, (ROWS, PAIR), 1) < TILE
 
     def fetch(slot):
         block = sel_ref[slot]
-        within = lax.rem(block, per_space)
-        lanes = pl.ds(pl.multiple_of(lax.div(within, 2) * PAIR, PAIR), PAIR)
-        found = source_ref[lax.div(block, per_space), :, lanes]
+        found = source_ref[lax.shift_right_logical(block, 1)]
         swapped = jnp.concatenate([found[:, TILE:], found[:, :TILE]], axis=1)
-        return found, swapped, lax.rem(within, 2) == 1
-
-    for owner in range(out_ref.shape[0]):
-        def tile(k, carry):
-            slot = ((group + owner) * tiles + k) * MAXB
-            a, a_swapped, a_odd = fetch(slot)
-            b, b_swapped, b_odd = fetch(slot + 1)
-            first = jnp.where(a_odd, a_swapped, a)
-            second = jnp.where(b_odd, b, b_swapped)
-            lanes = pl.ds(pl.multiple_of(k * PAIR, PAIR), PAIR)
-            out_ref[owner, :, lanes] = jnp.where(low, first, second)
-            return carry
-
-        lax.fori_loop(0, tiles, tile, 0, unroll=8)
-
-
-def pick(sel, source, owners, tiles, interpret=False):
-    spaces, rows, cells = source.shape
-    step = min(8, owners)
+        return found, swapped, (block & 1) == 1
+
+    def tile(k, carry):
+        slot = (start + k) * MAXB
+        a, a_swapped, a_odd = fetch(slot)
+        b, b_swapped, b_odd = fetch(slot + 1)
+        first = jnp.where(a_odd, a_swapped, a)
+        second = jnp.where(b_odd, b, b_swapped)
+        out_ref[k] = jnp.where(low, first, second)
+        return carry
+
+    lax.fori_loop(0, count, tile, 0, unroll=8)
+
+
+def pick(sel, source, interpret=False):
+    count = sel.shape[0] // MAXB
+    step = min(128, count)
     return pl.pallas_call(
-        functools.partial(pick_kernel, tiles, cells // TILE),
-        out_shape=jax.ShapeDtypeStruct((owners, rows, tiles * PAIR), BF16),
+        pick_kernel,
+        out_shape=jax.ShapeDtypeStruct((count, ROWS, PAIR), BF16),
         grid_spec=pltpu.PrefetchScalarGridSpec(
             num_scalar_prefetch=1,
-            grid=(owners // step,),
+            grid=(count // step,),
             in_specs=[
-                pl.BlockSpec((spaces, rows, cells), lambda i, sel: (0, 0, 0), pipeline_mode=pl.Buffered(1)),
+                pl.BlockSpec(source.shape, lambda i, sel: (0, 0, 0), pipeline_mode=pl.Buffered(1)),
             ],
-            out_specs=pl.BlockSpec((step, rows, tiles * PAIR), lambda i, sel: (i, 0, 0)),
+            out_specs=pl.BlockSpec((step, ROWS, PAIR), lambda i, sel: (i, 0, 0)),
         ),
         compiler_params=pltpu.CompilerParams(vmem_limit_bytes=40 << 20),
         name="pick",
@@ -74,7 +71,7 @@
     for k in range(group):
         both = counts_ref[step * group + k] > 1
         weights = jnp.where(jnp.logical_or(low, both), weights_ref[k].astype(F32), 0.0).astype(BF16)
-        picked = picked_ref[:, k * PAIR:(k + 1) * PAIR]
+        picked = picked_ref[:, k].reshape(-1, PAIR)
         pieces.append(
             lax.dot_general(weights, picked, (((1,), (1,)), ((), ())), preferred_element_type=F32)
         )
@@ -84,7 +81,7 @@
 
 
 def project(counts, picked, weights, basis, interpret=False):
-    snaps = picked.shape[0]
+    snaps = picked.shape[0] * ROWS
     tiles = weights.shape[0]
     cells, rank = basis.shape
     group = 4
@@ -98,7 +95,7 @@
             num_scalar_prefetch=1,
             grid=(tiles // group,),
             in_specs=[
-                pl.BlockSpec((snaps, group * PAIR), lambda i, counts: (0, i)),
+                pl.BlockSpec((picked.shape[0], group, ROWS, PAIR), lambda i, counts: (0, i, 0, 0)),
                 pl.BlockSpec((group, TILE, PAIR), lambda i, counts: (i, 0, 0)),
                 pl.BlockSpec((group * TILE, rank), lambda i, counts: (i, 0)),
             ],
@@ -164,8 +161,9 @@
     for source in sources:
         if messages:
             source, messages[0] = lax.optimization_barrier((source, messages[0]))
-        picked = pick(sel, source, owners, tiles, interpret)
-        arrived = exchange(picked, "tm").reshape(owners * ROWS, tiles * PAIR)
+        source = source.reshape(spaces, ROWS, -1, PAIR).transpose(0, 2, 1, 3)
+        picked = pick(sel, source.reshape(-1, ROWS, PAIR), interpret)
+        arrived = exchange(picked.reshape(owners, tiles, ROWS, PAIR), "tm")
         block, partial = project(tile_counts, arrived, remap_weights, basis, interpret)
         parts = exchange(partial.reshape(owners, ROWS, rank), "tm")
         column = jnp.sum(parts, axis=0)

time: 355 us -> 346 us (0.975)
  Pallas kernels: 58 us -> 41.2 us
  waiting for transfers between devices: 102 us -> 107 us
    pallas_call x2, Pallas kernels: 42.2 us -> 25.4 us  [pick(): pl.pallas_call(pick_kernel, out_shape=jax.ShapeDtypeStruct((count, ROWS,...]
  transfers between devices with their start and end apart: 4 -> 4, of which waited for: 3 -> 4; matrix products, arithmetic and copies ran while one was open for 0% -> 0% of each run, Pallas kernels for 7% -> 5%
where the time goes in v2:
time: 346 us
  blocking collectives  155 us (45%)
  waiting for transfers between devices  107 us (31%)
  Pallas kernels  41.2 us (12%)
  local copies, waits for them, and re-layouts  16.5 us (5%)
  between operations  14.2 us (4%)
  starting transfers between devices  8.93 us (3%)
    all_to_all x5, blocking collectives, exchange(): return lax.all_to_all(array, axis, split_axis=0, concat_axis=0, tiled=True)  129 us
    all_gather x2, waiting for transfers between devices, per_device(): lax.all_gather(snapshots[c * ROWS:(c + 1) * ROWS], 'space', axis=0)  73.1 us
    all_to_all x2, waiting for transfers between devices, exchange(): return lax.all_to_all(array, axis, split_axis=0, concat_axis=0, tiled=True)  33.5 us
    all_gather x1, blocking collectives, per_device(): sel = lax.all_gather(block_lists, 'tm', axis=0, tiled=True).reshape(-1)  25.9 us
    pallas_call x2, Pallas kernels, pick(): pl.pallas_call(pick_kernel, out_shape=jax.ShapeDtypeStruct((count, ROWS,...  25.4 us
    pallas_call x2, Pallas kernels, project(): pl.pallas_call(functools.partial(project_kernel, group), out_shape=(jax.S...  10.3 us
    unnamed x19, local copies, waits for them, and re-layouts  9.81 us
    all_to_all x2, starting transfers between devices, exchange(): return lax.all_to_all(array, axis, split_axis=0, concat_axis=0, tiled=True)  8.85 us
  transfers between devices with their start and end apart: 4, of which 4 were waited for; matrix products, arithmetic and copies ran while one was open for 0% of the time, Pallas kernels for 5%

profile of v2, /device:TPU:1, one launch (start us, length us, event | category | flops | bytes accessed | tf_op | source)
XLA Modules:
  0.0 345.6 jit_solution(73148082716632180)
XLA Ops:
  7.2 0.0 all-gather.8.cloned.1.call-start
  7.2 3.0 fusion.4
  10.2 0.0 copy-start.8
  10.2 0.0 all-gather.8.cloned.1.call-update
  10.2 0.0 all-gather.6.cloned.1.call-start
  10.3 0.7 all-gather.6.cloned.1.call-update
  11.0 0.0 copy-done.8
  11.0 25.9 %all-gather.2 = s32[32,32,2]{1,2,0:T(2,128)S(1)} all-gather(s32[1,32,2]{1,2,0:T(2,128)S(1)} %bitcast.32), channel_id=1, replica_groups=mesh['tm'=32,'space'=8] {'tm'}, dimensions={0}, use_global_device_ids=true | all-gather | bytes 8448 | tf_op jit(solution)/shard_map/all_gather | solution.py:158
  36.9 0.3 copy.13
  37.1 0.3 reshape.40.sel_ref
  37.4 70.7 %all-gather.8.cloned.1.call-done = bf16[64,65536]{1,0:T(8,128)(2,1)} async-done(((bf16[8,65536]{1,0:T(8,128)(2,1)}), bf16[64,65536]{1,0:T(8,128)(2,1)}) %all-gather.8.cloned.1.call-update) | async-done | bytes 8388624 | tf_op jit(solution)/shard_map/all_gather | solution.py:156
  108.1 0.0 copy-start.4
  108.1 3.4 copy-done.4
  111.5 0.0 copy-start.5
  111.5 0.0 copy-start.7
  111.5 12.7 %pick.2 = bf16[1024,8,128]{2,1,0:T(8,128)(2,1)S(1)} custom-call(s32[2048]{0:T(1024)S(1)} %reshape.40.sel_ref, bf16[4096,8,128]{2,1,0:T(8,128)(2,1)S(1)} %bitcast.25), custom_call_target="tpu_custom_call" | custom-call | tf_op jit(solution)/shard_map/pick/pallas_call | solution.py:45
  124.2 0.0 copy-start
  124.2 35.9 %all_to_all.35.picked_ref = bf16[32,32,8,128]{3,2,1,0:T(8,128)(2,1)S(1)} all-to-all(bf16[32,32,8,128]{3,2,1,0:T(8,128)(2,1)S(1)} %bitcast.27), channel_id=1, replica_groups=mesh['tm'=32,'space'=8] {'tm'}, dimensions={0} | all-to-all | bytes 4194304 | tf_op jit(solution)/shard_map/all_to_all | solution.py:144
  160.1 0.0 copy-done.5
  160.1 0.0 copy-done.7
  160.1 0.0 copy-done
  160.1 5.1 %project.2 = (bf16[2048,256]{1,0:T(8,128)(2,1)S(1)}, f32[256,1024]{1,0:T(8,128)S(1)}) custom-call(s32[32]{0:T(128)S(1)} %copy-done.7, bf16[32,32,8,128]{3,2,1,0:T(8,128)(2,1)S(1)} %all_to_all.35.picked_ref, bf16[32,64,128]{2,1,0:T(8,128)(2,1)S(1)} %copy-done.5, bf16[2048,1024]{1,0:T(8,128)(2,1)S(1)} %copy-done), custom_call_target="tpu_custom_call" | custom-call | tf_op jit(solution)/shard_map/project/pallas_call | solution.py:88
  165.3 20.6 %all_to_all.36 = f32[32,8,1024]{2,1,0:T(8,128)S(1)} all-to-all(f32[32,8,1024]{2,1,0:T(8,128)S(1)} %bitcast.28), channel_id=1, replica_groups=mesh['tm'=32,'space'=8] {'tm'}, dimensions={0} | all-to-all | bytes 2097152 | tf_op jit(solution)/shard_map/all_to_all | solution.py:144
  185.9 0.1 reduce_sum.36
  186.0 0.7 broadcast_in_dim.12
  186.7 4.0 %all-to-all-start.2 = ((f32[8,8,1024]{2,1,0:T(8,128)}), f32[8,8,1024]{2,1,0:T(8,128)S(1)}, u32[]{:S(2)}, u32[]{:S(2)}) async-start(f32[8,8,1024]{2,1,0:T(8,128)} %broadcast_in_dim.12), calls=%async_computation.2 | async-start | bytes 524288 | tf_op jit(solution)/shard_map/all_to_all | solution.py:144
  190.8 15.0 %all-to-all-done.2 = f32[8,8,1024]{2,1,0:T(8,128)S(1)} async-done(((f32[8,8,1024]{2,1,0:T(8,128)}), f32[8,8,1024]{2,1,0:T(8,128)S(1)}, u32[]{:S(2)}, u32[]{:S(2)}) %all-to-all-start.2) | async-done | bytes 262176 | tf_op jit(solution)/shard_map/all_to_all | solution.py:144
  205.8 2.5 all-gather.6.cloned.1.call-done
  208.3 3.4 copy-done.3
  211.7 12.7 %pick.3 = bf16[1024,8,128]{2,1,0:T(8,128)(2,1)S(1)} custom-call(s32[2048]{0:T(1024)S(1)} %reshape.40.sel_ref, bf16[4096,8,128]{2,1,0:T(8,128)(2,1)S(1)} %bitcast.24), custom_call_target="tpu_custom_call" | custom-call | tf_op jit(solution)/shard_map/pick/pallas_call | solution.py:45
  224.4 0.0 copy-start.1
  224.4 35.8 %all_to_all.37.picked_ref = bf16[32,32,8,128]{3,2,1,0:T(8,128)(2,1)S(1)} all-to-all(bf16[32,32,8,128]{3,2,1,0:T(8,128)(2,1)S(1)} %bitcast.26), channel_id=1, replica_groups=mesh['tm'=32,'space'=8] {'tm'}, dimensions={0} | all-to-all | bytes 4194304 | tf_op jit(solution)/shard_map/all_to_all | solution.py:144
  260.2 0.0 copy-done.1
  260.2 5.2 %project.3 = (bf16[2048,256]{1,0:T(8,128)(2,1)S(1)}, f32[256,1024]{1,0:T(8,128)S(1)}) custom-call(s32[32]{0:T(128)S(1)} %copy-done.7, bf16[32,32,8,128]{3,2,1,0:T(8,128)(2,1)S(1)} %all_to_all.37.picked_ref, bf16[32,64,128]{2,1,0:T(8,128)(2,1)S(1)} %copy-done.5, bf16[2048,1024]{1,0:T(8,128)(2,1)S(1)} %copy-done.1), custom_call_target="tpu_custom_call" | custom-call | tf_op jit(solution)/shard_map/project/pallas_call | solution.py:88
  265.4 20.7 %all_to_all.38 = f32[32,8,1024]{2,1,0:T(8,128)} all-to-all(f32[32,8,1024]{2,1,0:T(8,128)S(1)} %bitcast.29), channel_id=1, replica_groups=mesh['tm'=32,'space'=8] {'tm'}, dimensions={0} | all-to-all | bytes 2097152 | tf_op jit(solution)/shard_map/all_to_all | solution.py:144
  286.1 1.3 reduce_sum.38
  287.4 16.1 %all_to_all.39 = f32[8,8,1024]{2,1,0:T(8,128)S(1)} all-to-all(f32[8,8,1024]{2,1,0:T(8,128)S(1)} %broadcast_in_dim.13), channel_id=1, replica_groups=mesh['tm'=32,'space'=8] {'space'}, dimensions={0} | all-to-all | bytes 524288 | tf_op jit(solution)/shard_map/all_to_all | solution.py:144
  303.6 1.1 broadcast_in_dim.14
  304.7 4.8 %all-to-all-start.6 = ((bf16[32,16,1152]{2,1,0:T(8,128)(2,1)}), bf16[32,16,1152]{2,1,0:T(8,128)(2,1)}, u32[]{:S(2)}, u32[]{:S(2)}) async-start(bf16[32,16,1152]{2,1,0:T(8,128)(2,1)} %broadcast_in_dim.14), calls=%async_computation.6 | async-start | bytes 2359296 | tf_op jit(solution)/shard_map/all_to_all | solution.py:144
  309.5 0.0 copy-start.6
  309.5 18.5 %all-to-all-done.6 = bf16[32,16,1152]{2,1,0:T(8,128)(2,1)} async-done(((bf16[32,16,1152]{2,1,0:T(8,128)(2,1)}), bf16[32,16,1152]{2,1,0:T(8,128)(2,1)}, u32[]{:S(2)}, u32[]{:S(2)}) %all-to-all-start.6) | async-done | bytes 1179680 | tf_op jit(solution)/shard_map/all_to_all | solution.py:144
  328.0 1.0 convert_add_fusion
  329.0 0.8 copy.14
  329.9 1.3 slice_bitcast_fusion
  331.1 0.0 copy-done.6
  331.1 0.0 copy-start.2
  331.2 2.2 copy-done.2
  333.3 5.4 %rotate.1 = bf16[2048,1024]{1,0:T(8,128)(2,1)} custom-call(bf16[2048,256]{1,0:T(8,128)(2,1)S(1)} %get-tuple-element.12.r0_ref, bf16[2048,256]{1,0:T(8,128)(2,1)S(1)} %get-tuple-element.13.r1_ref, bf16[256,1024]{1,0:T(8,128)(2,1)S(1)} %get-tuple-element.23.c0_ref, bf16[256,1024]{1,0:T(8,128)(2,1)S(1)} %get-tuple-element.22.c1_ref, ...), custom_call_target="tpu_custom_call" | custom-call | tf_op jit(solution)/shard_map/rotate/pallas_call | solution.py:124
  (10 shorter events, 0.1 us)
Async XLA Ops:
  7.2 100.9 %all-gather.8.cloned.1.call-start = ((), (), s32[]{:S(2)}) async-start(), calls=%async_computation.8 | async-start | bytes 9437184 | tf_op jit(solution)/shard_map/all_gather | solution.py:156
  10.2 0.8 copy-start.8
  10.2 198.1 %all-gather.6.cloned.1.call-start = ((), (), s32[]{:S(2)}) async-start(), calls=%async_computation.7 | async-start | bytes 9437184 | tf_op jit(solution)/shard_map/all_gather | solution.py:156
  108.1 3.4 copy-start.4
  111.5 48.6 %copy-start.5 = (bf16[32,64,128]{2,1,0:T(8,128)(2,1)S(1)}, bf16[32,64,128]{2,1,0:T(8,128)(2,1)}, u32[]{:S(2)}) copy-start(bf16[32,64,128]{2,1,0:T(8,128)(2,1)} %weights_ref.3) | copy-start | bytes 1572868
  111.5 48.6 %copy-start.7 = (s32[32]{0:T(128)S(1)}, s32[32]{0:T(128)}, u32[]{:S(2)}) copy-start(s32[32]{0:T(128)} %counts_ref.3) | copy-start | bytes 388
  124.2 35.9 %copy-start = (bf16[2048,1024]{1,0:T(8,128)(2,1)S(1)}, bf16[2048,1024]{1,0:T(8,128)(2,1)}, u32[]{:S(2)}) copy-start(bf16[2048,1024]{1,0:T(8,128)(2,1)} %basis_ref.5) | copy-start | bytes 12582916
  186.7 19.1 %all-to-all-start.2 = ((f32[8,8,1024]{2,1,0:T(8,128)}), f32[8,8,1024]{2,1,0:T(8,128)S(1)}, u32[]{:S(2)}, u32[]{:S(2)}) async-start(f32[8,8,1024]{2,1,0:T(8,128)} %broadcast_in_dim.12), calls=%async_computation.2 | async-start | bytes 524288 | tf_op jit(solution)/shard_map/all_to_all | solution.py:144
  208.3 3.4 copy-start.3
  224.4 35.8 %copy-start.1 = (bf16[2048,1024]{1,0:T(8,128)(2,1)S(1)}, bf16[2048,1024]{1,0:T(8,128)(2,1)}, u32[]{:S(2)}) copy-start(bf16[2048,1024]{1,0:T(8,128)(2,1)} %basis_ref.5) | copy-start | bytes 12582916
  304.7 23.3 %all-to-all-start.6 = ((bf16[32,16,1152]{2,1,0:T(8,128)(2,1)}), bf16[32,16,1152]{2,1,0:T(8,128)(2,1)}, u32[]{:S(2)}, u32[]{:S(2)}) async-start(bf16[32,16,1152]{2,1,0:T(8,128)(2,1)} %broadcast_in_dim.14), calls=%async_computation.6 | async-start | bytes 2359296 | tf_op jit(solution)/shard_map/all_to_all | solution.py:144
  309.5 21.6 %copy-start.6 = (f32[1024]{0:T(1024)S(1)}, f32[1024]{0:T(1024)}, u32[]{:S(2)}) copy-start(f32[1024]{0:T(1024)} %param.11) | copy-start | bytes 12292
  331.1 2.2 copy-start.2
Sparse Core Ops, SparseCore 0:
  10.4 97.6 all-gather.7
  109.9 98.3 all-gather.5

commit v3 on v2

v3 whole, which is shorter than its diff:
```python
import functools
import math

import jax
import jax.numpy as jnp
from jax import lax
from jax.experimental import pallas as pl
from jax.experimental.pallas import tpu as pltpu
from jax.sharding import PartitionSpec as P


TILE = 64
MAXB = 2
PAIR = MAXB * TILE
ROWS = 8
LANES = 128
CAPACITY = 256
BF16 = jnp.bfloat16
F32 = jnp.float32


def pair_words(index):
    after = pltpu.roll(index, LANES - 1, 1)
    return (
        lax.shift_right_logical(index, 1)
        | (lax.shift_right_logical(after, 1) << 12)
        | ((index & 1) << 24)
        | ((1 - (after & 1)) << 25)
    )


def route_kernel(capacity, per_space, here_ref, codes_ref, request_ref, local_ref):
    owners = codes_ref.shape[0]
    spaces = request_ref.shape[0]
    here = here_ref[0]
    codes = codes_ref[...]
    owner_of = jnp.where(codes < 0, -1, lax.div(jnp.maximum(codes, 0), per_space))
    within = jnp.where(codes < 0, 0, lax.rem(jnp.maximum(codes, 0), per_space))
    upper = lax.broadcasted_iota(jnp.int32, (LANES, LANES), 0) <= lax.broadcasted_iota(jnp.int32, (LANES, LANES), 1)
    upper = jnp.where(upper, 1.0, 0.0).astype(BF16)
    lower = lax.broadcasted_iota(jnp.int32, (owners, owners), 0) > lax.broadcasted_iota(jnp.int32, (owners, owners), 1)
    lower = jnp.where(lower, 1.0, 0.0).astype(BF16)
    location = jnp.zeros_like(codes)
    target = jnp.full_like(codes, -1)
    most = jnp.zeros((1, LANES), F32)
    for s in range(spaces):
        match = owner_of == s
        ones = jnp.where(match, 1.0, 0.0).astype(BF16)
        prefix = jnp.dot(ones, upper, preferred_element_type=F32)
        sums = jnp.broadcast_to(prefix[:, LANES - 1:], (owners, LANES))
        ahead = jnp.dot(lower, sums.astype(BF16), preferred_element_type=F32)
        rank = (prefix + ahead).astype(jnp.int32) - 1
        most = jnp.maximum(most, ahead[owners - 1:] + sums[owners - 1:])
        location = jnp.where(match, rank + lax.rem(here - s + spaces, spaces) * capacity, location)
        target = jnp.where(match, rank + s * capacity, target)
    local_ref[...] = pair_words(location)

    rows = spaces * capacity // LANES
    row_id = lax.broadcasted_iota(jnp.int32, (rows, LANES), 0)
    lane_id = lax.broadcasted_iota(jnp.int32, (LANES, LANES), 1)
    lane_of = (target & (LANES - 1)).astype(F32)
    lane_of = jnp.concatenate([lane_of, jnp.zeros((LANES - owners, LANES), F32)], axis=0).T
    high = jnp.zeros((rows, LANES), F32)
    low = jnp.zeros((rows, LANES), F32)
    for r in range(owners):
        hit = jnp.broadcast_to(target[r:r + 1] >> 7, (rows, LANES)) == row_id
        value = jnp.broadcast_to(within[r:r + 1], (rows, LANES))
        upper_part = jnp.where(hit, lax.shift_right_logical(value, 6), 0).astype(F32).astype(BF16)
        lower_part = jnp.where(hit, value & 63, 0).astype(F32).astype(BF16)
        column = jnp.broadcast_to(lane_of[:, r:r + 1], (LANES, LANES)).astype(jnp.int32)
        onehot = jnp.where(column == lane_id, 1.0, 0.0).astype(BF16)
        high += jnp.dot(upper_part, onehot, preferred_element_type=F32)
        low += jnp.dot(lower_part, onehot, preferred_element_type=F32)
    wanted = high.astype(jnp.int32) * 64 + low.astype(jnp.int32)
    words = pair_words(wanted)
    overflow = jnp.where(most > capacity, 1, 0)
    each = capacity // LANES
    for s in range(spaces):
        request_ref[s, 0:each, :] = words[s * each:(s + 1) * each]
        request_ref[s, each:, :] = jnp.broadcast_to(overflow, (ROWS - each, LANES))


def route(here, codes, spaces, per_space, capacity, interpret=False):
    return pl.pallas_call(
        functools.partial(route_kernel, capacity, per_space),
        out_shape=(
            jax.ShapeDtypeStruct((spaces, ROWS, LANES), jnp.int32),
            jax.ShapeDtypeStruct(codes.shape, jnp.int32),
        ),
        in_specs=[pl.BlockSpec(memory_space=pltpu.SMEM), pl.BlockSpec(memory_space=pltpu.VMEM)],
        out_specs=(pl.BlockSpec(memory_space=pltpu.VMEM), pl.BlockSpec(memory_space=pltpu.VMEM)),
        name="route",
        interpret=interpret,
    )(here, codes)


def pick_kernel(halves, row_tiles, words_ref, *refs):
    sources, outs = refs[:halves], refs[halves:]
    count = outs[0].shape[0]
    start = pl.program_id(0) * (count // row_tiles) * LANES
    lane = lax.broadcasted_iota(jnp.int32, (ROWS, LANES), 1)
    low = lane < TILE
    bit = jnp.where(low, 1 << 24, 1 << 25)

    for row in range(count // row_tiles):
        def tile(k, carry):
            word = words_ref[start + row * LANES + k * MAXB]
            swap = (jnp.broadcast_to(word, (ROWS, LANES)) & bit) != 0
            first = word & 0xFFF
            second = lax.shift_right_logical(word, 12) & 0xFFF
            for source_ref, out_ref in zip(sources, outs):
                a, b = source_ref[first], source_ref[second]
                crossed = jnp.where(low, b, a)
                crossed = jnp.concatenate([crossed[:, TILE:], crossed[:, :TILE]], axis=1)
                out_ref[row * row_tiles + k] = jnp.where(swap, crossed, jnp.where(low, a, b))
            return carry

        lax.fori_loop(0, row_tiles, tile, 0, unroll=16)


def pick(words, sources, row_tiles, interpret=False):
    count = words.shape[0] // LANES * row_tiles
    step = min(128, count)
    shape = jax.ShapeDtypeStruct((count, ROWS, LANES), BF16)
    return pl.pallas_call(
        functools.partial(pick_kernel, len(sources), row_tiles),
        out_shape=[shape] * len(sources),
        grid_spec=pltpu.PrefetchScalarGridSpec(
            num_scalar_prefetch=1,
            grid=(count // step,),
            in_specs=[
                pl.BlockSpec(source.shape, lambda i, words: (0, 0, 0), pipeline_mode=pl.Buffered(1))
                for source in sources
            ],
            out_specs=[pl.BlockSpec((step, ROWS, LANES), lambda i, words: (i, 0, 0))] * len(sources),
        ),
        compiler_params=pltpu.CompilerParams(vmem_limit_bytes=40 << 20),
        name="pick",
        interpret=interpret,
    )(words, *sources)


def project_kernel(group, counts_ref, first_ref, second_ref, weights_ref, basis_ref, remapped_ref, partial_ref):
    step = pl.program_id(0)

    @pl.when(step == 0)
    def _():
        partial_ref[...] = jnp.zeros_like(partial_ref)

    low = lax.broadcasted_iota(jnp.int32, (TILE, PAIR), 1) < TILE
    pieces = []
    for k in range(group):
        both = counts_ref[step * group + k] > 1
        weights = jnp.where(jnp.logical_or(low, both), weights_ref[k].astype(F32), 0.0).astype(BF16)
        picked = jnp.concatenate(
            [first_ref[:, k].reshape(-1, PAIR), second_ref[:, k].reshape(-1, PAIR)], axis=0
        )
        pieces.append(
            lax.dot_general(weights, picked, (((1,), (1,)), ((), ())), preferred_element_type=F32)
        )
    block = jnp.concatenate(pieces, axis=0).astype(BF16)
    remapped_ref[...] = block
    half = block.shape[1] // 2
    for c in range(2):
        add = jnp.dot(block[:, c * half:(c + 1) * half].T, basis_ref[...], preferred_element_type=F32)
        partial_ref[:, c] += add.reshape(half // ROWS, ROWS, -1)


def project(counts, arrived, weights, basis, interpret=False):
    owners = arrived[0].shape[0]
    snaps = owners * 2 * ROWS
    tiles = weights.shape[0]
    cells, rank = basis.shape
    group = 4
    chunk = pl.BlockSpec((owners, group, ROWS, PAIR), lambda i, counts: (0, i, 0, 0))
    return pl.pallas_call(
        functools.partial(project_kernel, group),
        out_shape=(
            jax.ShapeDtypeStruct((cells, snaps), BF16),
            jax.ShapeDtypeStruct((owners, 2, ROWS, rank), F32),
        ),
        grid_spec=pltpu.PrefetchScalarGridSpec(
            num_scalar_prefetch=1,
            grid=(tiles // group,),
            in_specs=[
                chunk,
                chunk,
                pl.BlockSpec((group, TILE, PAIR), lambda i, counts: (i, 0, 0)),
                pl.BlockSpec((group * TILE, rank), lambda i, counts: (i, 0)),
            ],
            out_specs=(
                pl.BlockSpec((group * TILE, snaps), lambda i, counts: (i, 0)),
                pl.BlockSpec((owners, 2, ROWS, rank), lambda i, counts: (0, 0, 0, 0)),
            ),
        ),
        compiler_params=pltpu.CompilerParams(vmem_limit_bytes=40 << 20),
        name="project",
        interpret=interpret,
    )(counts, *arrived, weights, basis)


def rotate_kernel(scale, remapped_ref, c0_ref, c1_ref, basis_ref, variances_ref, out_ref):
    half = c0_ref.shape[0]
    update = jnp.dot(remapped_ref[:, :half], c0_ref[...], preferred_element_type=F32)
    update += jnp.dot(remapped_ref[:, half:], c1_ref[...], preferred_element_type=F32)
    out_ref[...] = (basis_ref[...].astype(F32) * variances_ref[...] + update * scale).astype(BF16)


def rotate(remapped, halves, basis, variances, interpret=False):
    cells, rank = basis.shape
    snaps = remapped.shape[1]
    rows = min(256, cells)
    resident = lambda i: (0, 0)
    return pl.pallas_call(
        functools.partial(rotate_kernel, 1.0 / math.sqrt(snaps)),
        out_shape=jax.ShapeDtypeStruct((cells, rank), BF16),
        grid=(cells // rows,),
        in_specs=[
            pl.BlockSpec((rows, snaps), lambda i: (i, 0)),
            pl.BlockSpec((snaps // 2, rank), resident),
            pl.BlockSpec((snaps // 2, rank), resident),
            pl.BlockSpec((rows, rank), lambda i: (i, 0)),
            pl.BlockSpec((1, rank), resident),
        ],
        out_specs=pl.BlockSpec((rows, rank), lambda i: (i, 0)),
        compiler_params=pltpu.CompilerParams(vmem_limit_bytes=40 << 20),
        name="rotate",
        interpret=interpret,
    )(remapped, *halves, basis, variances[None, :])


def exchange(array, axis):
    return lax.all_to_all(array, axis, split_axis=0, concat_axis=0, tiled=True)


def spread(array, axis):
    return exchange(jnp.broadcast_to(array, (lax.axis_size(axis),) + array.shape), axis)


def per_device(interpret, capacity, snapshots, block_lists, tile_counts, remap_weights, basis, variances):
    tiles = block_lists.shape[0]
    owners, spaces = lax.axis_size("tm"), lax.axis_size("space")
    cells, rank = basis.shape
    total = cells * owners * spaces
    own_ranks = rank // spaces
    here = lax.axis_index("space")
    per_space = snapshots.shape[1] // TILE

    used = lax.broadcasted_iota(jnp.int32, block_lists.shape, 1) < tile_counts[:, None]
    codes = jnp.where(used, block_lists, -1).reshape(1, tiles * MAXB)
    codes = jnp.pad(codes, ((0, 0), (0, LANES - tiles * MAXB)), constant_values=-1)
    codes = spread(codes, "tm").reshape(owners, LANES)
    requests, local_words = route(here[None], codes, spaces, per_space, capacity, interpret)
    asked = exchange(requests, "space")
    each = capacity // LANES
    around = lax.dynamic_slice_in_dim(jnp.concatenate([asked, asked], axis=0), here, spaces, 0)
    asked_words = around[:, :each].reshape(-1)
    overflow = jnp.max(asked[:, each]) > 0
    halves_tiles = snapshots.reshape(2, ROWS, -1, LANES).transpose(0, 2, 1, 3)
    local = [halves_tiles[c] for c in range(2)]

    def finish(chosen):
        arrived = [exchange(c.reshape(owners, tiles, ROWS, PAIR), "tm") for c in chosen]
        remapped, partial = project(tile_counts, arrived, remap_weights, basis, interpret)
        parts = exchange(partial.reshape(owners, 2 * ROWS, rank), "tm")
        column = spread(jnp.sum(parts, axis=0), "space")
        coeffs = jnp.sum(column, axis=0) * (1.0 / math.sqrt(total))
        half = coeffs.astype(BF16)
        rest = lax.dynamic_slice_in_dim(coeffs - half.astype(F32), here * own_ranks, own_ranks, 1)
        everyone = spread(jnp.concatenate([half, rest.astype(BF16)], axis=1), "tm")
        halves = [
            everyone[:, c * ROWS:(c + 1) * ROWS, :rank].reshape(owners * ROWS, rank) for c in range(2)
        ]
        high = lax.dynamic_slice_in_dim(everyone, here * own_ranks, own_ranks, 2)
        own = high.astype(F32) + everyone[:, :, rank:].astype(F32)
        own_coeffs = own.reshape(owners * 2 * ROWS, own_ranks).T
        return own_coeffs, rotate(remapped, halves, basis, variances, interpret)

    def dense():
        blocks = jnp.maximum(codes, 0)
        words = pair_words_plain(blocks).reshape(-1)
        sources = [spread(c, "space").reshape(-1, ROWS, LANES) for c in local]
        return finish([pick(words, [source], tiles, interpret)[0] for source in sources])

    def sparse():
        sent = pick(asked_words, local, LANES // MAXB, interpret)
        came = []
        for c in sent:
            c = c.reshape(spaces, -1, ROWS, LANES)
            parts = [c[0]] + [
                lax.ppermute(c[d], "space", [(i, (i + d) % spaces) for i in range(spaces)])
                for d in range(1, spaces)
            ]
            came.append(jnp.concatenate(parts, axis=0))
        words = local_words.reshape(-1)
        chosen = []
        for c in came:
            chosen += pick(words, [c.reshape(-1, ROWS, LANES)], tiles, interpret)
        return finish(chosen)

    return lax.cond(overflow, dense, sparse)


def pair_words_plain(index):
    after = jnp.roll(index, -1, axis=1)
    return (index >> 1) | ((after >> 1) << 12) | ((index & 1) << 24) | ((1 - (after & 1)) << 25)


def solution(mesh, interpret=False, capacity=CAPACITY):
    return jax.shard_map(
        functools.partial(per_device, interpret, capacity),
        mesh=mesh,
        in_specs=(
            P("tm", "space"),
            P(("tm", "space"), None),
            P(("tm", "space")),
            P(("tm", "space"), None, None),
            P(("tm", "space"), None),
            P(),
        ),
        out_specs=(P("space", None), P(("tm", "space"), None)),
        check_vma=False,
    )
```

time: 346 us -> 313 us (0.905)
  blocking collectives: 155 us -> 68.9 us
  starting transfers between devices: 8.93 us -> 55.7 us
  waiting for transfers between devices: 107 us -> 127 us
  between operations: 14.2 us -> 1.35 us
    ppermute x0 -> x14, waiting for transfers between devices: none -> 78.9 us  [sparse(): lax.ppermute(c[d], 'space', [(i, (i + d) % spaces) for i in range(spaces)])]
    all_gather x2 -> x0, waiting for transfers between devices: 73.1 us -> none  [per_device(): lax.all_gather(snapshots[c * ROWS:(c + 1) * ROWS], 'space', axis=0)]
    all_to_all x5 -> x2, blocking collectives: 129 us -> 68.9 us  [exchange(): return lax.all_to_all(array, axis, split_axis=0, concat_axis=0, tiled=True)]
    ppermute x0 -> x14, starting transfers between devices: none -> 25.9 us  [sparse(): lax.ppermute(c[d], 'space', [(i, (i + d) % spaces) for i in range(spaces)])]
    all_gather x1 -> x0, blocking collectives: 25.9 us -> none  [per_device(): sel = lax.all_gather(block_lists, 'tm', axis=0, tiled=True).reshape(-1)]
    all_to_all x2 -> x5, starting transfers between devices: 8.85 us -> 29.8 us  [exchange(): return lax.all_to_all(array, axis, split_axis=0, concat_axis=0, tiled=True)]
    all_to_all x2 -> x5, waiting for transfers between devices: 33.5 us -> 48.5 us  [exchange(): return lax.all_to_all(array, axis, split_axis=0, concat_axis=0, tiled=True)]
    unnamed x19 -> x4, local copies, waits for them, and re-layouts: 9.81 us -> 2.01 us
  transfers between devices with their start and end apart: 4 -> 19, of which waited for: 4 -> 14; matrix products, arithmetic and copies ran while one was open for 0% -> 1% of each run, Pallas kernels for 5% -> 3%
where the time goes in v3:
time: 313 us; the launch traced here: 312 us
  waiting for transfers between devices  127 us (41%)
  blocking collectives  68.9 us (22%)
  starting transfers between devices  55.7 us (18%)
  Pallas kernels  41.5 us (13%)
  local copies, waits for them, and re-layouts  14.9 us (5%)
    ppermute x14, waiting for transfers between devices, sparse(): lax.ppermute(c[d], 'space', [(i, (i + d) % spaces) for i in range(spaces)])  78.9 us
    all_to_all x2, blocking collectives, exchange(): return lax.all_to_all(array, axis, split_axis=0, concat_axis=0, tiled=True)  68.9 us
    all_to_all x5, waiting for transfers between devices, exchange(): return lax.all_to_all(array, axis, split_axis=0, concat_axis=0, tiled=True)  48.5 us
    all_to_all x5, starting transfers between devices, exchange(): return lax.all_to_all(array, axis, split_axis=0, concat_axis=0, tiled=True)  29.8 us
    ppermute x14, starting transfers between devices, sparse(): lax.ppermute(c[d], 'space', [(i, (i + d) % spaces) for i in range(spaces)])  25.9 us
    pallas_call x3, Pallas kernels, pick(): pl.pallas_call(functools.partial(pick_kernel, len(sources), row_tiles), o...  24.7 us
    pallas_call x1, Pallas kernels, project(): pl.pallas_call(functools.partial(project_kernel, group), out_shape=(jax.S...  6.85 us
    pallas_call x1, Pallas kernels, rotate(): pl.pallas_call(functools.partial(rotate_kernel, 1.0 / math.sqrt(snaps)),...  6.55 us
  transfers between devices with their start and end apart: 19, of which 14 were waited for; matrix products, arithmetic and copies ran while one was open for 1% of the time, Pallas kernels for 3%

profile of v3, /device:TPU:1, one launch (start us, length us, event | category | flops | bytes accessed | tf_op | source)
XLA Modules:
  0.0 311.9 jit_solution(17502735713827166624)
XLA Ops:
  2.1 8.6 %all-to-all-start.12 = ((s32[32,1,128]{2,1,0:T(1,128)}), s32[32,1,128]{2,1,0:T(1,128)S(1)}, u32[]{:S(2)}, u32[]{:S(2)}) async-start(s32[32,1,128]{2,1,0:T(1,128)} %broadcast_in_dim.37), calls=%async_computation.12 | async-start | bytes 32768 | tf_op jit(solution)/shard_map/all_to_all | solution.py:233
  10.7 6.9 %all-to-all-done.12 = s32[32,1,128]{2,1,0:T(1,128)S(1)} async-done(((s32[32,1,128]{2,1,0:T(1,128)}), s32[32,1,128]{2,1,0:T(1,128)S(1)}, u32[]{:S(2)}, u32[]{:S(2)}) %all-to-all-start.12) | async-done | bytes 16416 | tf_op jit(solution)/shard_map/all_to_all | solution.py:233
  17.6 3.4 %route.1 = (s32[8,8,128]{2,1,0:T(8,128)}, s32[32,128]{1,0:T(8,128)S(1)}) custom-call(s32[1]{0:T(128)} %bitcast.23.here_ref, s32[32,128]{1,0:T(8,128)S(1)} %bitcast.51), custom_call_target="tpu_custom_call" | custom-call | tf_op jit(solution)/shard_map/route/pallas_call | solution.py:84
  21.0 8.2 %all-to-all-start.13 = ((s32[8,8,128]{2,1,0:T(8,128)}), s32[8,8,128]{2,1,0:T(8,128)S(1)}, u32[]{:S(2)}, u32[]{:S(2)}) async-start(s32[8,8,128]{2,1,0:T(8,128)} %get-tuple-element.73), calls=%async_computation.13 | async-start | bytes 65536 | tf_op jit(solution)/shard_map/all_to_all | solution.py:233
  29.2 1.7 slice_bitcast_fusion.4
  30.9 5.2 %all-to-all-done.13 = s32[8,8,128]{2,1,0:T(8,128)S(1)} async-done(((s32[8,8,128]{2,1,0:T(8,128)}), s32[8,8,128]{2,1,0:T(8,128)S(1)}, u32[]{:S(2)}, u32[]{:S(2)}) %all-to-all-start.13) | async-done | bytes 32800 | tf_op jit(solution)/shard_map/all_to_all | solution.py:233
  37.4 272.4 %conditional.1 = (bf16[2048,1024]{1,0:T(8,128)(2,1)S(1)}, f32[128,512]{1,0:T(8,128)}) conditional(s32[]{:T(128)} %convert_element_type.33, (s32[32,128]{1,0:T(8,128)S(1)}, s32[]{:T(128)}, s32[16,8,128]{2,1,0:T(8,128)S(1)}, bf16[512,8,128]{2,1,0:T(8,128)(2,1)S(1)}, bf16[512,8,128]{2,1,0:T(8,128)(2,1)S(1)}, /*index=5*/s32[32]{0:T(128)S(1)}, ...), branch_computations={%region_1.4_spmd, %region_4.7_spmd} | conditional | flops 989190 | bytes 174682352 | solution.py:301
  37.4 8.6 %pick.5 = (bf16[1024,8,128]{2,1,0:T(8,128)(2,1)S(1)}, bf16[1024,8,128]{2,1,0:T(8,128)(2,1)S(1)}) custom-call(s32[2048]{0:T(1024)S(1)} %bitcast.47, bf16[512,8,128]{2,1,0:T(8,128)(2,1)S(1)} %get-tuple-element.50.refs_0_, bf16[512,8,128]{2,1,0:T(8,128)(2,1)S(1)} %get-tuple-element.51.refs_1_), custom_call_target="tpu_custom_call" | custom-call | tf_op jit(solution)/shard_map/cond/branch_0_fun/pick/pallas_call | solution.py:125
  46.2 1.2 copy-done.5
  47.9 2.1 collective-permute-start.9
  50.0 3.3 %collective-permute-start.10 = (bf16[128,8,128]{2,1,0:T(8,128)(2,1)S(1)}, bf16[128,8,128]{2,1,0:T(8,128)(2,1)S(1)}, u32[]{:S(2)}, u32[]{:S(2)}) collective-permute-start(bf16[128,8,128]{2,1,0:T(8,128)(2,1)S(1)} %get-tuple-element.89), channel_id=1, source_target_pairs={{0,4},{1,5},{2,6},{3,7},{4,0},{5,1},{6,2},{7,3},{8,12},{9,13},{10,... | collective-permute-start | bytes 786440 | tf_op jit(solution)/shard_map/cond/branch_0_fun/ppermute | solution.py:291
  53.3 2.0 collective-permute-start.11
  55.3 1.6 collective-permute-start.12
  57.0 4.2 %collective-permute-done.8 = bf16[128,8,128]{2,1,0:T(8,128)(2,1)S(1)} collective-permute-done((bf16[128,8,128]{2,1,0:T(8,128)(2,1)S(1)}, bf16[128,8,128]{2,1,0:T(8,128)(2,1)S(1)}, u32[]{:S(2)}, u32[]{:S(2)}) %collective-permute-start.8) | collective-permute-done | bytes 262176 | tf_op jit(solution)/shard_map/cond/branch_0_fun/ppermute | solution.py:291
  61.2 2.8 collective-permute-start.13
  64.0 17.0 %collective-permute-done.9 = bf16[128,8,128]{2,1,0:T(8,128)(2,1)S(1)} collective-permute-done((bf16[128,8,128]{2,1,0:T(8,128)(2,1)S(1)}, bf16[128,8,128]{2,1,0:T(8,128)(2,1)S(1)}, u32[]{:S(2)}, u32[]{:S(2)}) %collective-permute-start.9) | collective-permute-done | bytes 262176 | tf_op jit(solution)/shard_map/cond/branch_0_fun/ppermute | solution.py:291
  81.0 6.1 %collective-permute-done.10 = bf16[128,8,128]{2,1,0:T(8,128)(2,1)S(1)} collective-permute-done((bf16[128,8,128]{2,1,0:T(8,128)(2,1)S(1)}, bf16[128,8,128]{2,1,0:T(8,128)(2,1)S(1)}, u32[]{:S(2)}, u32[]{:S(2)}) %collective-permute-start.10) | collective-permute-done | bytes 262176 | tf_op jit(solution)/shard_map/cond/branch_0_fun/ppermute | solution.py:291
  87.3 6.9 %collective-permute-done.12 = bf16[128,8,128]{2,1,0:T(8,128)(2,1)S(1)} collective-permute-done((bf16[128,8,128]{2,1,0:T(8,128)(2,1)S(1)}, bf16[128,8,128]{2,1,0:T(8,128)(2,1)S(1)}, u32[]{:S(2)}, u32[]{:S(2)}) %collective-permute-start.12) | collective-permute-done | bytes 262176 | tf_op jit(solution)/shard_map/cond/branch_0_fun/ppermute | solution.py:291
  94.2 4.4 %collective-permute-done.13 = bf16[128,8,128]{2,1,0:T(8,128)(2,1)S(1)} collective-permute-done((bf16[128,8,128]{2,1,0:T(8,128)(2,1)S(1)}, bf16[128,8,128]{2,1,0:T(8,128)(2,1)S(1)}, u32[]{:S(2)}, u32[]{:S(2)}) %collective-permute-start.13) | collective-permute-done | bytes 262176 | tf_op jit(solution)/shard_map/cond/branch_0_fun/ppermute | solution.py:291
  98.6 8.1 %pick.7 = bf16[1024,8,128]{2,1,0:T(8,128)(2,1)S(1)} custom-call(s32[4096]{0:T(1024)S(1)} %bitcast.54, bf16[1024,8,128]{2,1,0:T(8,128)(2,1)S(1)} %constant_dynamic-update-slice_fusion.7.refs_0_), custom_call_target="tpu_custom_call" | custom-call | tf_op jit(solution)/shard_map/cond/branch_0_fun/pick/pallas_call | solution.py:125
  106.7 1.3 copy-done.3
  108.0 5.2 %all-to-all-start.8 = ((bf16[32,32,8,128]{3,2,1,0:T(8,128)(2,1)}), bf16[32,32,8,128]{3,2,1,0:T(8,128)(2,1)S(1)}, u32[]{:S(2)}, u32[]{:S(2)}) async-start(bf16[32,32,8,128]{3,2,1,0:T(8,128)(2,1)} %bitcast.43), calls=%async_computation.8 | async-start | bytes 4194304 | tf_op jit(solution)/shard_map/cond/branch_0_fun/all_to_all | solution.py:233
  113.3 1.7 fusion.5
  114.9 1.4 collective-permute-start
  116.3 1.9 collective-permute-start.1
  118.2 2.4 collective-permute-start.2
  120.7 1.2 collective-permute-start.3
  121.9 3.2 %collective-permute-start.4 = (bf16[128,8,128]{2,1,0:T(8,128)(2,1)S(1)}, bf16[128,8,128]{2,1,0:T(8,128)(2,1)S(1)}, u32[]{:S(2)}, u32[]{:S(2)}) collective-permute-start(bf16[128,8,128]{2,1,0:T(8,128)(2,1)S(1)} %get-tuple-element.96), channel_id=1, source_target_pairs={{0,5},{1,6},{2,7},{3,0},{4,1},{5,2},{6,3},{7,4},{8,13},{9,14},{10,... | collective-permute-start | bytes 786440 | tf_op jit(solution)/shard_map/cond/branch_0_fun/ppermute | solution.py:291
  125.1 3.3 %collective-permute-start.5 = (bf16[128,8,128]{2,1,0:T(8,128)(2,1)S(1)}, bf16[128,8,128]{2,1,0:T(8,128)(2,1)S(1)}, u32[]{:S(2)}, u32[]{:S(2)}) collective-permute-start(bf16[128,8,128]{2,1,0:T(8,128)(2,1)S(1)} %get-tuple-element.95), channel_id=1, source_target_pairs={{0,6},{1,7},{2,0},{3,1},{4,2},{5,3},{6,4},{7,5},{8,14},{9,15},{10,... | collective-permute-start | bytes 786440 | tf_op jit(solution)/shard_map/cond/branch_0_fun/ppermute | solution.py:291
  128.4 8.1 %collective-permute-done.1 = bf16[128,8,128]{2,1,0:T(8,128)(2,1)S(1)} collective-permute-done((bf16[128,8,128]{2,1,0:T(8,128)(2,1)S(1)}, bf16[128,8,128]{2,1,0:T(8,128)(2,1)S(1)}, u32[]{:S(2)}, u32[]{:S(2)}) %collective-permute-start.1) | collective-permute-done | bytes 262176 | tf_op jit(solution)/shard_map/cond/branch_0_fun/ppermute | solution.py:291
  136.6 14.6 %collective-permute-done.2 = bf16[128,8,128]{2,1,0:T(8,128)(2,1)S(1)} collective-permute-done((bf16[128,8,128]{2,1,0:T(8,128)(2,1)S(1)}, bf16[128,8,128]{2,1,0:T(8,128)(2,1)S(1)}, u32[]{:S(2)}, u32[]{:S(2)}) %collective-permute-start.2) | collective-permute-done | bytes 262176 | tf_op jit(solution)/shard_map/cond/branch_0_fun/ppermute | solution.py:291
  151.2 10.0 %collective-permute-done.3 = bf16[128,8,128]{2,1,0:T(8,128)(2,1)S(1)} collective-permute-done((bf16[128,8,128]{2,1,0:T(8,128)(2,1)S(1)}, bf16[128,8,128]{2,1,0:T(8,128)(2,1)S(1)}, u32[]{:S(2)}, u32[]{:S(2)}) %collective-permute-start.3) | collective-permute-done | bytes 262176 | tf_op jit(solution)/shard_map/cond/branch_0_fun/ppermute | solution.py:291
  161.4 4.8 %collective-permute-done.5 = bf16[128,8,128]{2,1,0:T(8,128)(2,1)S(1)} collective-permute-done((bf16[128,8,128]{2,1,0:T(8,128)(2,1)S(1)}, bf16[128,8,128]{2,1,0:T(8,128)(2,1)S(1)}, u32[]{:S(2)}, u32[]{:S(2)}) %collective-permute-start.5) | collective-permute-done | bytes 262176 | tf_op jit(solution)/shard_map/cond/branch_0_fun/ppermute | solution.py:291
  166.2 2.8 collective-permute-done.6
  169.1 8.1 %pick.6 = bf16[1024,8,128]{2,1,0:T(8,128)(2,1)S(1)} custom-call(s32[4096]{0:T(1024)S(1)} %bitcast.55, bf16[1024,8,128]{2,1,0:T(8,128)(2,1)S(1)} %constant_dynamic-update-slice_fusion.refs_0_), custom_call_target="tpu_custom_call" | custom-call | tf_op jit(solution)/shard_map/cond/branch_0_fun/pick/pallas_call | solution.py:125
  177.1 1.3 copy-done.4
  178.5 37.1 %all_to_all.58.first_ref = bf16[32,32,8,128]{3,2,1,0:T(8,128)(2,1)S(1)} all-to-all(bf16[32,32,8,128]{3,2,1,0:T(8,128)(2,1)} %bitcast.44), channel_id=1, replica_groups=mesh['tm'=32,'space'=8] {'tm'}, dimensions={0} | all-to-all | bytes 4194304 | tf_op jit(solution)/shard_map/cond/branch_0_fun/all_to_all | solution.py:233
  215.5 6.8 %project.2 = (bf16[2048,512]{1,0:T(8,128)(2,1)S(1)}, f32[32,2,8,1024]{3,2,1,0:T(8,128)S(1)}) custom-call(s32[32]{0:T(128)S(1)} %get-tuple-element.46.counts_ref, bf16[32,32,8,128]{3,2,1,0:T(8,128)(2,1)S(1)} %all_to_all.58.first_ref, bf16[32,32,8,128]{3,2,1,0:T(8,128)(2,1)S(1)} %all-to-all-done.8.second_ref, bf16[32,64,128]{2,1,0:T(8,128)(2,1)S(1)} %copy-done.13, ...), custom_call_target="tpu_custom_call" | custom-call | tf_op jit(solution)/shard_map/cond/branch_0_fun/project/pallas_call | solution.py:176
  222.4 1.3 copy-done.6
  223.7 31.9 %all_to_all.59 = f32[32,16,1024]{2,1,0:T(8,128)S(1)} all-to-all(f32[32,16,1024]{2,1,0:T(8,128)S(1)} %bitcast.45), channel_id=1, replica_groups=mesh['tm'=32,'space'=8] {'tm'}, dimensions={0} | all-to-all | bytes 4194304 | tf_op jit(solution)/shard_map/cond/branch_0_fun/all_to_all | solution.py:233
  255.7 0.9 broadcast_in_dim.24
  256.5 3.8 %all-to-all-start.10 = ((f32[8,16,1024]{2,1,0:T(8,128)}), f32[8,16,1024]{2,1,0:T(8,128)S(1)}, u32[]{:S(2)}, u32[]{:S(2)}) async-start(f32[8,16,1024]{2,1,0:T(8,128)} %broadcast_in_dim.24), calls=%async_computation.10 | async-start | bytes 1048576 | tf_op jit(solution)/shard_map/cond/branch_0_fun/all_to_all | solution.py:233
  260.3 18.0 %all-to-all-done.10 = f32[8,16,1024]{2,1,0:T(8,128)S(1)} async-done(((f32[8,16,1024]{2,1,0:T(8,128)}), f32[8,16,1024]{2,1,0:T(8,128)S(1)}, u32[]{:S(2)}, u32[]{:S(2)}) %all-to-all-start.10) | async-done | bytes 524320 | tf_op jit(solution)/shard_map/cond/branch_0_fun/all_to_all | solution.py:233
  278.4 1.1 broadcast_in_dim.25
  279.5 4.1 %all-to-all-start.11 = ((bf16[32,16,1152]{2,1,0:T(8,128)(2,1)}), bf16[32,16,1152]{2,1,0:T(8,128)(2,1)S(1)}, u32[]{:S(2)}, u32[]{:S(2)}) async-start(bf16[32,16,1152]{2,1,0:T(8,128)(2,1)} %broadcast_in_dim.25), calls=%async_computation.11 | async-start | bytes 2359296 | tf_op jit(solution)/shard_map/cond/branch_0_fun/all_to_all | solution.py:233
  283.6 18.4 %all-to-all-done.11 = bf16[32,16,1152]{2,1,0:T(8,128)(2,1)S(1)} async-done(((bf16[32,16,1152]{2,1,0:T(8,128)(2,1)}), bf16[32,16,1152]{2,1,0:T(8,128)(2,1)S(1)}, u32[]{:S(2)}, u32[]{:S(2)}) %all-to-all-start.11) | async-done | bytes 1179680 | tf_op jit(solution)/shard_map/cond/branch_0_fun/all_to_all | solution.py:233
  303.1 6.6 %rotate.2 = bf16[2048,1024]{1,0:T(8,128)(2,1)S(1)} custom-call(bf16[2048,512]{1,0:T(8,128)(2,1)S(1)} %copy-done.7, bf16[256,1024]{1,0:T(8,128)(2,1)S(1)} %get-tuple-element.103.c0_ref, bf16[256,1024]{1,0:T(8,128)(2,1)S(1)} %get-tuple-element.102.c1_ref, bf16[2048,1024]{1,0:T(8,128)(2,1)} %get-tuple-element.55.basis_ref, f32[1,1024]{1,0:T(1,128)S(1)} %bitcast.56), custom_call_target="tpu_custom_call" | custom-call | tf_op jit(solution)/shard_map/cond/branch_0_fun/rotate/pallas_call | solution.py:214
  309.9 2.0 copy-done.12
  (54 shorter events, 4.6 us)
Async XLA Ops:
  2.1 15.5 %all-to-all-start.12 = ((s32[32,1,128]{2,1,0:T(1,128)}), s32[32,1,128]{2,1,0:T(1,128)S(1)}, u32[]{:S(2)}, u32[]{:S(2)}) async-start(s32[32,1,128]{2,1,0:T(1,128)} %broadcast_in_dim.37), calls=%async_computation.12 | async-start | bytes 32768 | tf_op jit(solution)/shard_map/all_to_all | solution.py:233
  21.0 15.1 %all-to-all-start.13 = ((s32[8,8,128]{2,1,0:T(8,128)}), s32[8,8,128]{2,1,0:T(8,128)S(1)}, u32[]{:S(2)}, u32[]{:S(2)}) async-start(s32[8,8,128]{2,1,0:T(8,128)} %get-tuple-element.73), calls=%async_computation.13 | async-start | bytes 65536 | tf_op jit(solution)/shard_map/all_to_all | solution.py:233
  29.2 8.2 %copy-start.17 = (s32[32]{0:T(128)S(1)}, s32[32]{0:T(128)}, u32[]{:S(2)}) copy-start(s32[32]{0:T(128)} %param.10) | copy-start | bytes 388
  46.0 1.3 copy-start.5
  47.3 8.0 %collective-permute-start.7 = (bf16[128,8,128]{2,1,0:T(8,128)(2,1)S(1)}, bf16[128,8,128]{2,1,0:T(8,128)(2,1)S(1)}, u32[]{:S(2)}, u32[]{:S(2)}) collective-permute-start(bf16[128,8,128]{2,1,0:T(8,128)(2,1)S(1)} %get-tuple-element.92), channel_id=1, source_target_pairs={{0,1},{1,2},{2,3},{3,4},{4,5},{5,6},{6,7},{7,0},{8,9},{9,10},{10,1... | collective-permute-start | bytes 786440 | tf_op jit(solution)/shard_map/cond/branch_0_fun/ppermute | solution.py:291
  47.6 13.6 %collective-permute-start.8 = (bf16[128,8,128]{2,1,0:T(8,128)(2,1)S(1)}, bf16[128,8,128]{2,1,0:T(8,128)(2,1)S(1)}, u32[]{:S(2)}, u32[]{:S(2)}) collective-permute-start(bf16[128,8,128]{2,1,0:T(8,128)(2,1)S(1)} %get-tuple-element.91), channel_id=1, source_target_pairs={{0,2},{1,3},{2,4},{3,5},{4,6},{5,7},{6,0},{7,1},{8,10},{9,11},{10,... | collective-permute-start | bytes 786440 | tf_op jit(solution)/shard_map/cond/branch_0_fun/ppermute | solution.py:291
  47.9 33.1 %collective-permute-start.9 = (bf16[128,8,128]{2,1,0:T(8,128)(2,1)S(1)}, bf16[128,8,128]{2,1,0:T(8,128)(2,1)S(1)}, u32[]{:S(2)}, u32[]{:S(2)}) collective-permute-start(bf16[128,8,128]{2,1,0:T(8,128)(2,1)S(1)} %get-tuple-element.90), channel_id=1, source_target_pairs={{0,3},{1,4},{2,5},{3,6},{4,7},{5,0},{6,1},{7,2},{8,11},{9,12},{10,... | collective-permute-start | bytes 786440 | tf_op jit(solution)/shard_map/cond/branch_0_fun/ppermute | solution.py:291
  50.0 37.2 %collective-permute-start.10 = (bf16[128,8,128]{2,1,0:T(8,128)(2,1)S(1)}, bf16[128,8,128]{2,1,0:T(8,128)(2,1)S(1)}, u32[]{:S(2)}, u32[]{:S(2)}) collective-permute-start(bf16[128,8,128]{2,1,0:T(8,128)(2,1)S(1)} %get-tuple-element.89), channel_id=1, source_target_pairs={{0,4},{1,5},{2,6},{3,7},{4,0},{5,1},{6,2},{7,3},{8,12},{9,13},{10,... | collective-permute-start | bytes 786440 | tf_op jit(solution)/shard_map/cond/branch_0_fun/ppermute | solution.py:291
  53.3 33.9 %collective-permute-start.11 = (bf16[128,8,128]{2,1,0:T(8,128)(2,1)S(1)}, bf16[128,8,128]{2,1,0:T(8,128)(2,1)S(1)}, u32[]{:S(2)}, u32[]{:S(2)}) collective-permute-start(bf16[128,8,128]{2,1,0:T(8,128)(2,1)S(1)} %get-tuple-element.88), channel_id=1, source_target_pairs={{0,5},{1,6},{2,7},{3,0},{4,1},{5,2},{6,3},{7,4},{8,13},{9,14},{10,... | collective-permute-start | bytes 786440 | tf_op jit(solution)/shard_map/cond/branch_0_fun/ppermute | solution.py:291
  55.3 38.8 %collective-permute-start.12 = (bf16[128,8,128]{2,1,0:T(8,128)(2,1)S(1)}, bf16[128,8,128]{2,1,0:T(8,128)(2,1)S(1)}, u32[]{:S(2)}, u32[]{:S(2)}) collective-permute-start(bf16[128,8,128]{2,1,0:T(8,128)(2,1)S(1)} %get-tuple-element.87), channel_id=1, source_target_pairs={{0,6},{1,7},{2,0},{3,1},{4,2},{5,3},{6,4},{7,5},{8,14},{9,15},{10,... | collective-permute-start | bytes 786440 | tf_op jit(solution)/shard_map/cond/branch_0_fun/ppermute | solution.py:291
  61.2 37.4 %collective-permute-start.13 = (bf16[128,8,128]{2,1,0:T(8,128)(2,1)S(1)}, bf16[128,8,128]{2,1,0:T(8,128)(2,1)S(1)}, u32[]{:S(2)}, u32[]{:S(2)}) collective-permute-start(bf16[128,8,128]{2,1,0:T(8,128)(2,1)S(1)} %get-tuple-element.86), channel_id=1, source_target_pairs={{0,7},{1,0},{2,1},{3,2},{4,3},{5,4},{6,5},{7,6},{8,15},{9,8},{10,9... | collective-permute-start | bytes 786440 | tf_op jit(solution)/shard_map/cond/branch_0_fun/ppermute | solution.py:291
  106.7 1.3 copy-start.3
  108.0 70.4 %all-to-all-start.8 = ((bf16[32,32,8,128]{3,2,1,0:T(8,128)(2,1)}), bf16[32,32,8,128]{3,2,1,0:T(8,128)(2,1)S(1)}, u32[]{:S(2)}, u32[]{:S(2)}) async-start(bf16[32,32,8,128]{3,2,1,0:T(8,128)(2,1)} %bitcast.43), calls=%async_computation.8 | async-start | bytes 4194304 | tf_op jit(solution)/shard_map/cond/branch_0_fun/all_to_all | solution.py:233
  114.9 10.2 %collective-permute-start = (bf16[128,8,128]{2,1,0:T(8,128)(2,1)S(1)}, bf16[128,8,128]{2,1,0:T(8,128)(2,1)S(1)}, u32[]{:S(2)}, u32[]{:S(2)}) collective-permute-start(bf16[128,8,128]{2,1,0:T(8,128)(2,1)S(1)} %get-tuple-element.100), channel_id=1, source_target_pairs={{0,1},{1,2},{2,3},{3,4},{4,5},{5,6},{6,7},{7,0},{8,9},{9,10},{10,1... | collective-permute-start | bytes 786440 | tf_op jit(solution)/shard_map/cond/branch_0_fun/ppermute | solution.py:291
  116.3 20.3 %collective-permute-start.1 = (bf16[128,8,128]{2,1,0:T(8,128)(2,1)S(1)}, bf16[128,8,128]{2,1,0:T(8,128)(2,1)S(1)}, u32[]{:S(2)}, u32[]{:S(2)}) collective-permute-start(bf16[128,8,128]{2,1,0:T(8,128)(2,1)S(1)} %get-tuple-element.99), channel_id=1, source_target_pairs={{0,2},{1,3},{2,4},{3,5},{4,6},{5,7},{6,0},{7,1},{8,10},{9,11},{10,... | collective-permute-start | bytes 786440 | tf_op jit(solution)/shard_map/cond/branch_0_fun/ppermute | solution.py:291
  118.2 33.0 %collective-permute-start.2 = (bf16[128,8,128]{2,1,0:T(8,128)(2,1)S(1)}, bf16[128,8,128]{2,1,0:T(8,128)(2,1)S(1)}, u32[]{:S(2)}, u32[]{:S(2)}) collective-permute-start(bf16[128,8,128]{2,1,0:T(8,128)(2,1)S(1)} %get-tuple-element.98), channel_id=1, source_target_pairs={{0,3},{1,4},{2,5},{3,6},{4,7},{5,0},{6,1},{7,2},{8,11},{9,12},{10,... | collective-permute-start | bytes 786440 | tf_op jit(solution)/shard_map/cond/branch_0_fun/ppermute | solution.py:291
  120.7 40.6 %collective-permute-start.3 = (bf16[128,8,128]{2,1,0:T(8,128)(2,1)S(1)}, bf16[128,8,128]{2,1,0:T(8,128)(2,1)S(1)}, u32[]{:S(2)}, u32[]{:S(2)}) collective-permute-start(bf16[128,8,128]{2,1,0:T(8,128)(2,1)S(1)} %get-tuple-element.97), channel_id=1, source_target_pairs={{0,4},{1,5},{2,6},{3,7},{4,0},{5,1},{6,2},{7,3},{8,12},{9,13},{10,... | collective-permute-start | bytes 786440 | tf_op jit(solution)/shard_map/cond/branch_0_fun/ppermute | solution.py:291
  121.9 39.4 %collective-permute-start.4 = (bf16[128,8,128]{2,1,0:T(8,128)(2,1)S(1)}, bf16[128,8,128]{2,1,0:T(8,128)(2,1)S(1)}, u32[]{:S(2)}, u32[]{:S(2)}) collective-permute-start(bf16[128,8,128]{2,1,0:T(8,128)(2,1)S(1)} %get-tuple-element.96), channel_id=1, source_target_pairs={{0,5},{1,6},{2,7},{3,0},{4,1},{5,2},{6,3},{7,4},{8,13},{9,14},{10,... | collective-permute-start | bytes 786440 | tf_op jit(solution)/shard_map/cond/branch_0_fun/ppermute | solution.py:291
  125.1 41.1 %collective-permute-start.5 = (bf16[128,8,128]{2,1,0:T(8,128)(2,1)S(1)}, bf16[128,8,128]{2,1,0:T(8,128)(2,1)S(1)}, u32[]{:S(2)}, u32[]{:S(2)}) collective-permute-start(bf16[128,8,128]{2,1,0:T(8,128)(2,1)S(1)} %get-tuple-element.95), channel_id=1, source_target_pairs={{0,6},{1,7},{2,0},{3,1},{4,2},{5,3},{6,4},{7,5},{8,14},{9,15},{10,... | collective-permute-start | bytes 786440 | tf_op jit(solution)/shard_map/cond/branch_0_fun/ppermute | solution.py:291
  136.6 32.4 %collective-permute-start.6 = (bf16[128,8,128]{2,1,0:T(8,128)(2,1)S(1)}, bf16[128,8,128]{2,1,0:T(8,128)(2,1)S(1)}, u32[]{:S(2)}, u32[]{:S(2)}) collective-permute-start(bf16[128,8,128]{2,1,0:T(8,128)(2,1)S(1)} %get-tuple-element.94), channel_id=1, source_target_pairs={{0,7},{1,0},{2,1},{3,2},{4,3},{5,4},{6,5},{7,6},{8,15},{9,8},{10,9... | collective-permute-start | bytes 786440 | tf_op jit(solution)/shard_map/cond/branch_0_fun/ppermute | solution.py:291
  169.0 46.5 %copy-start.13 = (bf16[32,64,128]{2,1,0:T(8,128)(2,1)S(1)}, bf16[32,64,128]{2,1,0:T(8,128)(2,1)}, u32[]{:S(2)}) copy-start(bf16[32,64,128]{2,1,0:T(8,128)(2,1)} %get-tuple-element.54.weights_ref) | copy-start | bytes 1572868 | tf_op jit(solution)/shard_map/cond
  177.1 1.3 copy-start.4
  178.5 37.1 %copy-start.10 = (bf16[2048,1024]{1,0:T(8,128)(2,1)S(1)}, bf16[2048,1024]{1,0:T(8,128)(2,1)}, u32[]{:S(2)}) copy-start(bf16[2048,1024]{1,0:T(8,128)(2,1)} %get-tuple-element.55.basis_ref) | copy-start | bytes 12582916 | tf_op jit(solution)/shard_map/cond
  222.4 1.3 copy-start.6
  256.5 21.7 %all-to-all-start.10 = ((f32[8,16,1024]{2,1,0:T(8,128)}), f32[8,16,1024]{2,1,0:T(8,128)S(1)}, u32[]{:S(2)}, u32[]{:S(2)}) async-start(f32[8,16,1024]{2,1,0:T(8,128)} %broadcast_in_dim.24), calls=%async_computation.10 | async-start | bytes 1048576 | tf_op jit(solution)/shard_map/cond/branch_0_fun/all_to_all | solution.py:233
  279.5 22.5 %all-to-all-start.11 = ((bf16[32,16,1152]{2,1,0:T(8,128)(2,1)}), bf16[32,16,1152]{2,1,0:T(8,128)(2,1)S(1)}, u32[]{:S(2)}, u32[]{:S(2)}) async-start(bf16[32,16,1152]{2,1,0:T(8,128)(2,1)} %broadcast_in_dim.25), calls=%async_computation.11 | async-start | bytes 2359296 | tf_op jit(solution)/shard_map/cond/branch_0_fun/all_to_all | solution.py:233
  283.6 19.5 %copy-start.7 = (bf16[2048,512]{1,0:T(8,128)(2,1)S(1)}, bf16[2048,512]{1,0:T(8,128)(2,1)}, u32[]{:S(2)}) copy-start(bf16[2048,512]{1,0:T(8,128)(2,1)} %copy-done.6) | copy-start | bytes 6291460 | tf_op jit(solution)/shard_map/cond
  283.6 19.5 %copy-start.15 = (f32[1024]{0:T(1024)S(1)}, f32[1024]{0:T(1024)}, u32[]{:S(2)}) copy-start(f32[1024]{0:T(1024)} %get-tuple-element.58) | copy-start | bytes 12292 | tf_op jit(solution)/shard_map/cond
  309.9 2.0 copy-start.12

commit v4 on v3

--- a/solution.py
+++ b/solution.py
@@ -94,13 +94,29 @@
     )(here, codes)
 
 
-def pick_kernel(halves, row_tiles, words_ref, *refs):
-    sources, outs = refs[:halves], refs[halves:]
+def pick_kernel(halves, parts, row_tiles, words_ref, *refs):
+    inputs, rest = refs[:halves * parts], refs[halves * parts:]
+    outs, sources, sems = rest[:halves], rest[halves:2 * halves], rest[2 * halves]
     count = outs[0].shape[0]
     start = pl.program_id(0) * (count // row_tiles) * LANES
     lane = lax.broadcasted_iota(jnp.int32, (ROWS, LANES), 1)
     low = lane < TILE
     bit = jnp.where(low, 1 << 24, 1 << 25)
+
+    @pl.when(pl.program_id(0) == 0)
+    def _():
+        size = sources[0].shape[0] // parts
+        copies = [
+            pltpu.make_async_copy(
+                inputs[h * parts + p], sources[h].at[pl.ds(p * size, size)], sems.at[h * parts + p]
+            )
+            for h in range(halves)
+            for p in range(parts)
+        ]
+        for copy in copies:
+            copy.start()
+        for copy in copies:
+            copy.wait()
 
     for row in range(count // row_tiles):
         def tile(k, carry):
@@ -118,26 +134,30 @@
         lax.fori_loop(0, row_tiles, tile, 0, unroll=16)
 
 
+def in_hbm(shape, dtype, interpret):
+    return jax.ShapeDtypeStruct(shape, dtype) if interpret else pltpu.HBM(shape, dtype)
+
+
 def pick(words, sources, row_tiles, interpret=False):
     count = words.shape[0] // LANES * row_tiles
     step = min(128, count)
-    shape = jax.ShapeDtypeStruct((count, ROWS, LANES), BF16)
+    halves, parts = len(sources), len(sources[0])
+    size = parts * sources[0][0].shape[0]
     return pl.pallas_call(
-        functools.partial(pick_kernel, len(sources), row_tiles),
-        out_shape=[shape] * len(sources),
+        functools.partial(pick_kernel, halves, parts, row_tiles),
+        out_shape=[in_hbm((count, ROWS, LANES), BF16, interpret)] * halves,
         grid_spec=pltpu.PrefetchScalarGridSpec(
             num_scalar_prefetch=1,
             grid=(count // step,),
-            in_specs=[
-                pl.BlockSpec(source.shape, lambda i, words: (0, 0, 0), pipeline_mode=pl.Buffered(1))
-                for source in sources
-            ],
-            out_specs=[pl.BlockSpec((step, ROWS, LANES), lambda i, words: (i, 0, 0))] * len(sources),
+            in_specs=[pl.BlockSpec(memory_space=pl.ANY)] * (halves * parts),
+            out_specs=[pl.BlockSpec((step, ROWS, LANES), lambda i, words: (i, 0, 0))] * halves,
+            scratch_shapes=[pltpu.VMEM((size, ROWS, LANES), BF16)] * halves
+            + [pltpu.SemaphoreType.DMA((halves * parts,))],
         ),
         compiler_params=pltpu.CompilerParams(vmem_limit_bytes=40 << 20),
         name="pick",
         interpret=interpret,
-    )(words, *sources)
+    )(words, *[part for source in sources for part in source])
 
 
 def project_kernel(group, counts_ref, first_ref, second_ref, weights_ref, basis_ref, remapped_ref, partial_ref):
@@ -176,8 +196,8 @@
     return pl.pallas_call(
         functools.partial(project_kernel, group),
         out_shape=(
-            jax.ShapeDtypeStruct((cells, snaps), BF16),
-            jax.ShapeDtypeStruct((owners, 2, ROWS, rank), F32),
+            in_hbm((cells, snaps), BF16, interpret),
+            in_hbm((owners, 2, ROWS, rank), F32, interpret),
         ),
         grid_spec=pltpu.PrefetchScalarGridSpec(
             num_scalar_prefetch=1,
@@ -213,7 +233,7 @@
     resident = lambda i: (0, 0)
     return pl.pallas_call(
         functools.partial(rotate_kernel, 1.0 / math.sqrt(snaps)),
-        out_shape=jax.ShapeDtypeStruct((cells, rank), BF16),
+        out_shape=in_hbm((cells, rank), BF16, interpret),
         grid=(cells // rows,),
         in_specs=[
             pl.BlockSpec((rows, snaps), lambda i: (i, 0)),
@@ -280,10 +300,10 @@
         blocks = jnp.maximum(codes, 0)
         words = pair_words_plain(blocks).reshape(-1)
         sources = [spread(c, "space").reshape(-1, ROWS, LANES) for c in local]
-        return finish([pick(words, [source], tiles, interpret)[0] for source in sources])
+        return finish([pick(words, [[source]], tiles, interpret)[0] for source in sources])
 
     def sparse():
-        sent = pick(asked_words, local, LANES // MAXB, interpret)
+        sent = pick(asked_words, [[c] for c in local], LANES // MAXB, interpret)
         came = []
         for c in sent:
             c = c.reshape(spaces, -1, ROWS, LANES)
@@ -291,11 +311,11 @@
                 lax.ppermute(c[d], "space", [(i, (i + d) % spaces) for i in range(spaces)])
                 for d in range(1, spaces)
             ]
-            came.append(jnp.concatenate(parts, axis=0))
+            came.append(parts)
         words = local_words.reshape(-1)
         chosen = []
         for c in came:
-            chosen += pick(words, [c.reshape(-1, ROWS, LANES)], tiles, interpret)
+            chosen += pick(words, [c], tiles, interpret)
         return finish(chosen)
 
     return lax.cond(overflow, dense, sparse)

time: 313 us -> 317 us (1.013)
  local copies, waits for them, and re-layouts: 14.9 us -> 8.82 us
  Pallas kernels: 41.5 us -> 47.4 us
  waiting for transfers between devices: 127 us -> 132 us
    cond x28 -> x6, local copies, waits for them, and re-layouts: 5.55 us -> 0.02 us
    ppermute x14, waiting for transfers between devices: 78.9 us -> 84 us  [sparse(): lax.ppermute(c[d], 'space', [(i, (i + d) % spaces) for i in range(spaces)])]
    pallas_call x4, Pallas kernels: 31.5 us -> 35.9 us  [the longest x3 27.7 us: pick(): pl.pallas_call(functools.partial(pick_kernel, halves, parts, row_tiles),...]
where the time goes in v4:
time: 317 us; the launch traced here: 316 us
  waiting for transfers between devices  132 us (42%)
  blocking collectives  68.7 us (22%)
  starting transfers between devices  55.3 us (17%)
  Pallas kernels  47.4 us (15%)
  local copies, waits for them, and re-layouts  8.82 us (3%)
    ppermute x14, waiting for transfers between devices, sparse(): lax.ppermute(c[d], 'space', [(i, (i + d) % spaces) for i in range(spaces)])  84 us
    all_to_all x2, blocking collectives, exchange(): return lax.all_to_all(array, axis, split_axis=0, concat_axis=0, tiled=True)  68.7 us
    all_to_all x5, waiting for transfers between devices, exchange(): return lax.all_to_all(array, axis, split_axis=0, concat_axis=0, tiled=True)  48.4 us
    all_to_all x5, starting transfers between devices, exchange(): return lax.all_to_all(array, axis, split_axis=0, concat_axis=0, tiled=True)  31.3 us
    pallas_call x3, Pallas kernels, pick(): pl.pallas_call(functools.partial(pick_kernel, halves, parts, row_tiles),...  27.7 us
    ppermute x14, starting transfers between devices, sparse(): lax.ppermute(c[d], 'space', [(i, (i + d) % spaces) for i in range(spaces)])  24 us
    pallas_call x1, Pallas kernels, project(): pl.pallas_call(functools.partial(project_kernel, group), out_shape=(in_hb...  8.26 us
    pallas_call x1, Pallas kernels, rotate(): pl.pallas_call(functools.partial(rotate_kernel, 1.0 / math.sqrt(snaps)),...  8.04 us
  transfers between devices with their start and end apart: 19, of which 14 were waited for; matrix products, arithmetic and copies ran while one was open for 1% of the time, Pallas kernels for 3%

profile of v4, /device:TPU:1, one launch (start us, length us, event | category | flops | bytes accessed | tf_op | source)
XLA Modules:
  0.0 315.7 jit_solution(18354817165176190518)
XLA Ops:
  0.6 0.7 compare_select_fusion
  1.5 0.6 broadcast_in_dim.37
  2.1 8.6 %all-to-all-start.12 = ((s32[32,1,128]{2,1,0:T(1,128)}), s32[32,1,128]{2,1,0:T(1,128)S(1)}, u32[]{:S(2)}, u32[]{:S(2)}) async-start(s32[32,1,128]{2,1,0:T(1,128)} %broadcast_in_dim.37), calls=%async_computation.12 | async-start | bytes 32768 | tf_op jit(solution)/shard_map/all_to_all | solution.py:253
  10.7 6.9 %all-to-all-done.12 = s32[32,1,128]{2,1,0:T(1,128)S(1)} async-done(((s32[32,1,128]{2,1,0:T(1,128)}), s32[32,1,128]{2,1,0:T(1,128)S(1)}, u32[]{:S(2)}, u32[]{:S(2)}) %all-to-all-start.12) | async-done | bytes 16416 | tf_op jit(solution)/shard_map/all_to_all | solution.py:253
  17.6 3.4 %route.1 = (s32[8,8,128]{2,1,0:T(8,128)}, s32[32,128]{1,0:T(8,128)S(1)}) custom-call(s32[1]{0:T(128)} %bitcast.23.here_ref, s32[32,128]{1,0:T(8,128)S(1)} %bitcast.51), custom_call_target="tpu_custom_call" | custom-call | tf_op jit(solution)/shard_map/route/pallas_call | solution.py:84
  21.0 8.2 %all-to-all-start.13 = ((s32[8,8,128]{2,1,0:T(8,128)}), s32[8,8,128]{2,1,0:T(8,128)S(1)}, u32[]{:S(2)}, u32[]{:S(2)}) async-start(s32[8,8,128]{2,1,0:T(8,128)} %get-tuple-element.73), calls=%async_computation.13 | async-start | bytes 65536 | tf_op jit(solution)/shard_map/all_to_all | solution.py:253
  29.2 1.7 slice_bitcast_fusion.4
  31.0 5.1 %all-to-all-done.13 = s32[8,8,128]{2,1,0:T(8,128)S(1)} async-done(((s32[8,8,128]{2,1,0:T(8,128)}), s32[8,8,128]{2,1,0:T(8,128)S(1)}, u32[]{:S(2)}, u32[]{:S(2)}) %all-to-all-start.13) | async-done | bytes 32800 | tf_op jit(solution)/shard_map/all_to_all | solution.py:253
  36.1 0.6 slice_reduce_fusion
  37.4 278.3 %conditional.1 = (bf16[2048,1024]{1,0:T(8,128)(2,1)}, f32[128,512]{1,0:T(8,128)}) conditional(s32[]{:T(128)} %convert_element_type.33, (s32[32,128]{1,0:T(8,128)S(1)}, s32[]{:T(128)}, s32[16,8,128]{2,1,0:T(8,128)S(1)}, bf16[512,8,128]{2,1,0:T(8,128)(2,1)S(1)}, bf16[512,8,128]{2,1,0:T(8,128)(2,1)S(1)}, /*index=5*/s32[32]{0:T(128)S(1)}, ...), branch_computations={%region_1.4_spmd, %region_4.7_spmd} | conditional | flops 989190 | bytes 151613616 | solution.py:321
  37.4 9.5 %pick.5 = (bf16[1024,8,128]{2,1,0:T(8,128)(2,1)}, bf16[1024,8,128]{2,1,0:T(8,128)(2,1)}) custom-call(s32[2048]{0:T(1024)S(1)} %bitcast.41, bf16[512,8,128]{2,1,0:T(8,128)(2,1)S(1)} %get-tuple-element.50.refs_0_, bf16[512,8,128]{2,1,0:T(8,128)(2,1)S(1)} %get-tuple-element.51.refs_1_), custom_call_target="tpu_custom_call" | custom-call | tf_op jit(solution)/shard_map/cond/branch_0_fun/pick/pallas_call | solution.py:146
  46.9 1.7 fusion.4
  48.6 0.6 collective-permute-start.10
  49.2 3.9 %collective-permute-start.11 = (bf16[128,8,128]{2,1,0:T(8,128)(2,1)S(1)}, bf16[128,8,128]{2,1,0:T(8,128)(2,1)S(1)}, u32[]{:S(2)}, u32[]{:S(2)}) collective-permute-start(bf16[128,8,128]{2,1,0:T(8,128)(2,1)S(1)} %get-tuple-element.88), channel_id=1, source_target_pairs={{0,5},{1,6},{2,7},{3,0},{4,1},{5,2},{6,3},{7,4},{8,13},{9,14},{10,... | collective-permute-start | bytes 786440 | tf_op jit(solution)/shard_map/cond/branch_0_fun/ppermute | solution.py:311
  53.2 1.2 collective-permute-start.12
  54.7 1.1 collective-permute-start.7
  55.8 5.2 %collective-permute-done.10.refs_4_ = bf16[128,8,128]{2,1,0:T(8,128)(2,1)S(1)} collective-permute-done((bf16[128,8,128]{2,1,0:T(8,128)(2,1)S(1)}, bf16[128,8,128]{2,1,0:T(8,128)(2,1)S(1)}, u32[]{:S(2)}, u32[]{:S(2)}) %collective-permute-start.10) | collective-permute-done | bytes 262176 | tf_op jit(solution)/shard_map/cond/branch_0_fun/ppermute | solution.py:311
  61.0 1.3 collective-permute-start.8
  62.3 17.8 %collective-permute-done.11.refs_5_ = bf16[128,8,128]{2,1,0:T(8,128)(2,1)S(1)} collective-permute-done((bf16[128,8,128]{2,1,0:T(8,128)(2,1)S(1)}, bf16[128,8,128]{2,1,0:T(8,128)(2,1)S(1)}, u32[]{:S(2)}, u32[]{:S(2)}) %collective-permute-start.11) | collective-permute-done | bytes 262176 | tf_op jit(solution)/shard_map/cond/branch_0_fun/ppermute | solution.py:311
  80.1 3.4 %collective-permute-start.9 = (bf16[128,8,128]{2,1,0:T(8,128)(2,1)S(1)}, bf16[128,8,128]{2,1,0:T(8,128)(2,1)S(1)}, u32[]{:S(2)}, u32[]{:S(2)}) collective-permute-start(bf16[128,8,128]{2,1,0:T(8,128)(2,1)S(1)} %get-tuple-element.90), channel_id=1, source_target_pairs={{0,3},{1,4},{2,5},{3,6},{4,7},{5,0},{6,1},{7,2},{8,11},{9,12},{10,... | collective-permute-start | bytes 786440 | tf_op jit(solution)/shard_map/cond/branch_0_fun/ppermute | solution.py:311
  83.5 8.4 %collective-permute-done.12.refs_6_ = bf16[128,8,128]{2,1,0:T(8,128)(2,1)S(1)} collective-permute-done((bf16[128,8,128]{2,1,0:T(8,128)(2,1)S(1)}, bf16[128,8,128]{2,1,0:T(8,128)(2,1)S(1)}, u32[]{:S(2)}, u32[]{:S(2)}) %collective-permute-start.12) | collective-permute-done | bytes 262176 | tf_op jit(solution)/shard_map/cond/branch_0_fun/ppermute | solution.py:311
  91.8 3.4 %collective-permute-done.13.refs_7_ = bf16[128,8,128]{2,1,0:T(8,128)(2,1)S(1)} collective-permute-done((bf16[128,8,128]{2,1,0:T(8,128)(2,1)S(1)}, bf16[128,8,128]{2,1,0:T(8,128)(2,1)S(1)}, u32[]{:S(2)}, u32[]{:S(2)}) %collective-permute-start.13) | collective-permute-done | bytes 262176 | tf_op jit(solution)/shard_map/cond/branch_0_fun/ppermute | solution.py:311
  95.3 6.7 %collective-permute-done.9.refs_3_ = bf16[128,8,128]{2,1,0:T(8,128)(2,1)S(1)} collective-permute-done((bf16[128,8,128]{2,1,0:T(8,128)(2,1)S(1)}, bf16[128,8,128]{2,1,0:T(8,128)(2,1)S(1)}, u32[]{:S(2)}, u32[]{:S(2)}) %collective-permute-start.9) | collective-permute-done | bytes 262176 | tf_op jit(solution)/shard_map/cond/branch_0_fun/ppermute | solution.py:311
  102.0 9.1 %pick.7 = bf16[1024,8,128]{2,1,0:T(8,128)(2,1)} custom-call(s32[4096]{0:T(1024)S(1)} %bitcast.54, bf16[128,8,128]{2,1,0:T(8,128)(2,1)S(1)} %get-tuple-element.93.refs_0_, bf16[128,8,128]{2,1,0:T(8,128)(2,1)S(1)} %collective-permute-done.7.refs_1_, bf16[128,8,128]{2,1,0:T(8,128)(2,1)S(1)} %collective-permute-done.8.refs_2_, ...), custom_call_target="tpu_custom_call" | custom-call | tf_op jit(solution)/shard_map/cond/branch_0_fun/pick/pallas_call | solution.py:146
  111.1 5.1 %all-to-all-start.8 = ((bf16[32,32,8,128]{3,2,1,0:T(8,128)(2,1)}), bf16[32,32,8,128]{3,2,1,0:T(8,128)(2,1)S(1)}, u32[]{:S(2)}, u32[]{:S(2)}) async-start(bf16[32,32,8,128]{3,2,1,0:T(8,128)(2,1)} %bitcast.44), calls=%async_computation.8 | async-start | bytes 4194304 | tf_op jit(solution)/shard_map/cond/branch_0_fun/all_to_all | solution.py:253
  116.2 1.7 fusion.5
  117.9 3.1 collective-permute-start
  121.0 0.4 collective-permute-start.1
  121.4 0.7 collective-permute-start.2
  122.1 4.9 %collective-permute-start.3 = (bf16[128,8,128]{2,1,0:T(8,128)(2,1)S(1)}, bf16[128,8,128]{2,1,0:T(8,128)(2,1)S(1)}, u32[]{:S(2)}, u32[]{:S(2)}) collective-permute-start(bf16[128,8,128]{2,1,0:T(8,128)(2,1)S(1)} %get-tuple-element.97), channel_id=1, source_target_pairs={{0,4},{1,5},{2,6},{3,7},{4,0},{5,1},{6,2},{7,3},{8,12},{9,13},{10,... | collective-permute-start | bytes 786440 | tf_op jit(solution)/shard_map/cond/branch_0_fun/ppermute | solution.py:311
  127.3 2.8 collective-permute-start.5
  130.1 9.1 %collective-permute-done.1.refs_2_ = bf16[128,8,128]{2,1,0:T(8,128)(2,1)S(1)} collective-permute-done((bf16[128,8,128]{2,1,0:T(8,128)(2,1)S(1)}, bf16[128,8,128]{2,1,0:T(8,128)(2,1)S(1)}, u32[]{:S(2)}, u32[]{:S(2)}) %collective-permute-start.1) | collective-permute-done | bytes 262176 | tf_op jit(solution)/shard_map/cond/branch_0_fun/ppermute | solution.py:311
  139.2 12.8 %collective-permute-done.2.refs_3_ = bf16[128,8,128]{2,1,0:T(8,128)(2,1)S(1)} collective-permute-done((bf16[128,8,128]{2,1,0:T(8,128)(2,1)S(1)}, bf16[128,8,128]{2,1,0:T(8,128)(2,1)S(1)}, u32[]{:S(2)}, u32[]{:S(2)}) %collective-permute-start.2) | collective-permute-done | bytes 262176 | tf_op jit(solution)/shard_map/cond/branch_0_fun/ppermute | solution.py:311
  152.0 15.4 %collective-permute-done.3.refs_4_ = bf16[128,8,128]{2,1,0:T(8,128)(2,1)S(1)} collective-permute-done((bf16[128,8,128]{2,1,0:T(8,128)(2,1)S(1)}, bf16[128,8,128]{2,1,0:T(8,128)(2,1)S(1)}, u32[]{:S(2)}, u32[]{:S(2)}) %collective-permute-start.3) | collective-permute-done | bytes 262176 | tf_op jit(solution)/shard_map/cond/branch_0_fun/ppermute | solution.py:311
  167.4 0.7 collective-permute-done.5.refs_6_
  168.0 4.5 %collective-permute-done.6.refs_7_ = bf16[128,8,128]{2,1,0:T(8,128)(2,1)S(1)} collective-permute-done((bf16[128,8,128]{2,1,0:T(8,128)(2,1)S(1)}, bf16[128,8,128]{2,1,0:T(8,128)(2,1)S(1)}, u32[]{:S(2)}, u32[]{:S(2)}) %collective-permute-start.6) | collective-permute-done | bytes 262176 | tf_op jit(solution)/shard_map/cond/branch_0_fun/ppermute | solution.py:311
  172.5 9.1 %pick.6 = bf16[1024,8,128]{2,1,0:T(8,128)(2,1)} custom-call(s32[4096]{0:T(1024)S(1)} %bitcast.55, bf16[128,8,128]{2,1,0:T(8,128)(2,1)S(1)} %get-tuple-element.101.refs_0_, bf16[128,8,128]{2,1,0:T(8,128)(2,1)S(1)} %collective-permute-done.refs_1_, bf16[128,8,128]{2,1,0:T(8,128)(2,1)S(1)} %collective-permute-done.1.refs_2_, ...), custom_call_target="tpu_custom_call" | custom-call | tf_op jit(solution)/shard_map/cond/branch_0_fun/pick/pallas_call | solution.py:146
  181.6 36.7 %all_to_all.58.first_ref = bf16[32,32,8,128]{3,2,1,0:T(8,128)(2,1)S(1)} all-to-all(bf16[32,32,8,128]{3,2,1,0:T(8,128)(2,1)} %bitcast.45), channel_id=1, replica_groups=mesh['tm'=32,'space'=8] {'tm'}, dimensions={0} | all-to-all | bytes 4194304 | tf_op jit(solution)/shard_map/cond/branch_0_fun/all_to_all | solution.py:253
  218.3 8.3 %project.2 = (bf16[2048,512]{1,0:T(8,128)(2,1)}, f32[32,2,8,1024]{3,2,1,0:T(8,128)}) custom-call(s32[32]{0:T(128)S(1)} %get-tuple-element.46.counts_ref, bf16[32,32,8,128]{3,2,1,0:T(8,128)(2,1)S(1)} %all_to_all.58.first_ref, bf16[32,32,8,128]{3,2,1,0:T(8,128)(2,1)S(1)} %all-to-all-done.8.second_ref, bf16[32,64,128]{2,1,0:T(8,128)(2,1)S(1)} %get-tuple-element.54.weights_ref, ...), custom_call_target="tpu_custom_call" | custom-call | tf_op jit(solution)/shard_map/cond/branch_0_fun/project/pallas_call | solution.py:196
  226.6 32.1 %all_to_all.59 = f32[32,16,1024]{2,1,0:T(8,128)S(1)} all-to-all(f32[32,16,1024]{2,1,0:T(8,128)} %bitcast.47), channel_id=1, replica_groups=mesh['tm'=32,'space'=8] {'tm'}, dimensions={0} | all-to-all | bytes 4194304 | tf_op jit(solution)/shard_map/cond/branch_0_fun/all_to_all | solution.py:253
  258.7 0.8 broadcast_in_dim.24
  259.6 5.3 %all-to-all-start.10 = ((f32[8,16,1024]{2,1,0:T(8,128)}), f32[8,16,1024]{2,1,0:T(8,128)S(1)}, u32[]{:S(2)}, u32[]{:S(2)}) async-start(f32[8,16,1024]{2,1,0:T(8,128)} %broadcast_in_dim.24), calls=%async_computation.10 | async-start | bytes 1048576 | tf_op jit(solution)/shard_map/cond/branch_0_fun/all_to_all | solution.py:253
  264.9 18.0 %all-to-all-done.10 = f32[8,16,1024]{2,1,0:T(8,128)S(1)} async-done(((f32[8,16,1024]{2,1,0:T(8,128)}), f32[8,16,1024]{2,1,0:T(8,128)S(1)}, u32[]{:S(2)}, u32[]{:S(2)}) %all-to-all-start.10) | async-done | bytes 524320 | tf_op jit(solution)/shard_map/cond/branch_0_fun/all_to_all | solution.py:253
  283.0 1.1 broadcast_in_dim.25
  284.1 4.1 %all-to-all-start.11 = ((bf16[32,16,1152]{2,1,0:T(8,128)(2,1)}), bf16[32,16,1152]{2,1,0:T(8,128)(2,1)S(1)}, u32[]{:S(2)}, u32[]{:S(2)}) async-start(bf16[32,16,1152]{2,1,0:T(8,128)(2,1)} %broadcast_in_dim.25), calls=%async_computation.11 | async-start | bytes 2359296 | tf_op jit(solution)/shard_map/cond/branch_0_fun/all_to_all | solution.py:253
  288.2 18.4 %all-to-all-done.11 = bf16[32,16,1152]{2,1,0:T(8,128)(2,1)S(1)} async-done(((bf16[32,16,1152]{2,1,0:T(8,128)(2,1)}), bf16[32,16,1152]{2,1,0:T(8,128)(2,1)S(1)}, u32[]{:S(2)}, u32[]{:S(2)}) %all-to-all-start.11) | async-done | bytes 1179680 | tf_op jit(solution)/shard_map/cond/branch_0_fun/all_to_all | solution.py:253
  306.7 0.8 copy.20
  307.7 8.0 %rotate.2 = bf16[2048,1024]{1,0:T(8,128)(2,1)} custom-call(bf16[2048,512]{1,0:T(8,128)(2,1)S(1)} %copy-done.1, bf16[256,1024]{1,0:T(8,128)(2,1)S(1)} %get-tuple-element.103.c0_ref, bf16[256,1024]{1,0:T(8,128)(2,1)S(1)} %get-tuple-element.102.c1_ref, bf16[2048,1024]{1,0:T(8,128)(2,1)} %get-tuple-element.55.basis_ref, f32[1,1024]{1,0:T(1,128)S(1)} %bitcast.56), custom_call_target="tpu_custom_call" | custom-call | tf_op jit(solution)/shard_map/cond/branch_0_fun/rotate/pallas_call | solution.py:234
  (30 shorter events, 1.3 us)
Async XLA Ops:
  2.1 15.5 %all-to-all-start.12 = ((s32[32,1,128]{2,1,0:T(1,128)}), s32[32,1,128]{2,1,0:T(1,128)S(1)}, u32[]{:S(2)}, u32[]{:S(2)}) async-start(s32[32,1,128]{2,1,0:T(1,128)} %broadcast_in_dim.37), calls=%async_computation.12 | async-start | bytes 32768 | tf_op jit(solution)/shard_map/all_to_all | solution.py:253
  21.0 15.1 %all-to-all-start.13 = ((s32[8,8,128]{2,1,0:T(8,128)}), s32[8,8,128]{2,1,0:T(8,128)S(1)}, u32[]{:S(2)}, u32[]{:S(2)}) async-start(s32[8,8,128]{2,1,0:T(8,128)} %get-tuple-element.73), calls=%async_computation.13 | async-start | bytes 65536 | tf_op jit(solution)/shard_map/all_to_all | solution.py:253
  29.2 8.2 %copy-start.5 = (bf16[32,64,128]{2,1,0:T(8,128)(2,1)S(1)}, bf16[32,64,128]{2,1,0:T(8,128)(2,1)}, u32[]{:S(2)}) copy-start(bf16[32,64,128]{2,1,0:T(8,128)(2,1)} %param.11) | copy-start | bytes 1572868
  29.2 8.2 %copy-start.10 = (s32[32]{0:T(128)S(1)}, s32[32]{0:T(128)}, u32[]{:S(2)}) copy-start(s32[32]{0:T(128)} %param.10) | copy-start | bytes 388
  48.6 12.4 %collective-permute-start.10 = (bf16[128,8,128]{2,1,0:T(8,128)(2,1)S(1)}, bf16[128,8,128]{2,1,0:T(8,128)(2,1)S(1)}, u32[]{:S(2)}, u32[]{:S(2)}) collective-permute-start(bf16[128,8,128]{2,1,0:T(8,128)(2,1)S(1)} %get-tuple-element.89), channel_id=1, source_target_pairs={{0,4},{1,5},{2,6},{3,7},{4,0},{5,1},{6,2},{7,3},{8,12},{9,13},{10,... | collective-permute-start | bytes 786440 | tf_op jit(solution)/shard_map/cond/branch_0_fun/ppermute | solution.py:311
  49.2 30.9 %collective-permute-start.11 = (bf16[128,8,128]{2,1,0:T(8,128)(2,1)S(1)}, bf16[128,8,128]{2,1,0:T(8,128)(2,1)S(1)}, u32[]{:S(2)}, u32[]{:S(2)}) collective-permute-start(bf16[128,8,128]{2,1,0:T(8,128)(2,1)S(1)} %get-tuple-element.88), channel_id=1, source_target_pairs={{0,5},{1,6},{2,7},{3,0},{4,1},{5,2},{6,3},{7,4},{8,13},{9,14},{10,... | collective-permute-start | bytes 786440 | tf_op jit(solution)/shard_map/cond/branch_0_fun/ppermute | solution.py:311
  53.2 38.7 %collective-permute-start.12 = (bf16[128,8,128]{2,1,0:T(8,128)(2,1)S(1)}, bf16[128,8,128]{2,1,0:T(8,128)(2,1)S(1)}, u32[]{:S(2)}, u32[]{:S(2)}) collective-permute-start(bf16[128,8,128]{2,1,0:T(8,128)(2,1)S(1)} %get-tuple-element.87), channel_id=1, source_target_pairs={{0,6},{1,7},{2,0},{3,1},{4,2},{5,3},{6,4},{7,5},{8,14},{9,15},{10,... | collective-permute-start | bytes 786440 | tf_op jit(solution)/shard_map/cond/branch_0_fun/ppermute | solution.py:311
  54.3 41.0 %collective-permute-start.13 = (bf16[128,8,128]{2,1,0:T(8,128)(2,1)S(1)}, bf16[128,8,128]{2,1,0:T(8,128)(2,1)S(1)}, u32[]{:S(2)}, u32[]{:S(2)}) collective-permute-start(bf16[128,8,128]{2,1,0:T(8,128)(2,1)S(1)} %get-tuple-element.86), channel_id=1, source_target_pairs={{0,7},{1,0},{2,1},{3,2},{4,3},{5,4},{6,5},{7,6},{8,15},{9,8},{10,9... | collective-permute-start | bytes 786440 | tf_op jit(solution)/shard_map/cond/branch_0_fun/ppermute | solution.py:311
  54.7 40.6 %collective-permute-start.7 = (bf16[128,8,128]{2,1,0:T(8,128)(2,1)S(1)}, bf16[128,8,128]{2,1,0:T(8,128)(2,1)S(1)}, u32[]{:S(2)}, u32[]{:S(2)}) collective-permute-start(bf16[128,8,128]{2,1,0:T(8,128)(2,1)S(1)} %get-tuple-element.92), channel_id=1, source_target_pairs={{0,1},{1,2},{2,3},{3,4},{4,5},{5,6},{6,7},{7,0},{8,9},{9,10},{10,1... | collective-permute-start | bytes 786440 | tf_op jit(solution)/shard_map/cond/branch_0_fun/ppermute | solution.py:311
  61.0 34.3 %collective-permute-start.8 = (bf16[128,8,128]{2,1,0:T(8,128)(2,1)S(1)}, bf16[128,8,128]{2,1,0:T(8,128)(2,1)S(1)}, u32[]{:S(2)}, u32[]{:S(2)}) collective-permute-start(bf16[128,8,128]{2,1,0:T(8,128)(2,1)S(1)} %get-tuple-element.91), channel_id=1, source_target_pairs={{0,2},{1,3},{2,4},{3,5},{4,6},{5,7},{6,0},{7,1},{8,10},{9,11},{10,... | collective-permute-start | bytes 786440 | tf_op jit(solution)/shard_map/cond/branch_0_fun/ppermute | solution.py:311
  80.1 22.0 %collective-permute-start.9 = (bf16[128,8,128]{2,1,0:T(8,128)(2,1)S(1)}, bf16[128,8,128]{2,1,0:T(8,128)(2,1)S(1)}, u32[]{:S(2)}, u32[]{:S(2)}) collective-permute-start(bf16[128,8,128]{2,1,0:T(8,128)(2,1)S(1)} %get-tuple-element.90), channel_id=1, source_target_pairs={{0,3},{1,4},{2,5},{3,6},{4,7},{5,0},{6,1},{7,2},{8,11},{9,12},{10,... | collective-permute-start | bytes 786440 | tf_op jit(solution)/shard_map/cond/branch_0_fun/ppermute | solution.py:311
  111.1 70.5 %all-to-all-start.8 = ((bf16[32,32,8,128]{3,2,1,0:T(8,128)(2,1)}), bf16[32,32,8,128]{3,2,1,0:T(8,128)(2,1)S(1)}, u32[]{:S(2)}, u32[]{:S(2)}) async-start(bf16[32,32,8,128]{3,2,1,0:T(8,128)(2,1)} %bitcast.44), calls=%async_computation.8 | async-start | bytes 4194304 | tf_op jit(solution)/shard_map/cond/branch_0_fun/all_to_all | solution.py:253
  117.9 9.4 %collective-permute-start = (bf16[128,8,128]{2,1,0:T(8,128)(2,1)S(1)}, bf16[128,8,128]{2,1,0:T(8,128)(2,1)S(1)}, u32[]{:S(2)}, u32[]{:S(2)}) collective-permute-start(bf16[128,8,128]{2,1,0:T(8,128)(2,1)S(1)} %get-tuple-element.100), channel_id=1, source_target_pairs={{0,1},{1,2},{2,3},{3,4},{4,5},{5,6},{6,7},{7,0},{8,9},{9,10},{10,1... | collective-permute-start | bytes 786440 | tf_op jit(solution)/shard_map/cond/branch_0_fun/ppermute | solution.py:311
  121.0 18.2 %collective-permute-start.1 = (bf16[128,8,128]{2,1,0:T(8,128)(2,1)S(1)}, bf16[128,8,128]{2,1,0:T(8,128)(2,1)S(1)}, u32[]{:S(2)}, u32[]{:S(2)}) collective-permute-start(bf16[128,8,128]{2,1,0:T(8,128)(2,1)S(1)} %get-tuple-element.99), channel_id=1, source_target_pairs={{0,2},{1,3},{2,4},{3,5},{4,6},{5,7},{6,0},{7,1},{8,10},{9,11},{10,... | collective-permute-start | bytes 786440 | tf_op jit(solution)/shard_map/cond/branch_0_fun/ppermute | solution.py:311
  121.4 30.6 %collective-permute-start.2 = (bf16[128,8,128]{2,1,0:T(8,128)(2,1)S(1)}, bf16[128,8,128]{2,1,0:T(8,128)(2,1)S(1)}, u32[]{:S(2)}, u32[]{:S(2)}) collective-permute-start(bf16[128,8,128]{2,1,0:T(8,128)(2,1)S(1)} %get-tuple-element.98), channel_id=1, source_target_pairs={{0,3},{1,4},{2,5},{3,6},{4,7},{5,0},{6,1},{7,2},{8,11},{9,12},{10,... | collective-permute-start | bytes 786440 | tf_op jit(solution)/shard_map/cond/branch_0_fun/ppermute | solution.py:311
  122.1 45.3 %collective-permute-start.3 = (bf16[128,8,128]{2,1,0:T(8,128)(2,1)S(1)}, bf16[128,8,128]{2,1,0:T(8,128)(2,1)S(1)}, u32[]{:S(2)}, u32[]{:S(2)}) collective-permute-start(bf16[128,8,128]{2,1,0:T(8,128)(2,1)S(1)} %get-tuple-element.97), channel_id=1, source_target_pairs={{0,4},{1,5},{2,6},{3,7},{4,0},{5,1},{6,2},{7,3},{8,12},{9,13},{10,... | collective-permute-start | bytes 786440 | tf_op jit(solution)/shard_map/cond/branch_0_fun/ppermute | solution.py:311
  127.0 40.4 %collective-permute-start.4 = (bf16[128,8,128]{2,1,0:T(8,128)(2,1)S(1)}, bf16[128,8,128]{2,1,0:T(8,128)(2,1)S(1)}, u32[]{:S(2)}, u32[]{:S(2)}) collective-permute-start(bf16[128,8,128]{2,1,0:T(8,128)(2,1)S(1)} %get-tuple-element.96), channel_id=1, source_target_pairs={{0,5},{1,6},{2,7},{3,0},{4,1},{5,2},{6,3},{7,4},{8,13},{9,14},{10,... | collective-permute-start | bytes 786440 | tf_op jit(solution)/shard_map/cond/branch_0_fun/ppermute | solution.py:311
  127.3 40.7 %collective-permute-start.5 = (bf16[128,8,128]{2,1,0:T(8,128)(2,1)S(1)}, bf16[128,8,128]{2,1,0:T(8,128)(2,1)S(1)}, u32[]{:S(2)}, u32[]{:S(2)}) collective-permute-start(bf16[128,8,128]{2,1,0:T(8,128)(2,1)S(1)} %get-tuple-element.95), channel_id=1, source_target_pairs={{0,6},{1,7},{2,0},{3,1},{4,2},{5,3},{6,4},{7,5},{8,14},{9,15},{10,... | collective-permute-start | bytes 786440 | tf_op jit(solution)/shard_map/cond/branch_0_fun/ppermute | solution.py:311
  139.2 33.3 %collective-permute-start.6 = (bf16[128,8,128]{2,1,0:T(8,128)(2,1)S(1)}, bf16[128,8,128]{2,1,0:T(8,128)(2,1)S(1)}, u32[]{:S(2)}, u32[]{:S(2)}) collective-permute-start(bf16[128,8,128]{2,1,0:T(8,128)(2,1)S(1)} %get-tuple-element.94), channel_id=1, source_target_pairs={{0,7},{1,0},{2,1},{3,2},{4,3},{5,4},{6,5},{7,6},{8,15},{9,8},{10,9... | collective-permute-start | bytes 786440 | tf_op jit(solution)/shard_map/cond/branch_0_fun/ppermute | solution.py:311
  181.6 36.7 %copy-start.3 = (bf16[2048,1024]{1,0:T(8,128)(2,1)S(1)}, bf16[2048,1024]{1,0:T(8,128)(2,1)}, u32[]{:S(2)}) copy-start(bf16[2048,1024]{1,0:T(8,128)(2,1)} %get-tuple-element.55.basis_ref) | copy-start | bytes 12582916 | tf_op jit(solution)/shard_map/cond
  259.6 23.3 %all-to-all-start.10 = ((f32[8,16,1024]{2,1,0:T(8,128)}), f32[8,16,1024]{2,1,0:T(8,128)S(1)}, u32[]{:S(2)}, u32[]{:S(2)}) async-start(f32[8,16,1024]{2,1,0:T(8,128)} %broadcast_in_dim.24), calls=%async_computation.10 | async-start | bytes 1048576 | tf_op jit(solution)/shard_map/cond/branch_0_fun/all_to_all | solution.py:253
  284.1 22.5 %all-to-all-start.11 = ((bf16[32,16,1152]{2,1,0:T(8,128)(2,1)}), bf16[32,16,1152]{2,1,0:T(8,128)(2,1)S(1)}, u32[]{:S(2)}, u32[]{:S(2)}) async-start(bf16[32,16,1152]{2,1,0:T(8,128)(2,1)} %broadcast_in_dim.25), calls=%async_computation.11 | async-start | bytes 2359296 | tf_op jit(solution)/shard_map/cond/branch_0_fun/all_to_all | solution.py:253
  288.2 19.5 %copy-start.1 = (bf16[2048,512]{1,0:T(8,128)(2,1)S(1)}, bf16[2048,512]{1,0:T(8,128)(2,1)}, u32[]{:S(2)}) copy-start(bf16[2048,512]{1,0:T(8,128)(2,1)} %get-tuple-element.57.remapped_ref) | copy-start | bytes 6291460 | tf_op jit(solution)/shard_map/cond
  288.2 19.5 %copy-start.8 = (f32[1024]{0:T(1024)S(1)}, f32[1024]{0:T(1024)}, u32[]{:S(2)}) copy-start(f32[1024]{0:T(1024)} %get-tuple-element.58) | copy-start | bytes 12292 | tf_op jit(solution)/shard_map/cond

commit v5 on v4

--- a/solution.py
+++ b/solution.py
@@ -15,6 +15,7 @@
 ROWS = 8
 LANES = 128
 CAPACITY = 256
+UNROLL = 16
 BF16 = jnp.bfloat16
 F32 = jnp.float32
 
@@ -94,73 +95,107 @@
     )(here, codes)
 
 
-def pick_kernel(halves, parts, row_tiles, words_ref, *refs):
-    inputs, rest = refs[:halves * parts], refs[halves * parts:]
-    outs, sources, sems = rest[:halves], rest[halves:2 * halves], rest[2 * halves]
-    count = outs[0].shape[0]
-    start = pl.program_id(0) * (count // row_tiles) * LANES
-    lane = lax.broadcasted_iota(jnp.int32, (ROWS, LANES), 1)
-    low = lane < TILE
-    bit = jnp.where(low, 1 << 24, 1 << 25)
+def lane_masks():
+    low = lax.broadcasted_iota(jnp.int32, (ROWS, LANES), 1) < TILE
+    return low, jnp.where(low, 1 << 24, 1 << 25)
+
+
+def joined(word, source_ref, low, bit):
+    a = source_ref[word & 0xFFF]
+    b = source_ref[lax.shift_right_logical(word, 12) & 0xFFF]
+    swap = (jnp.broadcast_to(word, (ROWS, LANES)) & bit) != 0
+    crossed = jnp.where(low, b, a)
+    crossed = jnp.concatenate([crossed[:, TILE:], crossed[:, :TILE]], axis=1)
+    return jnp.where(swap, crossed, jnp.where(low, a, b))
+
+
+def pick_kernel(row_tiles, words_ref, *refs):
+    out_ref, source_ref, sems = refs[-3:]
+    inputs = refs[:-3]
+    start = pl.program_id(0) * (out_ref.shape[0] // row_tiles) * LANES
+    low, bit = lane_masks()
 
     @pl.when(pl.program_id(0) == 0)
     def _():
-        size = sources[0].shape[0] // parts
+        size = source_ref.shape[0] // len(inputs)
         copies = [
-            pltpu.make_async_copy(
-                inputs[h * parts + p], sources[h].at[pl.ds(p * size, size)], sems.at[h * parts + p]
-            )
-            for h in range(halves)
-            for p in range(parts)
+            pltpu.make_async_copy(part, source_ref.at[pl.ds(p * size, size)], sems.at[p])
+            for p, part in enumerate(inputs)
         ]
         for copy in copies:
             copy.start()
         for copy in copies:
             copy.wait()
 
-    for row in range(count // row_tiles):
+    for row in range(out_ref.shape[0] // row_tiles):
         def tile(k, carry):
             word = words_ref[start + row * LANES + k * MAXB]
-            swap = (jnp.broadcast_to(word, (ROWS, LANES)) & bit) != 0
-            first = word & 0xFFF
-            second = lax.shift_right_logical(word, 12) & 0xFFF
-            for source_ref, out_ref in zip(sources, outs):
-                a, b = source_ref[first], source_ref[second]
-                crossed = jnp.where(low, b, a)
-                crossed = jnp.concatenate([crossed[:, TILE:], crossed[:, :TILE]], axis=1)
-                out_ref[row * row_tiles + k] = jnp.where(swap, crossed, jnp.where(low, a, b))
+            out_ref[row * row_tiles + k] = joined(word, source_ref, low, bit)
             return carry
 
-        lax.fori_loop(0, row_tiles, tile, 0, unroll=16)
+        lax.fori_loop(0, row_tiles, tile, 0, unroll=min(UNROLL, row_tiles))
+
+
+def gather_kernel(pitch, words_ref, input_ref, *refs):
+    outs, (source_ref, sem) = refs[:-2], refs[-2:]
+    low, bit = lane_masks()
+    copy = pltpu.make_async_copy(input_ref, source_ref, sem)
+    copy.start()
+    copy.wait()
+    for d, out_ref in enumerate(outs):
+        def tile(k, carry):
+            out_ref[k] = joined(words_ref[d * pitch + k * MAXB], source_ref, low, bit)
+            return carry
+
+        lax.fori_loop(0, out_ref.shape[0], tile, 0, unroll=UNROLL)
+
+
+def gather(words, source, spaces, capacity, interpret=False):
+    shape = (capacity // MAXB, ROWS, LANES)
+    return pl.pallas_call(
+        functools.partial(gather_kernel, words.shape[0] // spaces),
+        out_shape=[jax.ShapeDtypeStruct(shape, BF16)] * spaces,
+        grid_spec=pltpu.PrefetchScalarGridSpec(
+            num_scalar_prefetch=1,
+            grid=(1,),
+            in_specs=[pl.BlockSpec(memory_space=pl.ANY)],
+            out_specs=[pl.BlockSpec(shape, lambda i, words: (0, 0, 0))] * spaces,
+            scratch_shapes=[pltpu.VMEM(source.shape, BF16), pltpu.SemaphoreType.DMA],
+        ),
+        compiler_params=pltpu.CompilerParams(vmem_limit_bytes=40 << 20),
+        name="gather",
+        interpret=interpret,
+    )(words, source)
 
 
 def in_hbm(shape, dtype, interpret):
     return jax.ShapeDtypeStruct(shape, dtype) if interpret else pltpu.HBM(shape, dtype)
 
 
-def pick(words, sources, row_tiles, interpret=False):
+def pick(words, parts, row_tiles, interpret=False):
     count = words.shape[0] // LANES * row_tiles
     step = min(128, count)
-    halves, parts = len(sources), len(sources[0])
-    size = parts * sources[0][0].shape[0]
-    return pl.pallas_call(
-        functools.partial(pick_kernel, halves, parts, row_tiles),
-        out_shape=[in_hbm((count, ROWS, LANES), BF16, interpret)] * halves,
+    size = len(parts) * parts[0].shape[0]
+    return pl.pallas_call(
+        functools.partial(pick_kernel, row_tiles),
+        out_shape=in_hbm((count, ROWS, LANES), BF16, interpret),
         grid_spec=pltpu.PrefetchScalarGridSpec(
             num_scalar_prefetch=1,
             grid=(count // step,),
-            in_specs=[pl.BlockSpec(memory_space=pl.ANY)] * (halves * parts),
-            out_specs=[pl.BlockSpec((step, ROWS, LANES), lambda i, words: (i, 0, 0))] * halves,
-            scratch_shapes=[pltpu.VMEM((size, ROWS, LANES), BF16)] * halves
-            + [pltpu.SemaphoreType.DMA((halves * parts,))],
+            in_specs=[pl.BlockSpec(memory_space=pl.ANY)] * len(parts),
+            out_specs=pl.BlockSpec((step, ROWS, LANES), lambda i, words: (i, 0, 0)),
+            scratch_shapes=[
+                pltpu.VMEM((size, ROWS, LANES), BF16),
+                pltpu.SemaphoreType.DMA((len(parts),)),
+            ],
         ),
         compiler_params=pltpu.CompilerParams(vmem_limit_bytes=40 << 20),
         name="pick",
         interpret=interpret,
-    )(words, *[part for source in sources for part in source])
-
-
-def project_kernel(group, counts_ref, first_ref, second_ref, weights_ref, basis_ref, remapped_ref, partial_ref):
+    )(words, *parts)
+
+
+def project_kernel(group, counts_ref, first_ref, second_ref, weights_ref, basis_ref, remapped_ref, rounded_ref, partial_ref):
     step = pl.program_id(0)
 
     @pl.when(step == 0)
@@ -185,6 +220,10 @@
         add = jnp.dot(block[:, c * half:(c + 1) * half].T, basis_ref[...], preferred_element_type=F32)
         partial_ref[:, c] += add.reshape(half // ROWS, ROWS, -1)
 
+    @pl.when(step == pl.num_programs(0) - 1)
+    def _():
+        rounded_ref[...] = partial_ref[...].astype(BF16)
+
 
 def project(counts, arrived, weights, basis, interpret=False):
     owners = arrived[0].shape[0]
@@ -197,7 +236,7 @@
         functools.partial(project_kernel, group),
         out_shape=(
             in_hbm((cells, snaps), BF16, interpret),
-            in_hbm((owners, 2, ROWS, rank), F32, interpret),
+            jax.ShapeDtypeStruct((owners, 2, ROWS, rank), BF16),
         ),
         grid_spec=pltpu.PrefetchScalarGridSpec(
             num_scalar_prefetch=1,
@@ -212,6 +251,7 @@
                 pl.BlockSpec((group * TILE, snaps), lambda i, counts: (i, 0)),
                 pl.BlockSpec((owners, 2, ROWS, rank), lambda i, counts: (0, 0, 0, 0)),
             ),
+            scratch_shapes=[pltpu.VMEM((owners, 2, ROWS, rank), F32)],
         ),
         compiler_params=pltpu.CompilerParams(vmem_limit_bytes=40 << 20),
         name="project",
@@ -283,7 +323,7 @@
         arrived = [exchange(c.reshape(owners, tiles, ROWS, PAIR), "tm") for c in chosen]
         remapped, partial = project(tile_counts, arrived, remap_weights, basis, interpret)
         parts = exchange(partial.reshape(owners, 2 * ROWS, rank), "tm")
-        column = spread(jnp.sum(parts, axis=0), "space")
+        column = spread(jnp.sum(parts.astype(F32), axis=0), "space")
         coeffs = jnp.sum(column, axis=0) * (1.0 / math.sqrt(total))
         half = coeffs.astype(BF16)
         rest = lax.dynamic_slice_in_dim(coeffs - half.astype(F32), here * own_ranks, own_ranks, 1)
@@ -300,22 +340,20 @@
         blocks = jnp.maximum(codes, 0)
         words = pair_words_plain(blocks).reshape(-1)
         sources = [spread(c, "space").reshape(-1, ROWS, LANES) for c in local]
-        return finish([pick(words, [[source]], tiles, interpret)[0] for source in sources])
+        return finish([pick(words, [source], tiles, interpret) for source in sources])
 
     def sparse():
-        sent = pick(asked_words, [[c] for c in local], LANES // MAXB, interpret)
         came = []
-        for c in sent:
-            c = c.reshape(spaces, -1, ROWS, LANES)
-            parts = [c[0]] + [
-                lax.ppermute(c[d], "space", [(i, (i + d) % spaces) for i in range(spaces)])
+        for source in local:
+            sent = gather(asked_words, source, spaces, capacity, interpret)
+            came.append([sent[0]] + [
+                lax.ppermute(sent[d], "space", [(j, (j + d) % spaces) for j in range(spaces)])
                 for d in range(1, spaces)
-            ]
-            came.append(parts)
+            ])
         words = local_words.reshape(-1)
         chosen = []
         for c in came:
-            chosen += pick(words, [c], tiles, interpret)
+            chosen.append(pick(words, c, tiles, interpret))
         return finish(chosen)
 
     return lax.cond(overflow, dense, sparse)

time: 317 us -> 312 us (0.984)
  blocking collectives: 68.7 us -> 57.3 us
  Pallas kernels: 47.4 us -> 54.6 us
    all_to_all x2, blocking collectives: 68.7 us -> 57.3 us  [exchange(): return lax.all_to_all(array, axis, split_axis=0, concat_axis=0, tiled=True)]
    pallas_call x3 -> x4, Pallas kernels: 27.7 us -> 34.3 us  [the longest x2 17.9 us: pick(): pl.pallas_call(functools.partial(pick_kernel, row_tiles), out_shape=in_hb...]
    slice x2 -> x0, local copies, waits for them, and re-layouts: 3.31 us -> none  [sparse(): c[d]]
  transfers between devices with their start and end apart: 19 -> 19, of which waited for: 14 -> 14; matrix products, arithmetic and copies ran while one was open for 1% -> 1% of each run, Pallas kernels for 3% -> 6%
where the time goes in v5:
time: 312 us; the launch traced here: 311 us
  waiting for transfers between devices  133 us (43%)
  blocking collectives  57.3 us (18%)
  starting transfers between devices  54.7 us (18%)
  Pallas kernels  54.6 us (18%)
  local copies, waits for them, and re-layouts  7.59 us (2%)
    ppermute x14, waiting for transfers between devices, sparse(): lax.ppermute(sent[d], 'space', [(j, (j + d) % spaces) for j in range(spac...  85.3 us
    all_to_all x2, blocking collectives, exchange(): return lax.all_to_all(array, axis, split_axis=0, concat_axis=0, tiled=True)  57.3 us
    all_to_all x5, waiting for transfers between devices, exchange(): return lax.all_to_all(array, axis, split_axis=0, concat_axis=0, tiled=True)  47.5 us
    all_to_all x5, starting transfers between devices, exchange(): return lax.all_to_all(array, axis, split_axis=0, concat_axis=0, tiled=True)  31.9 us
    ppermute x14, starting transfers between devices, sparse(): lax.ppermute(sent[d], 'space', [(j, (j + d) % spaces) for j in range(spac...  22.7 us
    pallas_call x2, Pallas kernels, pick(): pl.pallas_call(functools.partial(pick_kernel, row_tiles), out_shape=in_hb...  17.9 us
    pallas_call x2, Pallas kernels, gather(): pl.pallas_call(functools.partial(gather_kernel, words.shape[0] // spaces)...  16.4 us
    pallas_call x1, Pallas kernels, project(): pl.pallas_call(functools.partial(project_kernel, group), out_shape=(in_hb...  8.88 us
  transfers between devices with their start and end apart: 19, of which 14 were waited for; matrix products, arithmetic and copies ran while one was open for 1% of the time, Pallas kernels for 6%

profile of v5, /device:TPU:1, one launch (start us, length us, event | category | flops | bytes accessed | tf_op | source)
XLA Modules:
  0.0 311.1 jit_solution(4803552798890189066)
XLA Ops:
  0.6 0.7 compare_select_fusion
  1.5 0.6 broadcast_in_dim.37
  2.1 8.6 %all-to-all-start.12 = ((s32[32,1,128]{2,1,0:T(1,128)}), s32[32,1,128]{2,1,0:T(1,128)S(1)}, u32[]{:S(2)}, u32[]{:S(2)}) async-start(s32[32,1,128]{2,1,0:T(1,128)} %broadcast_in_dim.37), calls=%async_computation.12 | async-start | bytes 32768 | tf_op jit(solution)/shard_map/all_to_all | solution.py:293
  10.7 6.9 %all-to-all-done.12 = s32[32,1,128]{2,1,0:T(1,128)S(1)} async-done(((s32[32,1,128]{2,1,0:T(1,128)}), s32[32,1,128]{2,1,0:T(1,128)S(1)}, u32[]{:S(2)}, u32[]{:S(2)}) %all-to-all-start.12) | async-done | bytes 16416 | tf_op jit(solution)/shard_map/all_to_all | solution.py:293
  17.6 3.4 %route.1 = (s32[8,8,128]{2,1,0:T(8,128)}, s32[32,128]{1,0:T(8,128)S(1)}) custom-call(s32[1]{0:T(128)} %bitcast.23.here_ref, s32[32,128]{1,0:T(8,128)S(1)} %bitcast.52), custom_call_target="tpu_custom_call" | custom-call | tf_op jit(solution)/shard_map/route/pallas_call | solution.py:85
  21.0 8.2 %all-to-all-start.13 = ((s32[8,8,128]{2,1,0:T(8,128)}), s32[8,8,128]{2,1,0:T(8,128)S(1)}, u32[]{:S(2)}, u32[]{:S(2)}) async-start(s32[8,8,128]{2,1,0:T(8,128)} %get-tuple-element.87), calls=%async_computation.13 | async-start | bytes 65536 | tf_op jit(solution)/shard_map/all_to_all | solution.py:293
  29.2 2.7 slice_bitcast_fusion.4
  31.9 4.2 %all-to-all-done.13 = s32[8,8,128]{2,1,0:T(8,128)S(1)} async-done(((s32[8,8,128]{2,1,0:T(8,128)}), s32[8,8,128]{2,1,0:T(8,128)S(1)}, u32[]{:S(2)}, u32[]{:S(2)}) %all-to-all-start.13) | async-done | bytes 32800 | tf_op jit(solution)/shard_map/all_to_all | solution.py:293
  36.1 0.6 slice_reduce_fusion
  37.4 273.0 %conditional.1 = (bf16[2048,1024]{1,0:T(8,128)(2,1)}, f32[128,512]{1,0:T(8,128)S(1)}) conditional(s32[]{:T(128)} %convert_element_type.39, (s32[32,128]{1,0:T(8,128)S(1)}, s32[]{:T(128)}, s32[16,8,128]{2,1,0:T(8,128)S(1)}, bf16[512,8,128]{2,1,0:T(8,128)(2,1)}, bf16[512,8,128]{2,1,0:T(8,128)(2,1)S(1)}, /*index=5*/s32[32]{0:T(128)S(1)}, ...), branch_computations={%region_1.4_spmd, %region_4.7_spmd} | conditional | flops 1513478 | bytes 144257104 | solution.py:359
  37.4 7.6 %gather.3 = (bf16[128,8,128]{2,1,0:T(8,128)(2,1)S(1)}, bf16[128,8,128]{2,1,0:T(8,128)(2,1)S(1)}, bf16[128,8,128]{2,1,0:T(8,128)(2,1)S(1)}, bf16[128,8,128]{2,1,0...) custom-call(s32[2048]{0:T(1024)S(1)} %bitcast.43, ...), custom_call_target="tpu_custom_call" | custom-call | tf_op jit(solution)/shard_map/cond/branch_0_fun/gather/pallas_call | solution.py:155
  45.1 1.3 collective-permute-start.10
  46.4 3.3 %collective-permute-start.11 = (bf16[128,8,128]{2,1,0:T(8,128)(2,1)S(1)}, bf16[128,8,128]{2,1,0:T(8,128)(2,1)S(1)}, u32[]{:S(2)}, u32[]{:S(2)}) collective-permute-start(bf16[128,8,128]{2,1,0:T(8,128)(2,1)S(1)} %get-tuple-element.65), channel_id=1, source_target_pairs={{0,5},{1,6},{2,7},{3,0},{4,1},{5,2},{6,3},{7,4},{8,13},{9,14},{10,... | collective-permute-start | bytes 786440 | tf_op jit(solution)/shard_map/cond/branch_0_fun/ppermute | solution.py:350
  49.6 1.2 collective-permute-start.12
  51.1 1.1 collective-permute-start.7
  52.3 7.5 %collective-permute-done.10.refs_4_ = bf16[128,8,128]{2,1,0:T(8,128)(2,1)S(1)} collective-permute-done((bf16[128,8,128]{2,1,0:T(8,128)(2,1)S(1)}, bf16[128,8,128]{2,1,0:T(8,128)(2,1)S(1)}, u32[]{:S(2)}, u32[]{:S(2)}) %collective-permute-start.10) | collective-permute-done | bytes 262176 | tf_op jit(solution)/shard_map/cond/branch_0_fun/ppermute | solution.py:350
  59.7 16.8 %collective-permute-done.11.refs_5_ = bf16[128,8,128]{2,1,0:T(8,128)(2,1)S(1)} collective-permute-done((bf16[128,8,128]{2,1,0:T(8,128)(2,1)S(1)}, bf16[128,8,128]{2,1,0:T(8,128)(2,1)S(1)}, u32[]{:S(2)}, u32[]{:S(2)}) %collective-permute-start.11) | collective-permute-done | bytes 262176 | tf_op jit(solution)/shard_map/cond/branch_0_fun/ppermute | solution.py:350
  76.6 3.4 %collective-permute-start.9 = (bf16[128,8,128]{2,1,0:T(8,128)(2,1)S(1)}, bf16[128,8,128]{2,1,0:T(8,128)(2,1)S(1)}, u32[]{:S(2)}, u32[]{:S(2)}) collective-permute-start(bf16[128,8,128]{2,1,0:T(8,128)(2,1)S(1)} %get-tuple-element.63), channel_id=1, source_target_pairs={{0,3},{1,4},{2,5},{3,6},{4,7},{5,0},{6,1},{7,2},{8,11},{9,12},{10,... | collective-permute-start | bytes 786440 | tf_op jit(solution)/shard_map/cond/branch_0_fun/ppermute | solution.py:350
  79.9 8.4 %collective-permute-done.12.refs_6_ = bf16[128,8,128]{2,1,0:T(8,128)(2,1)S(1)} collective-permute-done((bf16[128,8,128]{2,1,0:T(8,128)(2,1)S(1)}, bf16[128,8,128]{2,1,0:T(8,128)(2,1)S(1)}, u32[]{:S(2)}, u32[]{:S(2)}) %collective-permute-start.12) | collective-permute-done | bytes 262176 | tf_op jit(solution)/shard_map/cond/branch_0_fun/ppermute | solution.py:350
  88.3 3.4 %collective-permute-done.13.refs_7_ = bf16[128,8,128]{2,1,0:T(8,128)(2,1)S(1)} collective-permute-done((bf16[128,8,128]{2,1,0:T(8,128)(2,1)S(1)}, bf16[128,8,128]{2,1,0:T(8,128)(2,1)S(1)}, u32[]{:S(2)}, u32[]{:S(2)}) %collective-permute-start.13) | collective-permute-done | bytes 262176 | tf_op jit(solution)/shard_map/cond/branch_0_fun/ppermute | solution.py:350
  91.8 6.7 %collective-permute-done.9.refs_3_ = bf16[128,8,128]{2,1,0:T(8,128)(2,1)S(1)} collective-permute-done((bf16[128,8,128]{2,1,0:T(8,128)(2,1)S(1)}, bf16[128,8,128]{2,1,0:T(8,128)(2,1)S(1)}, u32[]{:S(2)}, u32[]{:S(2)}) %collective-permute-start.9) | collective-permute-done | bytes 262176 | tf_op jit(solution)/shard_map/cond/branch_0_fun/ppermute | solution.py:350
  98.5 9.0 %pick.5 = bf16[1024,8,128]{2,1,0:T(8,128)(2,1)} custom-call(s32[4096]{0:T(1024)S(1)} %bitcast.55, bf16[128,8,128]{2,1,0:T(8,128)(2,1)S(1)} %get-tuple-element.60.refs_0_, bf16[128,8,128]{2,1,0:T(8,128)(2,1)S(1)} %collective-permute-done.7.refs_1_, bf16[128,8,128]{2,1,0:T(8,128)(2,1)S(1)} %collective-permute-done.8.refs_2_, ...), custom_call_target="tpu_custom_call" | custom-call | tf_op jit(solution)/shard_map/cond/branch_0_fun/pick/pallas_call | solution.py:179
  107.5 5.1 %all-to-all-start.1 = ((bf16[32,32,8,128]{3,2,1,0:T(8,128)(2,1)}), bf16[32,32,8,128]{3,2,1,0:T(8,128)(2,1)S(1)}, u32[]{:S(2)}, u32[]{:S(2)}) async-start(bf16[32,32,8,128]{3,2,1,0:T(8,128)(2,1)} %bitcast.47), calls=%async_computation.1 | async-start | bytes 4194304 | tf_op jit(solution)/shard_map/cond/branch_0_fun/all_to_all | solution.py:293
  112.6 8.8 %gather.2 = (bf16[128,8,128]{2,1,0:T(8,128)(2,1)S(1)}, bf16[128,8,128]{2,1,0:T(8,128)(2,1)S(1)}, bf16[128,8,128]{2,1,0:T(8,128)(2,1)S(1)}, bf16[128,8,128]{2,1,0...) custom-call(s32[2048]{0:T(1024)S(1)} %bitcast.44, ...), custom_call_target="tpu_custom_call" | custom-call | tf_op jit(solution)/shard_map/cond/branch_0_fun/gather/pallas_call | solution.py:155
  121.4 3.1 %collective-permute-start = (bf16[128,8,128]{2,1,0:T(8,128)(2,1)S(1)}, bf16[128,8,128]{2,1,0:T(8,128)(2,1)S(1)}, u32[]{:S(2)}, u32[]{:S(2)}) collective-permute-start(bf16[128,8,128]{2,1,0:T(8,128)(2,1)S(1)} %get-tuple-element.52), channel_id=1, source_target_pairs={{0,1},{1,2},{2,3},{3,4},{4,5},{5,6},{6,7},{7,0},{8,9},{9,10},{10,1... | collective-permute-start | bytes 786440 | tf_op jit(solution)/shard_map/cond/branch_0_fun/ppermute | solution.py:350
  124.5 0.4 collective-permute-start.1
  124.8 0.7 collective-permute-start.2
  125.6 4.9 %collective-permute-start.3 = (bf16[128,8,128]{2,1,0:T(8,128)(2,1)S(1)}, bf16[128,8,128]{2,1,0:T(8,128)(2,1)S(1)}, u32[]{:S(2)}, u32[]{:S(2)}) collective-permute-start(bf16[128,8,128]{2,1,0:T(8,128)(2,1)S(1)} %get-tuple-element.55), channel_id=1, source_target_pairs={{0,4},{1,5},{2,6},{3,7},{4,0},{5,1},{6,2},{7,3},{8,12},{9,13},{10,... | collective-permute-start | bytes 786440 | tf_op jit(solution)/shard_map/cond/branch_0_fun/ppermute | solution.py:350
  130.8 2.8 collective-permute-start.5
  133.5 9.1 %collective-permute-done.1.refs_2_ = bf16[128,8,128]{2,1,0:T(8,128)(2,1)S(1)} collective-permute-done((bf16[128,8,128]{2,1,0:T(8,128)(2,1)S(1)}, bf16[128,8,128]{2,1,0:T(8,128)(2,1)S(1)}, u32[]{:S(2)}, u32[]{:S(2)}) %collective-permute-start.1) | collective-permute-done | bytes 262176 | tf_op jit(solution)/shard_map/cond/branch_0_fun/ppermute | solution.py:350
  142.7 12.8 %collective-permute-done.2.refs_3_ = bf16[128,8,128]{2,1,0:T(8,128)(2,1)S(1)} collective-permute-done((bf16[128,8,128]{2,1,0:T(8,128)(2,1)S(1)}, bf16[128,8,128]{2,1,0:T(8,128)(2,1)S(1)}, u32[]{:S(2)}, u32[]{:S(2)}) %collective-permute-start.2) | collective-permute-done | bytes 262176 | tf_op jit(solution)/shard_map/cond/branch_0_fun/ppermute | solution.py:350
  155.5 15.4 %collective-permute-done.3.refs_4_ = bf16[128,8,128]{2,1,0:T(8,128)(2,1)S(1)} collective-permute-done((bf16[128,8,128]{2,1,0:T(8,128)(2,1)S(1)}, bf16[128,8,128]{2,1,0:T(8,128)(2,1)S(1)}, u32[]{:S(2)}, u32[]{:S(2)}) %collective-permute-start.3) | collective-permute-done | bytes 262176 | tf_op jit(solution)/shard_map/cond/branch_0_fun/ppermute | solution.py:350
  170.8 0.7 collective-permute-done.5.refs_6_
  171.5 4.5 %collective-permute-done.6.refs_7_ = bf16[128,8,128]{2,1,0:T(8,128)(2,1)S(1)} collective-permute-done((bf16[128,8,128]{2,1,0:T(8,128)(2,1)S(1)}, bf16[128,8,128]{2,1,0:T(8,128)(2,1)S(1)}, u32[]{:S(2)}, u32[]{:S(2)}) %collective-permute-start.6) | collective-permute-done | bytes 262176 | tf_op jit(solution)/shard_map/cond/branch_0_fun/ppermute | solution.py:350
  176.0 9.0 %pick.4 = bf16[1024,8,128]{2,1,0:T(8,128)(2,1)} custom-call(s32[4096]{0:T(1024)S(1)} %bitcast.56, bf16[128,8,128]{2,1,0:T(8,128)(2,1)S(1)} %get-tuple-element.51.refs_0_, bf16[128,8,128]{2,1,0:T(8,128)(2,1)S(1)} %collective-permute-done.refs_1_, bf16[128,8,128]{2,1,0:T(8,128)(2,1)S(1)} %collective-permute-done.1.refs_2_, ...), custom_call_target="tpu_custom_call" | custom-call | tf_op jit(solution)/shard_map/cond/branch_0_fun/pick/pallas_call | solution.py:179
  185.0 36.7 %all_to_all.58.first_ref = bf16[32,32,8,128]{3,2,1,0:T(8,128)(2,1)S(1)} all-to-all(bf16[32,32,8,128]{3,2,1,0:T(8,128)(2,1)} %bitcast.48), channel_id=1, replica_groups=mesh['tm'=32,'space'=8] {'tm'}, dimensions={0} | all-to-all | bytes 4194304 | tf_op jit(solution)/shard_map/cond/branch_0_fun/all_to_all | solution.py:293
  221.7 8.9 %project.2 = (bf16[2048,512]{1,0:T(8,128)(2,1)}, bf16[32,2,8,1024]{3,2,1,0:T(8,128)(2,1)S(1)}) custom-call(s32[32]{0:T(128)S(1)} %get-tuple-element.46.counts_ref, bf16[32,32,8,128]{3,2,1,0:T(8,128)(2,1)S(1)} %all_to_all.58.first_ref, bf16[32,32,8,128]{3,2,1,0:T(8,128)(2,1)S(1)} %all-to-all-done.1.second_ref, ...), custom_call_target="tpu_custom_call" | custom-call | tf_op jit(solution)/shard_map/cond/branch_0_fun/project/pallas_call | solution.py:235
  230.5 20.6 %all_to_all.59 = bf16[32,16,1024]{2,1,0:T(8,128)(2,1)S(1)} all-to-all(bf16[32,16,1024]{2,1,0:T(8,128)(2,1)S(1)} %bitcast.41), channel_id=1, replica_groups=mesh['tm'=32,'space'=8] {'tm'}, dimensions={0} | all-to-all | bytes 2097152 | tf_op jit(solution)/shard_map/cond/branch_0_fun/all_to_all | solution.py:293
  251.3 0.8 broadcast_in_dim.24
  252.2 5.3 %all-to-all-start.3 = ((f32[8,16,1024]{2,1,0:T(8,128)}), f32[8,16,1024]{2,1,0:T(8,128)S(1)}, u32[]{:S(2)}, u32[]{:S(2)}) async-start(f32[8,16,1024]{2,1,0:T(8,128)} %broadcast_in_dim.24), calls=%async_computation.3 | async-start | bytes 1048576 | tf_op jit(solution)/shard_map/cond/branch_0_fun/all_to_all | solution.py:293
  257.5 18.0 %all-to-all-done.3 = f32[8,16,1024]{2,1,0:T(8,128)S(1)} async-done(((f32[8,16,1024]{2,1,0:T(8,128)}), f32[8,16,1024]{2,1,0:T(8,128)S(1)}, u32[]{:S(2)}, u32[]{:S(2)}) %all-to-all-start.3) | async-done | bytes 524320 | tf_op jit(solution)/shard_map/cond/branch_0_fun/all_to_all | solution.py:293
  275.6 1.1 broadcast_in_dim.25
  276.7 4.7 %all-to-all-start.4 = ((bf16[32,16,1152]{2,1,0:T(8,128)(2,1)}), bf16[32,16,1152]{2,1,0:T(8,128)(2,1)}, u32[]{:S(2)}, u32[]{:S(2)}) async-start(bf16[32,16,1152]{2,1,0:T(8,128)(2,1)} %broadcast_in_dim.25), calls=%async_computation.4 | async-start | bytes 2359296 | tf_op jit(solution)/shard_map/cond/branch_0_fun/all_to_all | solution.py:293
  281.4 18.5 %all-to-all-done.4 = bf16[32,16,1152]{2,1,0:T(8,128)(2,1)} async-done(((bf16[32,16,1152]{2,1,0:T(8,128)(2,1)}), bf16[32,16,1152]{2,1,0:T(8,128)(2,1)}, u32[]{:S(2)}, u32[]{:S(2)}) %all-to-all-start.4) | async-done | bytes 1179680 | tf_op jit(solution)/shard_map/cond/branch_0_fun/all_to_all | solution.py:293
  299.9 1.0 convert_add_fusion
  301.0 1.3 slice_bitcast_fusion
  302.3 8.0 %rotate.2 = bf16[2048,1024]{1,0:T(8,128)(2,1)} custom-call(bf16[2048,512]{1,0:T(8,128)(2,1)S(1)} %copy-done.1, bf16[256,1024]{1,0:T(8,128)(2,1)S(1)} %get-tuple-element.101.c0_ref, bf16[256,1024]{1,0:T(8,128)(2,1)S(1)} %get-tuple-element.100.c1_ref, bf16[2048,1024]{1,0:T(8,128)(2,1)} %get-tuple-element.69.basis_ref, f32[1,1024]{1,0:T(1,128)S(1)} %bitcast.57), custom_call_target="tpu_custom_call" | custom-call | tf_op jit(solution)/shard_map/cond/branch_0_fun/rotate/pallas_call | solution.py:274
  310.4 0.7 copy-done.5
  (29 shorter events, 1.3 us)
Async XLA Ops:
  2.1 15.5 %all-to-all-start.12 = ((s32[32,1,128]{2,1,0:T(1,128)}), s32[32,1,128]{2,1,0:T(1,128)S(1)}, u32[]{:S(2)}, u32[]{:S(2)}) async-start(s32[32,1,128]{2,1,0:T(1,128)} %broadcast_in_dim.37), calls=%async_computation.12 | async-start | bytes 32768 | tf_op jit(solution)/shard_map/all_to_all | solution.py:293
  21.0 15.1 %all-to-all-start.13 = ((s32[8,8,128]{2,1,0:T(8,128)}), s32[8,8,128]{2,1,0:T(8,128)S(1)}, u32[]{:S(2)}, u32[]{:S(2)}) async-start(s32[8,8,128]{2,1,0:T(8,128)} %get-tuple-element.87), calls=%async_computation.13 | async-start | bytes 65536 | tf_op jit(solution)/shard_map/all_to_all | solution.py:293
  29.2 8.2 %copy-start.6 = (f32[1024]{0:T(1024)S(1)}, f32[1024]{0:T(1024)}, u32[]{:S(2)}) copy-start(f32[1024]{0:T(1024)} %param.13) | copy-start | bytes 12292
  29.2 8.2 %copy-start.7 = (s32[32]{0:T(128)S(1)}, s32[32]{0:T(128)}, u32[]{:S(2)}) copy-start(s32[32]{0:T(128)} %param.10) | copy-start | bytes 388
  45.1 14.7 %collective-permute-start.10 = (bf16[128,8,128]{2,1,0:T(8,128)(2,1)S(1)}, bf16[128,8,128]{2,1,0:T(8,128)(2,1)S(1)}, u32[]{:S(2)}, u32[]{:S(2)}) collective-permute-start(bf16[128,8,128]{2,1,0:T(8,128)(2,1)S(1)} %get-tuple-element.64), channel_id=1, source_target_pairs={{0,4},{1,5},{2,6},{3,7},{4,0},{5,1},{6,2},{7,3},{8,12},{9,13},{10,... | collective-permute-start | bytes 786440 | tf_op jit(solution)/shard_map/cond/branch_0_fun/ppermute | solution.py:350
  46.4 30.2 %collective-permute-start.11 = (bf16[128,8,128]{2,1,0:T(8,128)(2,1)S(1)}, bf16[128,8,128]{2,1,0:T(8,128)(2,1)S(1)}, u32[]{:S(2)}, u32[]{:S(2)}) collective-permute-start(bf16[128,8,128]{2,1,0:T(8,128)(2,1)S(1)} %get-tuple-element.65), channel_id=1, source_target_pairs={{0,5},{1,6},{2,7},{3,0},{4,1},{5,2},{6,3},{7,4},{8,13},{9,14},{10,... | collective-permute-start | bytes 786440 | tf_op jit(solution)/shard_map/cond/branch_0_fun/ppermute | solution.py:350
  49.6 38.7 %collective-permute-start.12 = (bf16[128,8,128]{2,1,0:T(8,128)(2,1)S(1)}, bf16[128,8,128]{2,1,0:T(8,128)(2,1)S(1)}, u32[]{:S(2)}, u32[]{:S(2)}) collective-permute-start(bf16[128,8,128]{2,1,0:T(8,128)(2,1)S(1)} %get-tuple-element.66), channel_id=1, source_target_pairs={{0,6},{1,7},{2,0},{3,1},{4,2},{5,3},{6,4},{7,5},{8,14},{9,15},{10,... | collective-permute-start | bytes 786440 | tf_op jit(solution)/shard_map/cond/branch_0_fun/ppermute | solution.py:350
  50.8 41.0 %collective-permute-start.13 = (bf16[128,8,128]{2,1,0:T(8,128)(2,1)S(1)}, bf16[128,8,128]{2,1,0:T(8,128)(2,1)S(1)}, u32[]{:S(2)}, u32[]{:S(2)}) collective-permute-start(bf16[128,8,128]{2,1,0:T(8,128)(2,1)S(1)} %get-tuple-element.67), channel_id=1, source_target_pairs={{0,7},{1,0},{2,1},{3,2},{4,3},{5,4},{6,5},{7,6},{8,15},{9,8},{10,9... | collective-permute-start | bytes 786440 | tf_op jit(solution)/shard_map/cond/branch_0_fun/ppermute | solution.py:350
  51.1 40.6 %collective-permute-start.7 = (bf16[128,8,128]{2,1,0:T(8,128)(2,1)S(1)}, bf16[128,8,128]{2,1,0:T(8,128)(2,1)S(1)}, u32[]{:S(2)}, u32[]{:S(2)}) collective-permute-start(bf16[128,8,128]{2,1,0:T(8,128)(2,1)S(1)} %get-tuple-element.61), channel_id=1, source_target_pairs={{0,1},{1,2},{2,3},{3,4},{4,5},{5,6},{6,7},{7,0},{8,9},{9,10},{10,1... | collective-permute-start | bytes 786440 | tf_op jit(solution)/shard_map/cond/branch_0_fun/ppermute | solution.py:350
  59.7 32.0 %collective-permute-start.8 = (bf16[128,8,128]{2,1,0:T(8,128)(2,1)S(1)}, bf16[128,8,128]{2,1,0:T(8,128)(2,1)S(1)}, u32[]{:S(2)}, u32[]{:S(2)}) collective-permute-start(bf16[128,8,128]{2,1,0:T(8,128)(2,1)S(1)} %get-tuple-element.62), channel_id=1, source_target_pairs={{0,2},{1,3},{2,4},{3,5},{4,6},{5,7},{6,0},{7,1},{8,10},{9,11},{10,... | collective-permute-start | bytes 786440 | tf_op jit(solution)/shard_map/cond/branch_0_fun/ppermute | solution.py:350
  76.6 22.0 %collective-permute-start.9 = (bf16[128,8,128]{2,1,0:T(8,128)(2,1)S(1)}, bf16[128,8,128]{2,1,0:T(8,128)(2,1)S(1)}, u32[]{:S(2)}, u32[]{:S(2)}) collective-permute-start(bf16[128,8,128]{2,1,0:T(8,128)(2,1)S(1)} %get-tuple-element.63), channel_id=1, source_target_pairs={{0,3},{1,4},{2,5},{3,6},{4,7},{5,0},{6,1},{7,2},{8,11},{9,12},{10,... | collective-permute-start | bytes 786440 | tf_op jit(solution)/shard_map/cond/branch_0_fun/ppermute | solution.py:350
  107.5 77.5 %all-to-all-start.1 = ((bf16[32,32,8,128]{3,2,1,0:T(8,128)(2,1)}), bf16[32,32,8,128]{3,2,1,0:T(8,128)(2,1)S(1)}, u32[]{:S(2)}, u32[]{:S(2)}) async-start(bf16[32,32,8,128]{3,2,1,0:T(8,128)(2,1)} %bitcast.47), calls=%async_computation.1 | async-start | bytes 4194304 | tf_op jit(solution)/shard_map/cond/branch_0_fun/all_to_all | solution.py:293
  121.4 9.4 %collective-permute-start = (bf16[128,8,128]{2,1,0:T(8,128)(2,1)S(1)}, bf16[128,8,128]{2,1,0:T(8,128)(2,1)S(1)}, u32[]{:S(2)}, u32[]{:S(2)}) collective-permute-start(bf16[128,8,128]{2,1,0:T(8,128)(2,1)S(1)} %get-tuple-element.52), channel_id=1, source_target_pairs={{0,1},{1,2},{2,3},{3,4},{4,5},{5,6},{6,7},{7,0},{8,9},{9,10},{10,1... | collective-permute-start | bytes 786440 | tf_op jit(solution)/shard_map/cond/branch_0_fun/ppermute | solution.py:350
  124.5 18.2 %collective-permute-start.1 = (bf16[128,8,128]{2,1,0:T(8,128)(2,1)S(1)}, bf16[128,8,128]{2,1,0:T(8,128)(2,1)S(1)}, u32[]{:S(2)}, u32[]{:S(2)}) collective-permute-start(bf16[128,8,128]{2,1,0:T(8,128)(2,1)S(1)} %get-tuple-element.53), channel_id=1, source_target_pairs={{0,2},{1,3},{2,4},{3,5},{4,6},{5,7},{6,0},{7,1},{8,10},{9,11},{10,... | collective-permute-start | bytes 786440 | tf_op jit(solution)/shard_map/cond/branch_0_fun/ppermute | solution.py:350
  124.8 30.6 %collective-permute-start.2 = (bf16[128,8,128]{2,1,0:T(8,128)(2,1)S(1)}, bf16[128,8,128]{2,1,0:T(8,128)(2,1)S(1)}, u32[]{:S(2)}, u32[]{:S(2)}) collective-permute-start(bf16[128,8,128]{2,1,0:T(8,128)(2,1)S(1)} %get-tuple-element.54), channel_id=1, source_target_pairs={{0,3},{1,4},{2,5},{3,6},{4,7},{5,0},{6,1},{7,2},{8,11},{9,12},{10,... | collective-permute-start | bytes 786440 | tf_op jit(solution)/shard_map/cond/branch_0_fun/ppermute | solution.py:350
  125.6 45.3 %collective-permute-start.3 = (bf16[128,8,128]{2,1,0:T(8,128)(2,1)S(1)}, bf16[128,8,128]{2,1,0:T(8,128)(2,1)S(1)}, u32[]{:S(2)}, u32[]{:S(2)}) collective-permute-start(bf16[128,8,128]{2,1,0:T(8,128)(2,1)S(1)} %get-tuple-element.55), channel_id=1, source_target_pairs={{0,4},{1,5},{2,6},{3,7},{4,0},{5,1},{6,2},{7,3},{8,12},{9,13},{10,... | collective-permute-start | bytes 786440 | tf_op jit(solution)/shard_map/cond/branch_0_fun/ppermute | solution.py:350
  130.4 40.4 %collective-permute-start.4 = (bf16[128,8,128]{2,1,0:T(8,128)(2,1)S(1)}, bf16[128,8,128]{2,1,0:T(8,128)(2,1)S(1)}, u32[]{:S(2)}, u32[]{:S(2)}) collective-permute-start(bf16[128,8,128]{2,1,0:T(8,128)(2,1)S(1)} %get-tuple-element.56), channel_id=1, source_target_pairs={{0,5},{1,6},{2,7},{3,0},{4,1},{5,2},{6,3},{7,4},{8,13},{9,14},{10,... | collective-permute-start | bytes 786440 | tf_op jit(solution)/shard_map/cond/branch_0_fun/ppermute | solution.py:350
  130.8 40.7 %collective-permute-start.5 = (bf16[128,8,128]{2,1,0:T(8,128)(2,1)S(1)}, bf16[128,8,128]{2,1,0:T(8,128)(2,1)S(1)}, u32[]{:S(2)}, u32[]{:S(2)}) collective-permute-start(bf16[128,8,128]{2,1,0:T(8,128)(2,1)S(1)} %get-tuple-element.57), channel_id=1, source_target_pairs={{0,6},{1,7},{2,0},{3,1},{4,2},{5,3},{6,4},{7,5},{8,14},{9,15},{10,... | collective-permute-start | bytes 786440 | tf_op jit(solution)/shard_map/cond/branch_0_fun/ppermute | solution.py:350
  142.7 33.3 %collective-permute-start.6 = (bf16[128,8,128]{2,1,0:T(8,128)(2,1)S(1)}, bf16[128,8,128]{2,1,0:T(8,128)(2,1)S(1)}, u32[]{:S(2)}, u32[]{:S(2)}) collective-permute-start(bf16[128,8,128]{2,1,0:T(8,128)(2,1)S(1)} %get-tuple-element.58), channel_id=1, source_target_pairs={{0,7},{1,0},{2,1},{3,2},{4,3},{5,4},{6,5},{7,6},{8,15},{9,8},{10,9... | collective-permute-start | bytes 786440 | tf_op jit(solution)/shard_map/cond/branch_0_fun/ppermute | solution.py:350
  185.0 36.7 %copy-start.3 = (bf16[2048,1024]{1,0:T(8,128)(2,1)S(1)}, bf16[2048,1024]{1,0:T(8,128)(2,1)}, u32[]{:S(2)}) copy-start(bf16[2048,1024]{1,0:T(8,128)(2,1)} %get-tuple-element.69.basis_ref) | copy-start | bytes 12582916 | tf_op jit(solution)/shard_map/cond
  252.2 23.3 %all-to-all-start.3 = ((f32[8,16,1024]{2,1,0:T(8,128)}), f32[8,16,1024]{2,1,0:T(8,128)S(1)}, u32[]{:S(2)}, u32[]{:S(2)}) async-start(f32[8,16,1024]{2,1,0:T(8,128)} %broadcast_in_dim.24), calls=%async_computation.3 | async-start | bytes 1048576 | tf_op jit(solution)/shard_map/cond/branch_0_fun/all_to_all | solution.py:293
  276.7 23.2 %all-to-all-start.4 = ((bf16[32,16,1152]{2,1,0:T(8,128)(2,1)}), bf16[32,16,1152]{2,1,0:T(8,128)(2,1)}, u32[]{:S(2)}, u32[]{:S(2)}) async-start(bf16[32,16,1152]{2,1,0:T(8,128)(2,1)} %broadcast_in_dim.25), calls=%async_computation.4 | async-start | bytes 2359296 | tf_op jit(solution)/shard_map/cond/branch_0_fun/all_to_all | solution.py:293
  281.4 20.9 %copy-start.1 = (bf16[2048,512]{1,0:T(8,128)(2,1)S(1)}, bf16[2048,512]{1,0:T(8,128)(2,1)}, u32[]{:S(2)}) copy-start(bf16[2048,512]{1,0:T(8,128)(2,1)} %get-tuple-element.71.remapped_ref) | copy-start | bytes 6291460 | tf_op jit(solution)/shard_map/cond
  310.4 0.7 copy-start.5

commit v6 on v5

v6 whole, which is shorter than its diff:
```python
import functools
import math

import jax
import jax.numpy as jnp
from jax import lax
from jax.experimental import pallas as pl
from jax.experimental.pallas import tpu as pltpu
from jax.sharding import PartitionSpec as P


TILE = 64
MAXB = 2
PAIR = MAXB * TILE
ROWS = 8
LANES = 128
LIMITS = (112, 200, 256)
SHARES = (12, 24, 32)
BF16 = jnp.bfloat16
F32 = jnp.float32


def pair_words(index):
    after = pltpu.roll(index, LANES - 1, 1)
    return (
        lax.shift_right_logical(index, 1)
        | (lax.shift_right_logical(after, 1) << 12)
        | ((index & 1) << 24)
        | ((1 - (after & 1)) << 25)
    )


def staged(values, edges, at):
    result = values[-1]
    for value, edge in reversed(list(zip(values[:-1], edges[:-1]))):
        result = jnp.where(at < edge, value, result)
    return result


def route_kernel(limits, edges, per_space, here_ref, codes_ref, request_ref, local_ref):
    owners = codes_ref.shape[0]
    spaces = request_ref.shape[0]
    pitch = -(-limits[-1] // LANES) * LANES
    here = here_ref[0]
    codes = codes_ref[...]
    owner_of = jnp.where(codes < 0, -1, lax.div(jnp.maximum(codes, 0), per_space))
    within = jnp.where(codes < 0, 0, lax.rem(jnp.maximum(codes, 0), per_space))
    from_lane = lax.broadcasted_iota(jnp.int32, (LANES, LANES), 0)
    to_lane = lax.broadcasted_iota(jnp.int32, (LANES, LANES), 1)
    numbers = list(range(len(edges)))
    same = staged(numbers, edges, from_lane) == staged(numbers, edges, to_lane)
    upper = jnp.where(same, jnp.where(from_lane <= to_lane, 1.0, 0.0), 0.0).astype(BF16)
    same = jnp.where(same, 1.0, 0.0).astype(BF16)
    lower = lax.broadcasted_iota(jnp.int32, (owners, owners), 0) > lax.broadcasted_iota(jnp.int32, (owners, owners), 1)
    lower = jnp.where(lower, 1.0, 0.0).astype(BF16)
    row_lane = lax.broadcasted_iota(jnp.int32, (1, LANES), 1)
    location = jnp.zeros_like(codes)
    target = jnp.full_like(codes, -1)
    overflow = jnp.zeros((1, LANES), F32)
    for s in range(spaces):
        match = owner_of == s
        ones = jnp.where(match, 1.0, 0.0).astype(BF16)
        prefix = jnp.dot(ones, upper, preferred_element_type=F32)
        sums = jnp.dot(ones, same, preferred_element_type=F32)
        ahead = jnp.dot(lower, sums.astype(BF16), preferred_element_type=F32)
        totals = ahead[owners - 1:] + sums[owners - 1:]
        bases, running = [], jnp.zeros((1, LANES), F32)
        for edge, first, limit in zip(edges, (0,) + edges[:-1], limits):
            bases.append(running)
            running = running + jnp.broadcast_to(totals[:, first:first + 1], (1, LANES))
            overflow = jnp.maximum(overflow, jnp.where(running > limit, 1.0, 0.0))
        base = staged(bases, edges, row_lane)
        rank = (prefix + ahead + base).astype(jnp.int32) - 1
        d = lax.rem(here - s + spaces, spaces)
        places, begin = [], 0
        for limit in limits:
            places.append(spaces * begin + d * (limit - begin) + rank - begin)
            begin = limit
        location = jnp.where(match, staged(places, limits, rank), location)
        target = jnp.where(match, rank + s * pitch, target)
    local_ref[...] = pair_words(location)

    rows = spaces * pitch // LANES
    row_id = lax.broadcasted_iota(jnp.int32, (rows, LANES), 0)
    lane_of = (target & (LANES - 1)).astype(F32)
    lane_of = jnp.concatenate([lane_of, jnp.zeros((LANES - owners, LANES), F32)], axis=0).T
    high = jnp.zeros((rows, LANES), F32)
    low = jnp.zeros((rows, LANES), F32)
    for r in range(owners):
        hit = jnp.broadcast_to(target[r:r + 1] >> 7, (rows, LANES)) == row_id
        value = jnp.broadcast_to(within[r:r + 1], (rows, LANES))
        upper_part = jnp.where(hit, lax.shift_right_logical(value, 6), 0).astype(F32).astype(BF16)
        lower_part = jnp.where(hit, value & 63, 0).astype(F32).astype(BF16)
        column = jnp.broadcast_to(lane_of[:, r:r + 1], (LANES, LANES)).astype(jnp.int32)
        onehot = jnp.where(column == to_lane, 1.0, 0.0).astype(BF16)
        high += jnp.dot(upper_part, onehot, preferred_element_type=F32)
        low += jnp.dot(lower_part, onehot, preferred_element_type=F32)
    wanted = high.astype(jnp.int32) * 64 + low.astype(jnp.int32)
    words = pair_words(wanted)
    each = pitch // LANES
    for s in range(spaces):
        request_ref[s, 0:each, :] = words[s * each:(s + 1) * each]
        request_ref[s, each:, :] = jnp.broadcast_to(overflow.astype(jnp.int32), (ROWS - each, LANES))


def route(here, codes, spaces, per_space, limits, edges, interpret=False):
    return pl.pallas_call(
        functools.partial(route_kernel, limits, edges, per_space),
        out_shape=(
            jax.ShapeDtypeStruct((spaces, ROWS, LANES), jnp.int32),
            jax.ShapeDtypeStruct(codes.shape, jnp.int32),
        ),
        in_specs=[pl.BlockSpec(memory_space=pltpu.SMEM), pl.BlockSpec(memory_space=pltpu.VMEM)],
        out_specs=(pl.BlockSpec(memory_space=pltpu.VMEM), pl.BlockSpec(memory_space=pltpu.VMEM)),
        name="route",
        interpret=interpret,
    )(here, codes)


def lane_masks():
    low = lax.broadcasted_iota(jnp.int32, (ROWS, LANES), 1) < TILE
    return low, jnp.where(low, 1 << 24, 1 << 25)


def joined(a, b, word, low, bit):
    swap = (jnp.broadcast_to(word, (ROWS, LANES)) & bit) != 0
    crossed = jnp.where(low, b, a)
    crossed = jnp.concatenate([crossed[:, TILE:], crossed[:, :TILE]], axis=1)
    return jnp.where(swap, crossed, jnp.where(low, a, b))


def both(word):
    return word & 0xFFF, lax.shift_right_logical(word, 12) & 0xFFF


def pick_kernel(first_tile, words_ref, *refs):
    out_ref, source_ref, sems = refs[-3:]
    inputs = refs[:-3]
    step_owners, tiles = out_ref.shape[:2]
    start = pl.program_id(0) * step_owners * LANES
    low, bit = lane_masks()

    @pl.when(pl.program_id(0) == 0)
    def _():
        copies, begin = [], 0
        for p, part in enumerate(inputs):
            size = part.shape[0]
            copies.append(pltpu.make_async_copy(part, source_ref.at[pl.ds(begin, size)], sems.at[p]))
            begin += size
        for copy in copies:
            copy.start()
        for copy in copies:
            copy.wait()

    def owner(row, carry):
        def tile(k, carry):
            word = words_ref[start + row * LANES + (first_tile + k) * MAXB]
            first, second = both(word)
            for h in range(2):
                out_ref[row, k, h] = joined(source_ref[first, h], source_ref[second, h], word, low, bit)
            return carry

        return lax.fori_loop(0, tiles, tile, carry, unroll=tiles if tiles <= 16 else 4)

    lax.fori_loop(0, step_owners, owner, 0)


def gather_kernel(pitch, spans, words_ref, input_ref, *refs):
    outs, (source_ref, sem) = refs[:-2], refs[-2:]
    spaces = len(outs) // len(spans)
    low, bit = lane_masks()
    copy = pltpu.make_async_copy(input_ref, source_ref, sem)
    copy.start()
    copy.wait()
    for n, out_ref in enumerate(outs):
        begin = (n % spaces) * pitch + spans[n // spaces][0]

        def tile(k, carry):
            word = words_ref[begin + k * MAXB]
            first, second = both(word)
            for h in range(2):
                out_ref[k, h] = joined(source_ref[h, first], source_ref[h, second], word, low, bit)
            return carry

        lax.fori_loop(0, out_ref.shape[0], tile, 0, unroll=4)


def gather(words, source, spaces, spans, interpret=False):
    shapes = [((end - begin) // MAXB, 2, ROWS, LANES) for begin, end in spans for _ in range(spaces)]
    outs = pl.pallas_call(
        functools.partial(gather_kernel, words.shape[0] // spaces, spans),
        out_shape=[jax.ShapeDtypeStruct(shape, BF16) for shape in shapes],
        grid_spec=pltpu.PrefetchScalarGridSpec(
            num_scalar_prefetch=1,
            grid=(1,),
            in_specs=[pl.BlockSpec(memory_space=pl.ANY)],
            out_specs=[pl.BlockSpec(shape, lambda i, words: (0, 0, 0, 0)) for shape in shapes],
            scratch_shapes=[pltpu.VMEM(source.shape, BF16), pltpu.SemaphoreType.DMA],
        ),
        compiler_params=pltpu.CompilerParams(vmem_limit_bytes=40 << 20),
        name="gather",
        interpret=interpret,
    )(words, source)
    return [outs[n * spaces:(n + 1) * spaces] for n in range(len(spans))]


def in_hbm(shape, dtype, interpret):
    return jax.ShapeDtypeStruct(shape, dtype) if interpret else pltpu.HBM(shape, dtype)


def pick(words, parts, owners, first_tile, tiles, interpret=False):
    step = min(4, owners)
    size = sum(part.shape[0] for part in parts)
    return pl.pallas_call(
        functools.partial(pick_kernel, first_tile),
        out_shape=in_hbm((owners, tiles, 2, ROWS, LANES), BF16, interpret),
        grid_spec=pltpu.PrefetchScalarGridSpec(
            num_scalar_prefetch=1,
            grid=(owners // step,),
            in_specs=[pl.BlockSpec(memory_space=pl.ANY)] * len(parts),
            out_specs=pl.BlockSpec((step, tiles, 2, ROWS, LANES), lambda i, words: (i, 0, 0, 0, 0)),
            scratch_shapes=[
                pltpu.VMEM((size, 2, ROWS, LANES), BF16),
                pltpu.SemaphoreType.DMA((len(parts),)),
            ],
        ),
        compiler_params=pltpu.CompilerParams(vmem_limit_bytes=48 << 20),
        name="pick",
        interpret=interpret,
    )(words, *parts)


def project_kernel(group, starts, counts_ref, *refs):
    arrived, (weights_ref, basis_ref, remapped_ref, rounded_ref, partial_ref) = refs[:-5], refs[-5:]
    step = pl.program_id(0)

    @pl.when(step == 0)
    def _():
        partial_ref[...] = jnp.zeros_like(partial_ref)

    def remap(picked_ref):
        low = lax.broadcasted_iota(jnp.int32, (TILE, PAIR), 1) < TILE
        pieces = []
        for k in range(group):
            full = counts_ref[step * group + k] > 1
            weights = jnp.where(jnp.logical_or(low, full), weights_ref[k].astype(F32), 0.0).astype(BF16)
            picked = picked_ref[:, k].reshape(-1, PAIR)
            pieces.append(
                lax.dot_general(weights, picked, (((1,), (1,)), ((), ())), preferred_element_type=F32)
            )
        remapped_ref[...] = jnp.concatenate(pieces, axis=0).astype(BF16)

    for picked_ref, begin, end in zip(arrived, starts, starts[1:] + (None,)):
        here = step >= begin if end is None else jnp.logical_and(step >= begin, step < end)
        pl.when(here)(functools.partial(remap, picked_ref))

    add = jnp.dot(remapped_ref[...].T, basis_ref[...], preferred_element_type=F32)
    partial_ref[...] += add.reshape(partial_ref.shape)

    @pl.when(step == pl.num_programs(0) - 1)
    def _():
        rounded_ref[...] = partial_ref[...].astype(BF16)


def project(counts, arrived, weights, basis, interpret=False):
    owners = arrived[0].shape[0]
    snaps = owners * 2 * ROWS
    tiles = weights.shape[0]
    cells, rank = basis.shape
    group = 4
    starts, begin = [], 0
    for part in arrived:
        starts.append(begin)
        begin += part.shape[1] // group

    def chunk(start, part):
        last = part.shape[1] // group - 1
        return pl.BlockSpec(
            (owners, group, 2, ROWS, PAIR),
            lambda i, counts: (0, jnp.clip(i - start, 0, last), 0, 0, 0),
        )

    return pl.pallas_call(
        functools.partial(project_kernel, group, tuple(starts)),
        out_shape=(
            in_hbm((cells, snaps), BF16, interpret),
            jax.ShapeDtypeStruct((owners, 2 * ROWS, rank), BF16),
        ),
        grid_spec=pltpu.PrefetchScalarGridSpec(
            num_scalar_prefetch=1,
            grid=(tiles // group,),
            in_specs=[chunk(start, part) for start, part in zip(starts, arrived)] + [
                pl.BlockSpec((group, TILE, PAIR), lambda i, counts: (i, 0, 0)),
                pl.BlockSpec((group * TILE, rank), lambda i, counts: (i, 0)),
            ],
            out_specs=(
                pl.BlockSpec((group * TILE, snaps), lambda i, counts: (i, 0)),
                pl.BlockSpec((owners, 2 * ROWS, rank), lambda i, counts: (0, 0, 0)),
            ),
            scratch_shapes=[pltpu.VMEM((owners, 2 * ROWS, rank), F32)],
        ),
        compiler_params=pltpu.CompilerParams(vmem_limit_bytes=40 << 20),
        name="project",
        interpret=interpret,
    )(counts, *arrived, weights, basis)


def rotate_kernel(scale, remapped_ref, coeffs_ref, basis_ref, variances_ref, out_ref):
    update = jnp.dot(remapped_ref[...], coeffs_ref[...], preferred_element_type=F32)
    out_ref[...] = (basis_ref[...].astype(F32) * variances_ref[...] + update * scale).astype(BF16)


def rotate(remapped, coeffs, basis, variances, interpret=False):
    cells, rank = basis.shape
    snaps = remapped.shape[1]
    rows = min(256, cells)
    resident = lambda i: (0, 0)
    return pl.pallas_call(
        functools.partial(rotate_kernel, 1.0 / math.sqrt(snaps)),
        out_shape=in_hbm((cells, rank), BF16, interpret),
        grid=(cells // rows,),
        in_specs=[
            pl.BlockSpec((rows, snaps), lambda i: (i, 0)),
            pl.BlockSpec((snaps, rank), resident),
            pl.BlockSpec((rows, rank), lambda i: (i, 0)),
            pl.BlockSpec((1, rank), resident),
        ],
        out_specs=pl.BlockSpec((rows, rank), lambda i: (i, 0)),
        compiler_params=pltpu.CompilerParams(vmem_limit_bytes=40 << 20),
        name="rotate",
        interpret=interpret,
    )(remapped, coeffs, basis, variances[None, :])


def exchange(array, axis):
    return lax.all_to_all(array, axis, split_axis=0, concat_axis=0, tiled=True)


def spread(array, axis):
    return exchange(jnp.broadcast_to(array, (lax.axis_size(axis),) + array.shape), axis)


def per_device(interpret, limits, shares, snapshots, block_lists, tile_counts, remap_weights, basis, variances):
    tiles = block_lists.shape[0]
    owners, spaces = lax.axis_size("tm"), lax.axis_size("space")
    cells, rank = basis.shape
    total = cells * owners * spaces
    own_ranks = rank // spaces
    here = lax.axis_index("space")
    per_space = snapshots.shape[1] // TILE

    used = lax.broadcasted_iota(jnp.int32, block_lists.shape, 1) < tile_counts[:, None]
    codes = jnp.where(used, block_lists, -1).reshape(1, tiles * MAXB)
    codes = jnp.pad(codes, ((0, 0), (0, LANES - tiles * MAXB)), constant_values=-1)
    codes = spread(codes, "tm").reshape(owners, LANES)
    edges = tuple(share * MAXB for share in shares)
    requests, local_words = route(here[None], codes, spaces, per_space, limits, edges, interpret)
    asked = exchange(requests, "space")
    each = -(-limits[-1] // LANES)
    around = lax.dynamic_slice_in_dim(jnp.concatenate([asked, asked], axis=0), here, spaces, 0)
    asked_words = around[:, :each].reshape(-1)
    overflow = jnp.max(asked[:, each]) > 0
    chunks = [(begin, end - begin) for begin, end in zip((0,) + shares, shares)]

    def finish(arrived):
        remapped, partial = project(tile_counts, arrived, remap_weights, basis, interpret)
        parts = exchange(partial, "tm")
        column = spread(jnp.sum(parts.astype(F32), axis=0), "space")
        coeffs = jnp.sum(column, axis=0) * (1.0 / math.sqrt(total))
        half = coeffs.astype(BF16)
        rest = lax.dynamic_slice_in_dim(coeffs - half.astype(F32), here * own_ranks, own_ranks, 1)
        everyone = spread(jnp.concatenate([half, rest.astype(BF16)], axis=1), "tm")
        high = lax.dynamic_slice_in_dim(everyone, here * own_ranks, own_ranks, 2)
        own = high.astype(F32) + everyone[:, :, rank:].astype(F32)
        own_coeffs = own.reshape(owners * 2 * ROWS, own_ranks).T
        whole = everyone[:, :, :rank].reshape(owners * 2 * ROWS, rank)
        return own_coeffs, rotate(remapped, whole, basis, variances, interpret)

    def dense():
        words = pair_words_plain(jnp.maximum(codes, 0)).reshape(-1)
        local = snapshots.reshape(2, ROWS, -1, LANES).transpose(2, 0, 1, 3)
        source = spread(local, "space").reshape(-1, 2, ROWS, LANES)
        arrived = exchange(pick(words, [source], owners, 0, tiles, interpret), "tm")
        return finish([arrived[:, begin:begin + count] for begin, count in chunks])

    def sparse():
        local = snapshots.reshape(2, ROWS, -1, LANES).transpose(0, 2, 1, 3)
        spans = list(zip((0,) + limits, limits))
        sent = gather(asked_words, local, spaces, spans[:1], interpret)
        sent += gather(asked_words, local, spaces, spans[1:], interpret)
        words = local_words.reshape(-1)
        came, arrived = [], []
        for i, parts in enumerate(sent):
            came.append(parts[0])
            for d in range(1, spaces):
                ring = [(j, (j + d) % spaces) for j in range(spaces)]
                came.append(lax.ppermute(parts[d], "space", ring))
            chosen = pick(words, list(came), owners, *chunks[i], interpret)
            arrived.append(exchange(chosen, "tm"))
        return finish(arrived)

    return lax.cond(overflow, dense, sparse)


def pair_words_plain(index):
    after = jnp.roll(index, -1, axis=1)
    return (index >> 1) | ((after >> 1) << 12) | ((index & 1) << 24) | ((1 - (after & 1)) << 25)


def solution(mesh, interpret=False, limits=LIMITS, shares=SHARES):
    return jax.shard_map(
        functools.partial(per_device, interpret, limits, shares),
        mesh=mesh,
        in_specs=(
            P("tm", "space"),
            P(("tm", "space"), None),
            P(("tm", "space")),
            P(("tm", "space"), None, None),
            P(("tm", "space"), None),
            P(),
        ),
        out_specs=(P("space", None), P(("tm", "space"), None)),
        check_vma=False,
    )
```

time: 312 us -> 365 us (1.17)
  starting transfers between devices: 54.7 us -> 85.1 us
  Pallas kernels: 54.6 us -> 75 us
  blocking collectives: 57.3 us -> 47.4 us
  local copies, waits for them, and re-layouts: 7.59 us -> 15.5 us
  waiting for transfers between devices: 133 us -> 138 us
    ppermute x14 -> x21, starting transfers between devices: 22.7 us -> 44.6 us  [sparse(): came.append(lax.ppermute(parts[d], 'space', ring))]
    pallas_call x6 -> x7, Pallas kernels: 46.6 us -> 67 us  [the longest x3 30.5 us: pick(): pl.pallas_call(functools.partial(pick_kernel, first_tile), out_shape=in_h...]
    all_to_all x5 -> x6, waiting for transfers between devices: 47.5 us -> 62.3 us  [exchange(): return lax.all_to_all(array, axis, split_axis=0, concat_axis=0, tiled=True)]
    cond x4 -> x50, local copies, waits for them, and re-layouts: 0.01 us -> 11.7 us
    ppermute x14 -> x21, waiting for transfers between devices: 85.3 us -> 75.3 us  [sparse(): came.append(lax.ppermute(parts[d], 'space', ring))]
    all_to_all x2, blocking collectives: 57.3 us -> 47.4 us  [exchange(): return lax.all_to_all(array, axis, split_axis=0, concat_axis=0, tiled=True)]
    all_to_all x5 -> x6, starting transfers between devices: 31.9 us -> 40.5 us  [exchange(): return lax.all_to_all(array, axis, split_axis=0, concat_axis=0, tiled=True)]
  transfers between devices with their start and end apart: 19 -> 27, of which waited for: 14 -> 16; matrix products, arithmetic and copies ran while one was open for 1% -> 0% of each run, Pallas kernels for 6% -> 8%
where the time goes in v6:
time: 365 us; the launch traced here: 364 us
  waiting for transfers between devices  138 us (38%)
  starting transfers between devices  85.1 us (23%)
  Pallas kernels  75 us (21%)
  blocking collectives  47.4 us (13%)
  local copies, waits for them, and re-layouts  15.5 us (4%)
    ppermute x21, waiting for transfers between devices, sparse(): came.append(lax.ppermute(parts[d], 'space', ring))  75.3 us
    all_to_all x6, waiting for transfers between devices, exchange(): return lax.all_to_all(array, axis, split_axis=0, concat_axis=0, tiled=True)  62.3 us
    all_to_all x2, blocking collectives, exchange(): return lax.all_to_all(array, axis, split_axis=0, concat_axis=0, tiled=True)  47.4 us
    ppermute x21, starting transfers between devices, sparse(): came.append(lax.ppermute(parts[d], 'space', ring))  44.6 us
    all_to_all x6, starting transfers between devices, exchange(): return lax.all_to_all(array, axis, split_axis=0, concat_axis=0, tiled=True)  40.5 us
    pallas_call x3, Pallas kernels, pick(): pl.pallas_call(functools.partial(pick_kernel, first_tile), out_shape=in_h...  30.5 us
    pallas_call x2, Pallas kernels, gather(): pl.pallas_call(functools.partial(gather_kernel, words.shape[0] // spaces,...  24 us
    cond x50, local copies, waits for them, and re-layouts  11.7 us
  transfers between devices with their start and end apart: 27, of which 16 were waited for; matrix products, arithmetic and copies ran while one was open for 0% of the time, Pallas kernels for 8%

profile of v6, /device:TPU:1, one launch (start us, length us, event | category | flops | bytes accessed | tf_op | source)
XLA Modules:
  0.0 363.8 jit_solution(1745675752258100902)
XLA Ops:
  2.1 8.6 %all-to-all-start.11 = ((s32[32,1,128]{2,1,0:T(1,128)}), s32[32,1,128]{2,1,0:T(1,128)S(1)}, u32[]{:S(2)}, u32[]{:S(2)}) async-start(s32[32,1,128]{2,1,0:T(1,128)} %broadcast_in_dim.34), calls=%async_computation.11 | async-start | bytes 32768 | tf_op jit(solution)/shard_map/all_to_all | solution.py:336
  10.7 6.9 %all-to-all-done.11 = s32[32,1,128]{2,1,0:T(1,128)S(1)} async-done(((s32[32,1,128]{2,1,0:T(1,128)}), s32[32,1,128]{2,1,0:T(1,128)S(1)}, u32[]{:S(2)}, u32[]{:S(2)}) %all-to-all-start.11) | async-done | bytes 16416 | tf_op jit(solution)/shard_map/all_to_all | solution.py:336
  17.6 2.3 route.1
  19.9 8.2 %all-to-all-start.12 = ((s32[8,8,128]{2,1,0:T(8,128)}), s32[8,8,128]{2,1,0:T(8,128)S(1)}, u32[]{:S(2)}, u32[]{:S(2)}) async-start(s32[8,8,128]{2,1,0:T(8,128)} %get-tuple-element.77), calls=%async_computation.12 | async-start | bytes 65536 | tf_op jit(solution)/shard_map/all_to_all | solution.py:336
  28.1 6.9 %all-to-all-done.12 = s32[8,8,128]{2,1,0:T(8,128)S(1)} async-done(((s32[8,8,128]{2,1,0:T(8,128)}), s32[8,8,128]{2,1,0:T(8,128)S(1)}, u32[]{:S(2)}, u32[]{:S(2)}) %all-to-all-start.12) | async-done | bytes 32800 | tf_op jit(solution)/shard_map/all_to_all | solution.py:336
  36.3 327.5 %conditional.1 = (bf16[2048,1024]{1,0:T(8,128)(2,1)}, f32[128,512]{1,0:T(8,128)}) conditional(s32[]{:T(128)} %convert_element_type.39, (s32[32,128]{1,0:T(8,128)S(1)}, bf16[16,65536]{1,0:T(8,128)(2,1)}, s32[16,8,128]{2,1,0:T(8,128)S(1)}, s32[32]{0:T(128)}, bf16[32,64,128]{2,1,0:T(8,128)(2,1)}, /*index=5*/bf16[2048,1024]{1,0:T(8,128)(2,1)}, s32[]{:T(128)}, ...), branch_computations={%region_1.4_spmd, %region_4.7_spmd} | conditional | flops 1513478 | bytes 131691088 | solution.py:402
  36.4 14.0 %gather.3 = (bf16[44,2,8,128]{3,2,1,0:T(8,128)(2,1)S(1)}, bf16[44,2,8,128]{3,2,1,0:T(8,128)(2,1)S(1)}, bf16[44,2,8,128]{3,2,1,0:T(8,128)(2,1)S(1)}, bf16[44,2,8,...) custom-call(s32[2048]{0:T(1024)S(1)} %bitcast.28, ...), custom_call_target="tpu_custom_call" | custom-call | tf_op jit(solution)/shard_map/cond/branch_0_fun/gather/pallas_call | solution.py:190
  51.0 2.1 collective-permute-start.16
  53.2 3.3 collective-permute-start.17
  56.5 2.0 collective-permute-start.18
  58.5 1.6 collective-permute-start.19
  60.1 4.1 %collective-permute-start.10 = (bf16[44,2,8,128]{3,2,1,0:T(8,128)(2,1)S(1)}, bf16[44,2,8,128]{3,2,1,0:T(8,128)(2,1)S(1)}, u32[]{:S(2)}, u32[]{:S(2)}) collective-permute-start(bf16[44,2,8,128]{3,2,1,0:T(8,128)(2,1)S(1)} %get-tuple-element.46), channel_id=1, source_target_pairs={{0,4},{1,5},{2,6},{3,7},{4,0},{5,1},{6,2},{7,3},{8,12},{9,13},{10,... | collective-permute-start | bytes 540680 | tf_op jit(solution)/shard_map/cond/branch_0_fun/ppermute | solution.py:397
  64.2 4.5 %collective-permute-done.16.refs_19_ = bf16[28,2,8,128]{3,2,1,0:T(8,128)(2,1)S(1)} collective-permute-done((bf16[28,2,8,128]{3,2,1,0:T(8,128)(2,1)S(1)}, bf16[28,2,8,128]{3,2,1,0:T(8,128)(2,1)S(1)}, u32[]{:S(2)}, u32[]{:S(2)}) %collective-permute-start.16) | collective-permute-done | bytes 114720 | tf_op jit(solution)/shard_map/cond/branch_0_fun/ppermute | solution.py:397
  68.7 5.6 %collective-permute-start.12 = (bf16[44,2,8,128]{3,2,1,0:T(8,128)(2,1)S(1)}, bf16[44,2,8,128]{3,2,1,0:T(8,128)(2,1)S(1)}, u32[]{:S(2)}, u32[]{:S(2)}) collective-permute-start(bf16[44,2,8,128]{3,2,1,0:T(8,128)(2,1)S(1)} %get-tuple-element.48), channel_id=1, source_target_pairs={{0,6},{1,7},{2,0},{3,1},{4,2},{5,3},{6,4},{7,5},{8,14},{9,15},{10,... | collective-permute-start | bytes 540680 | tf_op jit(solution)/shard_map/cond/branch_0_fun/ppermute | solution.py:397
  74.2 2.6 collective-permute-done.19.refs_22_
  76.9 10.0 %gather.2 = (bf16[56,2,8,128]{3,2,1,0:T(8,128)(2,1)S(1)}, bf16[56,2,8,128]{3,2,1,0:T(8,128)(2,1)S(1)}, bf16[56,2,8,128]{3,2,1,0:T(8,128)(2,1)S(1)}, bf16[56,2,8,...) custom-call(s32[2048]{0:T(1024)S(1)} %bitcast.29, ...), custom_call_target="tpu_custom_call" | custom-call | tf_op jit(solution)/shard_map/cond/branch_0_fun/gather/pallas_call | solution.py:190
  86.9 21.9 %collective-permute-done.20.refs_23_ = bf16[28,2,8,128]{3,2,1,0:T(8,128)(2,1)S(1)} collective-permute-done((bf16[28,2,8,128]{3,2,1,0:T(8,128)(2,1)S(1)}, bf16[28,2,8,128]{3,2,1,0:T(8,128)(2,1)S(1)}, u32[]{:S(2)}, u32[]{:S(2)}) %collective-permute-start.20) | collective-permute-done | bytes 114720 | tf_op jit(solution)/shard_map/cond/branch_0_fun/ppermute | solution.py:397
  108.8 2.8 collective-permute-start.1
  111.6 2.5 collective-permute-start.8
  114.9 16.3 %collective-permute-done.7.refs_9_ = bf16[44,2,8,128]{3,2,1,0:T(8,128)(2,1)S(1)} collective-permute-done((bf16[44,2,8,128]{3,2,1,0:T(8,128)(2,1)S(1)}, bf16[44,2,8,128]{3,2,1,0:T(8,128)(2,1)S(1)}, u32[]{:S(2)}, u32[]{:S(2)}) %collective-permute-start.7) | collective-permute-done | bytes 180256 | tf_op jit(solution)/shard_map/cond/branch_0_fun/ppermute | solution.py:397
  131.2 1.8 collective-permute-start.2
  132.9 1.1 collective-permute-done.8.refs_10_
  134.0 15.6 %collective-permute-start.3 = (bf16[56,2,8,128]{3,2,1,0:T(8,128)(2,1)S(1)}, bf16[56,2,8,128]{3,2,1,0:T(8,128)(2,1)S(1)}, u32[]{:S(2)}, u32[]{:S(2)}) collective-permute-start(bf16[56,2,8,128]{3,2,1,0:T(8,128)(2,1)S(1)} %get-tuple-element.38), channel_id=1, source_target_pairs={{0,4},{1,5},{2,6},{3,7},{4,0},{5,1},{6,2},{7,3},{8,12},{9,13},{10,... | collective-permute-start | bytes 688136 | tf_op jit(solution)/shard_map/cond/branch_0_fun/ppermute | solution.py:397
  149.6 5.2 %collective-permute-done.9.refs_11_ = bf16[44,2,8,128]{3,2,1,0:T(8,128)(2,1)S(1)} collective-permute-done((bf16[44,2,8,128]{3,2,1,0:T(8,128)(2,1)S(1)}, bf16[44,2,8,128]{3,2,1,0:T(8,128)(2,1)S(1)}, u32[]{:S(2)}, u32[]{:S(2)}) %collective-permute-start.9) | collective-permute-done | bytes 180256 | tf_op jit(solution)/shard_map/cond/branch_0_fun/ppermute | solution.py:397
  154.8 1.6 collective-permute-start.4
  156.7 9.1 %collective-permute-done.2.refs_3_ = bf16[56,2,8,128]{3,2,1,0:T(8,128)(2,1)S(1)} collective-permute-done((bf16[56,2,8,128]{3,2,1,0:T(8,128)(2,1)S(1)}, bf16[56,2,8,128]{3,2,1,0:T(8,128)(2,1)S(1)}, u32[]{:S(2)}, u32[]{:S(2)}) %collective-permute-start.2) | collective-permute-done | bytes 229408 | tf_op jit(solution)/shard_map/cond/branch_0_fun/ppermute | solution.py:397
  165.8 6.0 %collective-permute-done.3.refs_4_ = bf16[56,2,8,128]{3,2,1,0:T(8,128)(2,1)S(1)} collective-permute-done((bf16[56,2,8,128]{3,2,1,0:T(8,128)(2,1)S(1)}, bf16[56,2,8,128]{3,2,1,0:T(8,128)(2,1)S(1)}, u32[]{:S(2)}, u32[]{:S(2)}) %collective-permute-start.3) | collective-permute-done | bytes 229408 | tf_op jit(solution)/shard_map/cond/branch_0_fun/ppermute | solution.py:397
  171.9 1.7 collective-permute-done.4.refs_5_
  173.6 6.7 %collective-permute-done.6.refs_7_ = bf16[56,2,8,128]{3,2,1,0:T(8,128)(2,1)S(1)} collective-permute-done((bf16[56,2,8,128]{3,2,1,0:T(8,128)(2,1)S(1)}, bf16[56,2,8,128]{3,2,1,0:T(8,128)(2,1)S(1)}, u32[]{:S(2)}, u32[]{:S(2)}) %collective-permute-start.6) | collective-permute-done | bytes 229408 | tf_op jit(solution)/shard_map/cond/branch_0_fun/ppermute | solution.py:397
  180.3 11.6 %pick.6 = bf16[32,8,2,8,128]{4,3,2,1,0:T(8,128)(2,1)} custom-call(s32[4096]{0:T(1024)S(1)} %bitcast.37, bf16[56,2,8,128]{3,2,1,0:T(8,128)(2,1)S(1)} %get-tuple-element.34.refs_0_, bf16[56,2,8,128]{3,2,1,0:T(8,128)(2,1)S(1)} %collective-permute-done.refs_1_, bf16[56,2,8,128]{3,2,1,0:T(8,128)(2,1)S(1)} %collective-permute-done.1.refs_2_, ...), custom_call_target="tpu_custom_call" | custom-call | tf_op jit(solution)/shard_map/cond/branch_0_fun/pick/pallas_call | solution.py:214
  195.2 7.4 %all-to-all-start.2 = ((bf16[32,8,2,8,128]{4,3,2,1,0:T(8,128)(2,1)}), bf16[32,8,2,8,128]{4,3,2,1,0:T(8,128)(2,1)S(1)}, u32[]{:S(2)}, u32[]{:S(2)}) async-start(bf16[32,8,2,8,128]{4,3,2,1,0:T(8,128)(2,1)} %pick.6), calls=%async_computation.2 | async-start | bytes 2097152 | tf_op jit(solution)/shard_map/cond/branch_0_fun/all_to_all | solution.py:336
  207.3 10.6 %pick.5 = bf16[32,12,2,8,128]{4,3,2,1,0:T(8,128)(2,1)} custom-call(s32[4096]{0:T(1024)S(1)} %bitcast.38, bf16[56,2,8,128]{3,2,1,0:T(8,128)(2,1)S(1)} %get-tuple-element.34.refs_0_, bf16[56,2,8,128]{3,2,1,0:T(8,128)(2,1)S(1)} %collective-permute-done.refs_1_, bf16[56,2,8,128]{3,2,1,0:T(8,128)(2,1)S(1)} %collective-permute-done.1.refs_2_, ...), custom_call_target="tpu_custom_call" | custom-call | tf_op jit(solution)/shard_map/cond/branch_0_fun/pick/pallas_call | solution.py:214
  217.9 1.7 all-to-all-done.2.refs_2_
  219.5 5.7 %all-to-all-start.1 = ((bf16[32,12,2,8,128]{4,3,2,1,0:T(8,128)(2,1)}), bf16[32,12,2,8,128]{4,3,2,1,0:T(8,128)(2,1)S(1)}, u32[]{:S(2)}, u32[]{:S(2)}) async-start(bf16[32,12,2,8,128]{4,3,2,1,0:T(8,128)(2,1)} %pick.5), calls=%async_computation.1 | async-start | bytes 3145728 | tf_op jit(solution)/shard_map/cond/branch_0_fun/all_to_all | solution.py:336
  226.2 0.9 copy-done.5
  227.2 0.9 copy-done.7
  228.1 0.9 copy-done.9
  229.0 8.4 %pick.4 = bf16[32,12,2,8,128]{4,3,2,1,0:T(8,128)(2,1)} custom-call(s32[4096]{0:T(1024)S(1)} %bitcast.39, bf16[56,2,8,128]{3,2,1,0:T(8,128)(2,1)S(1)} %get-tuple-element.34.refs_0_, bf16[56,2,8,128]{3,2,1,0:T(8,128)(2,1)S(1)} %collective-permute-done.refs_1_, bf16[56,2,8,128]{3,2,1,0:T(8,128)(2,1)S(1)} %collective-permute-done.1.refs_2_, ...), custom_call_target="tpu_custom_call" | custom-call | tf_op jit(solution)/shard_map/cond/branch_0_fun/pick/pallas_call | solution.py:214
  237.5 10.5 %all-to-all-done.1.refs_1_ = bf16[32,12,2,8,128]{4,3,2,1,0:T(8,128)(2,1)S(1)} async-done(((bf16[32,12,2,8,128]{4,3,2,1,0:T(8,128)(2,1)}), bf16[32,12,2,8,128]{4,3,2,1,0:T(8,128)(2,1)S(1)}, u32[]{:S(2)}, u32[]{:S(2)}) %all-to-all-start.1) | async-done | bytes 1572896 | tf_op jit(solution)/shard_map/cond/branch_0_fun/all_to_all | solution.py:336
  247.9 27.1 %all_to_all.54.refs_0_ = bf16[32,12,2,8,128]{4,3,2,1,0:T(8,128)(2,1)S(1)} all-to-all(bf16[32,12,2,8,128]{4,3,2,1,0:T(8,128)(2,1)} %pick.4), channel_id=1, replica_groups=mesh['tm'=32,'space'=8] {'tm'}, dimensions={0} | all-to-all | bytes 3145728 | tf_op jit(solution)/shard_map/cond/branch_0_fun/all_to_all | solution.py:336
  275.0 10.1 %project.2 = (bf16[2048,512]{1,0:T(8,128)(2,1)}, bf16[32,16,1024]{2,1,0:T(8,128)(2,1)S(1)}) custom-call(s32[32]{0:T(128)S(1)} %copy-done.28, bf16[32,12,2,8,128]{4,3,2,1,0:T(8,128)(2,1)S(1)} %all_to_all.54.refs_0_, bf16[32,12,2,8,128]{4,3,2,1,0:T(8,128)(2,1)S(1)} %all-to-all-done.1.refs_1_, bf16[32,8,2,8,128]{4,3,2,1,0:T(8,128)(2,1)S(1)} %all-to-all-done.2.refs_2_, ...), custom_call_target="tpu_custom_call" | custom-call | tf_op jit(solution)/shard_map/cond/branch_0_fun/project/pallas_call | solution.py:283
  285.2 20.3 %all_to_all.55 = bf16[32,16,1024]{2,1,0:T(8,128)(2,1)S(1)} all-to-all(bf16[32,16,1024]{2,1,0:T(8,128)(2,1)S(1)} %get-tuple-element.60), channel_id=1, replica_groups=mesh['tm'=32,'space'=8] {'tm'}, dimensions={0} | all-to-all | bytes 2097152 | tf_op jit(solution)/shard_map/cond/branch_0_fun/all_to_all | solution.py:336
  306.5 6.5 %all-to-all-start.4 = ((f32[8,16,1024]{2,1,0:T(8,128)}), f32[8,16,1024]{2,1,0:T(8,128)S(1)}, u32[]{:S(2)}, u32[]{:S(2)}) async-start(f32[8,16,1024]{2,1,0:T(8,128)} %broadcast_in_dim.22), calls=%async_computation.4 | async-start | bytes 1048576 | tf_op jit(solution)/shard_map/cond/branch_0_fun/all_to_all | solution.py:336
  313.0 18.0 %all-to-all-done.4 = f32[8,16,1024]{2,1,0:T(8,128)S(1)} async-done(((f32[8,16,1024]{2,1,0:T(8,128)}), f32[8,16,1024]{2,1,0:T(8,128)S(1)}, u32[]{:S(2)}, u32[]{:S(2)}) %all-to-all-start.4) | async-done | bytes 524320 | tf_op jit(solution)/shard_map/cond/branch_0_fun/all_to_all | solution.py:336
  331.1 1.1 broadcast_in_dim.23
  332.2 4.1 %all-to-all-start.5 = ((bf16[32,16,1152]{2,1,0:T(8,128)(2,1)}), bf16[32,16,1152]{2,1,0:T(8,128)(2,1)S(1)}, u32[]{:S(2)}, u32[]{:S(2)}) async-start(bf16[32,16,1152]{2,1,0:T(8,128)(2,1)} %broadcast_in_dim.23), calls=%async_computation.5 | async-start | bytes 2359296 | tf_op jit(solution)/shard_map/cond/branch_0_fun/all_to_all | solution.py:336
  336.3 18.4 %all-to-all-done.5 = bf16[32,16,1152]{2,1,0:T(8,128)(2,1)S(1)} async-done(((bf16[32,16,1152]{2,1,0:T(8,128)(2,1)}), bf16[32,16,1152]{2,1,0:T(8,128)(2,1)S(1)}, u32[]{:S(2)}, u32[]{:S(2)}) %all-to-all-start.5) | async-done | bytes 1179680 | tf_op jit(solution)/shard_map/cond/branch_0_fun/all_to_all | solution.py:336
  355.8 8.0 %rotate.2 = bf16[2048,1024]{1,0:T(8,128)(2,1)} custom-call(bf16[2048,512]{1,0:T(8,128)(2,1)S(1)} %copy-done, bf16[512,1024]{1,0:T(8,128)(2,1)S(1)} %bitcast.26, bf16[2048,1024]{1,0:T(8,128)(2,1)} %get-tuple-element.59.refs_4_.basis_ref, f32[1,1024]{1,0:T(1,128)S(1)} %bitcast.41), custom_call_target="tpu_custom_call" | custom-call | tf_op jit(solution)/shard_map/cond/branch_0_fun/rotate/pallas_call | solution.py:318
  (85 shorter events, 14.8 us)
Async XLA Ops:
  2.1 15.5 %all-to-all-start.11 = ((s32[32,1,128]{2,1,0:T(1,128)}), s32[32,1,128]{2,1,0:T(1,128)S(1)}, u32[]{:S(2)}, u32[]{:S(2)}) async-start(s32[32,1,128]{2,1,0:T(1,128)} %broadcast_in_dim.34), calls=%async_computation.11 | async-start | bytes 32768 | tf_op jit(solution)/shard_map/all_to_all | solution.py:336
  19.9 15.1 %all-to-all-start.12 = ((s32[8,8,128]{2,1,0:T(8,128)}), s32[8,8,128]{2,1,0:T(8,128)S(1)}, u32[]{:S(2)}, u32[]{:S(2)}) async-start(s32[8,8,128]{2,1,0:T(8,128)} %get-tuple-element.77), calls=%async_computation.12 | async-start | bytes 65536 | tf_op jit(solution)/shard_map/all_to_all | solution.py:336
  36.3 144.0 %copy-start.24 = (s32[32,128]{1,0:T(8,128)}, s32[32,128]{1,0:T(8,128)S(1)}, u32[]{:S(2)}) copy-start(s32[32,128]{1,0:T(8,128)S(1)} %get-tuple-element.31) | copy-start | bytes 49156 | tf_op jit(solution)/shard_map/cond
  36.3 40.6 %copy-start.21 = (bf16[16,65536]{1,0:T(8,128)(2,1)S(1)}, bf16[16,65536]{1,0:T(8,128)(2,1)}, u32[]{:S(2)}) copy-start(bf16[16,65536]{1,0:T(8,128)(2,1)} %get-tuple-element.33) | copy-start | bytes 6291460 | tf_op jit(solution)/shard_map/cond
  50.4 8.1 %collective-permute-start.14 = (bf16[28,2,8,128]{3,2,1,0:T(8,128)(2,1)S(1)}, bf16[28,2,8,128]{3,2,1,0:T(8,128)(2,1)S(1)}, u32[]{:S(2)}, u32[]{:S(2)}) collective-permute-start(bf16[28,2,8,128]{3,2,1,0:T(8,128)(2,1)S(1)} %get-tuple-element.51), channel_id=1, source_target_pairs={{0,1},{1,2},{2,3},{3,4},{4,5},{5,6},{6,7},{7,0},{8,9},{9,10},{10,1... | collective-permute-start | bytes 344072 | tf_op jit(solution)/shard_map/cond/branch_0_fun/ppermute | solution.py:397
  50.8 9.3 %collective-permute-start.15 = (bf16[28,2,8,128]{3,2,1,0:T(8,128)(2,1)S(1)}, bf16[28,2,8,128]{3,2,1,0:T(8,128)(2,1)S(1)}, u32[]{:S(2)}, u32[]{:S(2)}) collective-permute-start(bf16[28,2,8,128]{3,2,1,0:T(8,128)(2,1)S(1)} %get-tuple-element.52), channel_id=1, source_target_pairs={{0,2},{1,3},{2,4},{3,5},{4,6},{5,7},{6,0},{7,1},{8,10},{9,11},{10,... | collective-permute-start | bytes 344072 | tf_op jit(solution)/shard_map/cond/branch_0_fun/ppermute | solution.py:397
  51.0 17.6 %collective-permute-start.16 = (bf16[28,2,8,128]{3,2,1,0:T(8,128)(2,1)S(1)}, bf16[28,2,8,128]{3,2,1,0:T(8,128)(2,1)S(1)}, u32[]{:S(2)}, u32[]{:S(2)}) collective-permute-start(bf16[28,2,8,128]{3,2,1,0:T(8,128)(2,1)S(1)} %get-tuple-element.53), channel_id=1, source_target_pairs={{0,3},{1,4},{2,5},{3,6},{4,7},{5,0},{6,1},{7,2},{8,11},{9,12},{10,... | collective-permute-start | bytes 344072 | tf_op jit(solution)/shard_map/cond/branch_0_fun/ppermute | solution.py:397
  53.2 15.5 %collective-permute-start.17 = (bf16[28,2,8,128]{3,2,1,0:T(8,128)(2,1)S(1)}, bf16[28,2,8,128]{3,2,1,0:T(8,128)(2,1)S(1)}, u32[]{:S(2)}, u32[]{:S(2)}) collective-permute-start(bf16[28,2,8,128]{3,2,1,0:T(8,128)(2,1)S(1)} %get-tuple-element.54), channel_id=1, source_target_pairs={{0,4},{1,5},{2,6},{3,7},{4,0},{5,1},{6,2},{7,3},{8,12},{9,13},{10,... | collective-permute-start | bytes 344072 | tf_op jit(solution)/shard_map/cond/branch_0_fun/ppermute | solution.py:397
  56.5 17.8 %collective-permute-start.18 = (bf16[28,2,8,128]{3,2,1,0:T(8,128)(2,1)S(1)}, bf16[28,2,8,128]{3,2,1,0:T(8,128)(2,1)S(1)}, u32[]{:S(2)}, u32[]{:S(2)}) collective-permute-start(bf16[28,2,8,128]{3,2,1,0:T(8,128)(2,1)S(1)} %get-tuple-element.55), channel_id=1, source_target_pairs={{0,5},{1,6},{2,7},{3,0},{4,1},{5,2},{6,3},{7,4},{8,13},{9,14},{10,... | collective-permute-start | bytes 344072 | tf_op jit(solution)/shard_map/cond/branch_0_fun/ppermute | solution.py:397
  58.5 18.4 %collective-permute-start.19 = (bf16[28,2,8,128]{3,2,1,0:T(8,128)(2,1)S(1)}, bf16[28,2,8,128]{3,2,1,0:T(8,128)(2,1)S(1)}, u32[]{:S(2)}, u32[]{:S(2)}) collective-permute-start(bf16[28,2,8,128]{3,2,1,0:T(8,128)(2,1)S(1)} %get-tuple-element.56), channel_id=1, source_target_pairs={{0,6},{1,7},{2,0},{3,1},{4,2},{5,3},{6,4},{7,5},{8,14},{9,15},{10,... | collective-permute-start | bytes 344072 | tf_op jit(solution)/shard_map/cond/branch_0_fun/ppermute | solution.py:397
  60.1 48.7 %collective-permute-start.10 = (bf16[44,2,8,128]{3,2,1,0:T(8,128)(2,1)S(1)}, bf16[44,2,8,128]{3,2,1,0:T(8,128)(2,1)S(1)}, u32[]{:S(2)}, u32[]{:S(2)}) collective-permute-start(bf16[44,2,8,128]{3,2,1,0:T(8,128)(2,1)S(1)} %get-tuple-element.46), channel_id=1, source_target_pairs={{0,4},{1,5},{2,6},{3,7},{4,0},{5,1},{6,2},{7,3},{8,12},{9,13},{10,... | collective-permute-start | bytes 540680 | tf_op jit(solution)/shard_map/cond/branch_0_fun/ppermute | solution.py:397
  68.7 43.0 %collective-permute-start.11 = (bf16[44,2,8,128]{3,2,1,0:T(8,128)(2,1)S(1)}, bf16[44,2,8,128]{3,2,1,0:T(8,128)(2,1)S(1)}, u32[]{:S(2)}, u32[]{:S(2)}) collective-permute-start(bf16[44,2,8,128]{3,2,1,0:T(8,128)(2,1)S(1)} %get-tuple-element.47), channel_id=1, source_target_pairs={{0,5},{1,6},{2,7},{3,0},{4,1},{5,2},{6,3},{7,4},{8,13},{9,14},{10,... | collective-permute-start | bytes 540680 | tf_op jit(solution)/shard_map/cond/branch_0_fun/ppermute | solution.py:397
  68.7 43.0 %collective-permute-start.12 = (bf16[44,2,8,128]{3,2,1,0:T(8,128)(2,1)S(1)}, bf16[44,2,8,128]{3,2,1,0:T(8,128)(2,1)S(1)}, u32[]{:S(2)}, u32[]{:S(2)}) collective-permute-start(bf16[44,2,8,128]{3,2,1,0:T(8,128)(2,1)S(1)} %get-tuple-element.48), channel_id=1, source_target_pairs={{0,6},{1,7},{2,0},{3,1},{4,2},{5,3},{6,4},{7,5},{8,14},{9,15},{10,... | collective-permute-start | bytes 540680 | tf_op jit(solution)/shard_map/cond/branch_0_fun/ppermute | solution.py:397
  74.2 39.9 %collective-permute-start.13 = (bf16[44,2,8,128]{3,2,1,0:T(8,128)(2,1)S(1)}, bf16[44,2,8,128]{3,2,1,0:T(8,128)(2,1)S(1)}, u32[]{:S(2)}, u32[]{:S(2)}) collective-permute-start(bf16[44,2,8,128]{3,2,1,0:T(8,128)(2,1)S(1)} %get-tuple-element.49), channel_id=1, source_target_pairs={{0,7},{1,0},{2,1},{3,2},{4,3},{5,4},{6,5},{7,6},{8,15},{9,8},{10,9... | collective-permute-start | bytes 540680 | tf_op jit(solution)/shard_map/cond/branch_0_fun/ppermute | solution.py:397
  76.9 31.9 %collective-permute-start.20 = (bf16[28,2,8,128]{3,2,1,0:T(8,128)(2,1)S(1)}, bf16[28,2,8,128]{3,2,1,0:T(8,128)(2,1)S(1)}, u32[]{:S(2)}, u32[]{:S(2)}) collective-permute-start(bf16[28,2,8,128]{3,2,1,0:T(8,128)(2,1)S(1)} %get-tuple-element.57), channel_id=1, source_target_pairs={{0,7},{1,0},{2,1},{3,2},{4,3},{5,4},{6,5},{7,6},{8,15},{9,8},{10,9... | collective-permute-start | bytes 344072 | tf_op jit(solution)/shard_map/cond/branch_0_fun/ppermute | solution.py:397
  108.8 47.6 %collective-permute-start = (bf16[56,2,8,128]{3,2,1,0:T(8,128)(2,1)S(1)}, bf16[56,2,8,128]{3,2,1,0:T(8,128)(2,1)S(1)}, u32[]{:S(2)}, u32[]{:S(2)}) collective-permute-start(bf16[56,2,8,128]{3,2,1,0:T(8,128)(2,1)S(1)} %get-tuple-element.35), channel_id=1, source_target_pairs={{0,1},{1,2},{2,3},{3,4},{4,5},{5,6},{6,7},{7,0},{8,9},{9,10},{10,1... | collective-permute-start | bytes 688136 | tf_op jit(solution)/shard_map/cond/branch_0_fun/ppermute | solution.py:397
  108.8 47.6 %collective-permute-start.1 = (bf16[56,2,8,128]{3,2,1,0:T(8,128)(2,1)S(1)}, bf16[56,2,8,128]{3,2,1,0:T(8,128)(2,1)S(1)}, u32[]{:S(2)}, u32[]{:S(2)}) collective-permute-start(bf16[56,2,8,128]{3,2,1,0:T(8,128)(2,1)S(1)} %get-tuple-element.36), channel_id=1, source_target_pairs={{0,2},{1,3},{2,4},{3,5},{4,6},{5,7},{6,0},{7,1},{8,10},{9,11},{10,... | collective-permute-start | bytes 688136 | tf_op jit(solution)/shard_map/cond/branch_0_fun/ppermute | solution.py:397
  111.6 19.5 %collective-permute-start.7 = (bf16[44,2,8,128]{3,2,1,0:T(8,128)(2,1)S(1)}, bf16[44,2,8,128]{3,2,1,0:T(8,128)(2,1)S(1)}, u32[]{:S(2)}, u32[]{:S(2)}) collective-permute-start(bf16[44,2,8,128]{3,2,1,0:T(8,128)(2,1)S(1)} %get-tuple-element.43), channel_id=1, source_target_pairs={{0,1},{1,2},{2,3},{3,4},{4,5},{5,6},{6,7},{7,0},{8,9},{9,10},{10,1... | collective-permute-start | bytes 540680 | tf_op jit(solution)/shard_map/cond/branch_0_fun/ppermute | solution.py:397
  111.6 22.4 %collective-permute-start.8 = (bf16[44,2,8,128]{3,2,1,0:T(8,128)(2,1)S(1)}, bf16[44,2,8,128]{3,2,1,0:T(8,128)(2,1)S(1)}, u32[]{:S(2)}, u32[]{:S(2)}) collective-permute-start(bf16[44,2,8,128]{3,2,1,0:T(8,128)(2,1)S(1)} %get-tuple-element.44), channel_id=1, source_target_pairs={{0,2},{1,3},{2,4},{3,5},{4,6},{5,7},{6,0},{7,1},{8,10},{9,11},{10,... | collective-permute-start | bytes 540680 | tf_op jit(solution)/shard_map/cond/branch_0_fun/ppermute | solution.py:397
  114.2 40.7 %collective-permute-start.9 = (bf16[44,2,8,128]{3,2,1,0:T(8,128)(2,1)S(1)}, bf16[44,2,8,128]{3,2,1,0:T(8,128)(2,1)S(1)}, u32[]{:S(2)}, u32[]{:S(2)}) collective-permute-start(bf16[44,2,8,128]{3,2,1,0:T(8,128)(2,1)S(1)} %get-tuple-element.45), channel_id=1, source_target_pairs={{0,3},{1,4},{2,5},{3,6},{4,7},{5,0},{6,1},{7,2},{8,11},{9,12},{10,... | collective-permute-start | bytes 540680 | tf_op jit(solution)/shard_map/cond/branch_0_fun/ppermute | solution.py:397
  131.2 34.7 %collective-permute-start.2 = (bf16[56,2,8,128]{3,2,1,0:T(8,128)(2,1)S(1)}, bf16[56,2,8,128]{3,2,1,0:T(8,128)(2,1)S(1)}, u32[]{:S(2)}, u32[]{:S(2)}) collective-permute-start(bf16[56,2,8,128]{3,2,1,0:T(8,128)(2,1)S(1)} %get-tuple-element.37), channel_id=1, source_target_pairs={{0,3},{1,4},{2,5},{3,6},{4,7},{5,0},{6,1},{7,2},{8,11},{9,12},{10,... | collective-permute-start | bytes 688136 | tf_op jit(solution)/shard_map/cond/branch_0_fun/ppermute | solution.py:397
  134.0 37.8 %collective-permute-start.3 = (bf16[56,2,8,128]{3,2,1,0:T(8,128)(2,1)S(1)}, bf16[56,2,8,128]{3,2,1,0:T(8,128)(2,1)S(1)}, u32[]{:S(2)}, u32[]{:S(2)}) collective-permute-start(bf16[56,2,8,128]{3,2,1,0:T(8,128)(2,1)S(1)} %get-tuple-element.38), channel_id=1, source_target_pairs={{0,4},{1,5},{2,6},{3,7},{4,0},{5,1},{6,2},{7,3},{8,12},{9,13},{10,... | collective-permute-start | bytes 688136 | tf_op jit(solution)/shard_map/cond/branch_0_fun/ppermute | solution.py:397
  154.8 18.8 %collective-permute-start.4 = (bf16[56,2,8,128]{3,2,1,0:T(8,128)(2,1)S(1)}, bf16[56,2,8,128]{3,2,1,0:T(8,128)(2,1)S(1)}, u32[]{:S(2)}, u32[]{:S(2)}) collective-permute-start(bf16[56,2,8,128]{3,2,1,0:T(8,128)(2,1)S(1)} %get-tuple-element.39), channel_id=1, source_target_pairs={{0,5},{1,6},{2,7},{3,0},{4,1},{5,2},{6,3},{7,4},{8,13},{9,14},{10,... | collective-permute-start | bytes 688136 | tf_op jit(solution)/shard_map/cond/branch_0_fun/ppermute | solution.py:397
  156.4 17.2 %collective-permute-start.5 = (bf16[56,2,8,128]{3,2,1,0:T(8,128)(2,1)S(1)}, bf16[56,2,8,128]{3,2,1,0:T(8,128)(2,1)S(1)}, u32[]{:S(2)}, u32[]{:S(2)}) collective-permute-start(bf16[56,2,8,128]{3,2,1,0:T(8,128)(2,1)S(1)} %get-tuple-element.40), channel_id=1, source_target_pairs={{0,6},{1,7},{2,0},{3,1},{4,2},{5,3},{6,4},{7,5},{8,14},{9,15},{10,... | collective-permute-start | bytes 688136 | tf_op jit(solution)/shard_map/cond/branch_0_fun/ppermute | solution.py:397
  156.4 23.9 %collective-permute-start.6 = (bf16[56,2,8,128]{3,2,1,0:T(8,128)(2,1)S(1)}, bf16[56,2,8,128]{3,2,1,0:T(8,128)(2,1)S(1)}, u32[]{:S(2)}, u32[]{:S(2)}) collective-permute-start(bf16[56,2,8,128]{3,2,1,0:T(8,128)(2,1)S(1)} %get-tuple-element.41), channel_id=1, source_target_pairs={{0,7},{1,0},{2,1},{3,2},{4,3},{5,4},{6,5},{7,6},{8,15},{9,8},{10,9... | collective-permute-start | bytes 688136 | tf_op jit(solution)/shard_map/cond/branch_0_fun/ppermute | solution.py:397
  171.9 30.8 %copy-start.2 = (bf16[56,2,8,128]{3,2,1,0:T(8,128)(2,1)}, bf16[56,2,8,128]{3,2,1,0:T(8,128)(2,1)S(1)}, u32[]{:S(2)}) copy-start(bf16[56,2,8,128]{3,2,1,0:T(8,128)(2,1)S(1)} %collective-permute-done.3.refs_4_) | copy-start | bytes 688132 | tf_op jit(solution)/shard_map/cond
  173.6 29.0 %copy-start.4 = (bf16[56,2,8,128]{3,2,1,0:T(8,128)(2,1)}, bf16[56,2,8,128]{3,2,1,0:T(8,128)(2,1)S(1)}, u32[]{:S(2)}) copy-start(bf16[56,2,8,128]{3,2,1,0:T(8,128)(2,1)S(1)} %collective-permute-done.4.refs_5_) | copy-start | bytes 688132 | tf_op jit(solution)/shard_map/cond
  173.6 29.0 %copy-start.6 = (bf16[56,2,8,128]{3,2,1,0:T(8,128)(2,1)}, bf16[56,2,8,128]{3,2,1,0:T(8,128)(2,1)S(1)}, u32[]{:S(2)}) copy-start(bf16[56,2,8,128]{3,2,1,0:T(8,128)(2,1)S(1)} %collective-permute-done.5.refs_6_) | copy-start | bytes 688132 | tf_op jit(solution)/shard_map/cond
  180.3 22.3 %copy-start.8 = (bf16[56,2,8,128]{3,2,1,0:T(8,128)(2,1)}, bf16[56,2,8,128]{3,2,1,0:T(8,128)(2,1)S(1)}, u32[]{:S(2)}) copy-start(bf16[56,2,8,128]{3,2,1,0:T(8,128)(2,1)S(1)} %collective-permute-done.6.refs_7_) | copy-start | bytes 688132 | tf_op jit(solution)/shard_map/cond
  193.2 0.7 copy-start.14
  195.2 7.4 %copy-start.25 = (s32[32,128]{1,0:T(8,128)S(1)}, s32[32,128]{1,0:T(8,128)}, u32[]{:S(2)}) copy-start(s32[32,128]{1,0:T(8,128)} %copy-done.24) | copy-start | bytes 49156 | tf_op jit(solution)/shard_map/cond
  195.2 24.3 %all-to-all-start.2 = ((bf16[32,8,2,8,128]{4,3,2,1,0:T(8,128)(2,1)}), bf16[32,8,2,8,128]{4,3,2,1,0:T(8,128)(2,1)S(1)}, u32[]{:S(2)}, u32[]{:S(2)}) async-start(bf16[32,8,2,8,128]{4,3,2,1,0:T(8,128)(2,1)} %pick.6), calls=%async_computation.2 | async-start | bytes 2097152 | tf_op jit(solution)/shard_map/cond/branch_0_fun/all_to_all | solution.py:336
  202.7 0.9 copy-start.11
  203.6 0.9 copy-start.13
  204.5 0.9 copy-start.15
  205.4 0.9 copy-start.17
  206.4 0.9 copy-start.19
  219.5 28.4 %all-to-all-start.1 = ((bf16[32,12,2,8,128]{4,3,2,1,0:T(8,128)(2,1)}), bf16[32,12,2,8,128]{4,3,2,1,0:T(8,128)(2,1)S(1)}, u32[]{:S(2)}, u32[]{:S(2)}) async-start(bf16[32,12,2,8,128]{4,3,2,1,0:T(8,128)(2,1)} %pick.5), calls=%async_computation.1 | async-start | bytes 3145728 | tf_op jit(solution)/shard_map/cond/branch_0_fun/all_to_all | solution.py:336
  225.3 0.9 copy-start.3
  226.2 0.9 copy-start.5
  227.2 0.9 copy-start.7
  228.1 0.9 copy-start.9
  237.5 37.6 %copy-start.22 = (bf16[32,64,128]{2,1,0:T(8,128)(2,1)S(1)}, bf16[32,64,128]{2,1,0:T(8,128)(2,1)}, u32[]{:S(2)}) copy-start(bf16[32,64,128]{2,1,0:T(8,128)(2,1)} %get-tuple-element.58.refs_3_) | copy-start | bytes 1572868 | tf_op jit(solution)/shard_map/cond
  237.5 37.6 %copy-start.28 = (s32[32]{0:T(128)S(1)}, s32[32]{0:T(128)}, u32[]{:S(2)}) copy-start(s32[32]{0:T(128)} %get-tuple-element.30.counts_ref) | copy-start | bytes 388 | tf_op jit(solution)/shard_map/cond
  306.5 24.5 %all-to-all-start.4 = ((f32[8,16,1024]{2,1,0:T(8,128)}), f32[8,16,1024]{2,1,0:T(8,128)S(1)}, u32[]{:S(2)}, u32[]{:S(2)}) async-start(f32[8,16,1024]{2,1,0:T(8,128)} %broadcast_in_dim.22), calls=%async_computation.4 | async-start | bytes 1048576 | tf_op jit(solution)/shard_map/cond/branch_0_fun/all_to_all | solution.py:336
  332.2 22.5 %all-to-all-start.5 = ((bf16[32,16,1152]{2,1,0:T(8,128)(2,1)}), bf16[32,16,1152]{2,1,0:T(8,128)(2,1)S(1)}, u32[]{:S(2)}, u32[]{:S(2)}) async-start(bf16[32,16,1152]{2,1,0:T(8,128)(2,1)} %broadcast_in_dim.23), calls=%async_computation.5 | async-start | bytes 2359296 | tf_op jit(solution)/shard_map/cond/branch_0_fun/all_to_all | solution.py:336
  336.3 19.5 %copy-start = (bf16[2048,512]{1,0:T(8,128)(2,1)S(1)}, bf16[2048,512]{1,0:T(8,128)(2,1)}, u32[]{:S(2)}) copy-start(bf16[2048,512]{1,0:T(8,128)(2,1)} %get-tuple-element.62.remapped_ref) | copy-start | bytes 6291460 | tf_op jit(solution)/shard_map/cond
  336.3 19.5 %copy-start.26 = (f32[1024]{0:T(1024)S(1)}, f32[1024]{0:T(1024)}, u32[]{:S(2)}) copy-start(f32[1024]{0:T(1024)} %get-tuple-element.63) | copy-start | bytes 12292 | tf_op jit(solution)/shard_map/cond
  (4 other events, 2.7 us)

commit v7 on v6

--- a/solution.py
+++ b/solution.py
@@ -14,8 +14,8 @@
 PAIR = MAXB * TILE
 ROWS = 8
 LANES = 128
-LIMITS = (112, 200, 256)
-SHARES = (12, 24, 32)
+LIMITS = (112, 172, 256)
+SHARES = (12, 20, 32)
 BF16 = jnp.bfloat16
 F32 = jnp.float32
 
@@ -162,7 +162,7 @@
 
         return lax.fori_loop(0, tiles, tile, carry, unroll=tiles if tiles <= 16 else 4)
 
-    lax.fori_loop(0, step_owners, owner, 0)
+    lax.fori_loop(0, step_owners, owner, 0, unroll=2)
 
 
 def gather_kernel(pitch, spans, words_ref, input_ref, *refs):
@@ -182,14 +182,15 @@
                 out_ref[k, h] = joined(source_ref[h, first], source_ref[h, second], word, low, bit)
             return carry
 
-        lax.fori_loop(0, out_ref.shape[0], tile, 0, unroll=4)
+        count = out_ref.shape[0]
+        lax.fori_loop(0, count, tile, 0, unroll=max(u for u in range(1, 15) if count % u == 0))
 
 
 def gather(words, source, spaces, spans, interpret=False):
     shapes = [((end - begin) // MAXB, 2, ROWS, LANES) for begin, end in spans for _ in range(spaces)]
     outs = pl.pallas_call(
         functools.partial(gather_kernel, words.shape[0] // spaces, spans),
-        out_shape=[jax.ShapeDtypeStruct(shape, BF16) for shape in shapes],
+        out_shape=[in_hbm(shape, BF16, interpret) for shape in shapes],
         grid_spec=pltpu.PrefetchScalarGridSpec(
             num_scalar_prefetch=1,
             grid=(1,),
@@ -217,7 +218,7 @@
         grid_spec=pltpu.PrefetchScalarGridSpec(
             num_scalar_prefetch=1,
             grid=(owners // step,),
-            in_specs=[pl.BlockSpec(memory_space=pl.ANY)] * len(parts),
+            in_specs=[pl.BlockSpec(memory_space=pl.ANY if interpret else pltpu.HBM)] * len(parts),
             out_specs=pl.BlockSpec((step, tiles, 2, ROWS, LANES), lambda i, words: (i, 0, 0, 0, 0)),
             scratch_shapes=[
                 pltpu.VMEM((size, 2, ROWS, LANES), BF16),
@@ -395,7 +396,10 @@
             for d in range(1, spaces):
                 ring = [(j, (j + d) % spaces) for j in range(spaces)]
                 came.append(lax.ppermute(parts[d], "space", ring))
-            chosen = pick(words, list(came), owners, *chunks[i], interpret)
+            parts = came if interpret else [
+                pltpu.with_memory_space_constraint(part, pltpu.HBM) for part in came
+            ]
+            chosen = pick(words, list(parts), owners, *chunks[i], interpret)
             arrived.append(exchange(chosen, "tm"))
         return finish(arrived)
 

time: 365 us -> 328 us (0.90)
  Pallas kernels: 75 us -> 54.8 us
  waiting for transfers between devices: 138 us -> 120 us
  starting transfers between devices: 85.1 us -> 96 us
  local copies, waits for them, and re-layouts: 15.5 us -> 5.12 us
    ppermute x21, waiting for transfers between devices: 75.3 us -> 53.9 us  [sparse(): came.append(lax.ppermute(parts[d], 'space', ring))]
    cond x50 -> x76, local copies, waits for them, and re-layouts: 11.7 us -> 1.35 us
    pallas_call x2, Pallas kernels: 24 us -> 13.8 us  [gather(): pl.pallas_call(functools.partial(gather_kernel, words.shape[0] // spaces,...]
    pallas_call x3, Pallas kernels: 30.5 us -> 20.5 us  [pick(): pl.pallas_call(functools.partial(pick_kernel, first_tile), out_shape=in_h...]
    ppermute x21, starting transfers between devices: 44.6 us -> 50.7 us  [sparse(): came.append(lax.ppermute(parts[d], 'space', ring))]
    all_to_all x6, starting transfers between devices: 40.5 us -> 45.3 us  [exchange(): return lax.all_to_all(array, axis, split_axis=0, concat_axis=0, tiled=True)]
    all_to_all x6, waiting for transfers between devices: 62.3 us -> 66.3 us  [exchange(): return lax.all_to_all(array, axis, split_axis=0, concat_axis=0, tiled=True)]
  transfers between devices with their start and end apart: 27 -> 27, of which waited for: 16 -> 17; matrix products, arithmetic and copies ran while one was open for 0% -> 0% of each run, Pallas kernels for 8% -> 6%
where the time goes in v7:
time: 328 us; the launch traced here: 327 us
  waiting for transfers between devices  120 us (37%)
  starting transfers between devices  96 us (29%)
  Pallas kernels  54.8 us (17%)
  blocking collectives  47.4 us (14%)
  local copies, waits for them, and re-layouts  5.12 us (2%)
    all_to_all x6, waiting for transfers between devices, exchange(): return lax.all_to_all(array, axis, split_axis=0, concat_axis=0, tiled=True)  66.3 us
    ppermute x21, waiting for transfers between devices, sparse(): came.append(lax.ppermute(parts[d], 'space', ring))  53.9 us
    ppermute x21, starting transfers between devices, sparse(): came.append(lax.ppermute(parts[d], 'space', ring))  50.7 us
    all_to_all x2, blocking collectives, exchange(): return lax.all_to_all(array, axis, split_axis=0, concat_axis=0, tiled=True)  47.4 us
    all_to_all x6, starting transfers between devices, exchange(): return lax.all_to_all(array, axis, split_axis=0, concat_axis=0, tiled=True)  45.3 us
    pallas_call x3, Pallas kernels, pick(): pl.pallas_call(functools.partial(pick_kernel, first_tile), out_shape=in_h...  20.5 us
    pallas_call x2, Pallas kernels, gather(): pl.pallas_call(functools.partial(gather_kernel, words.shape[0] // spaces,...  13.8 us
    pallas_call x1, Pallas kernels, project(): pl.pallas_call(functools.partial(project_kernel, group, tuple(starts)), o...  10.1 us
  transfers between devices with their start and end apart: 27, of which 17 were waited for; matrix products, arithmetic and copies ran while one was open for 0% of the time, Pallas kernels for 6%

profile of v7, /device:TPU:1, one launch (start us, length us, event | category | flops | bytes accessed | tf_op | source)
XLA Modules:
  0.0 326.8 jit_solution(13921392569497514213)
XLA Ops:
  2.1 8.6 %all-to-all-start.11 = ((s32[32,1,128]{2,1,0:T(1,128)}), s32[32,1,128]{2,1,0:T(1,128)S(1)}, u32[]{:S(2)}, u32[]{:S(2)}) async-start(s32[32,1,128]{2,1,0:T(1,128)} %broadcast_in_dim.34), calls=%async_computation.11 | async-start | bytes 32768 | tf_op jit(solution)/shard_map/all_to_all | solution.py:337
  10.7 6.9 %all-to-all-done.11 = s32[32,1,128]{2,1,0:T(1,128)S(1)} async-done(((s32[32,1,128]{2,1,0:T(1,128)}), s32[32,1,128]{2,1,0:T(1,128)S(1)}, u32[]{:S(2)}, u32[]{:S(2)}) %all-to-all-start.11) | async-done | bytes 16416 | tf_op jit(solution)/shard_map/all_to_all | solution.py:337
  17.6 2.3 route.1
  19.9 8.2 %all-to-all-start.12 = ((s32[8,8,128]{2,1,0:T(8,128)}), s32[8,8,128]{2,1,0:T(8,128)S(1)}, u32[]{:S(2)}, u32[]{:S(2)}) async-start(s32[8,8,128]{2,1,0:T(8,128)} %get-tuple-element.77), calls=%async_computation.12 | async-start | bytes 65536 | tf_op jit(solution)/shard_map/all_to_all | solution.py:337
  28.1 6.9 %all-to-all-done.12 = s32[8,8,128]{2,1,0:T(8,128)S(1)} async-done(((s32[8,8,128]{2,1,0:T(8,128)}), s32[8,8,128]{2,1,0:T(8,128)S(1)}, u32[]{:S(2)}, u32[]{:S(2)}) %all-to-all-start.12) | async-done | bytes 32800 | tf_op jit(solution)/shard_map/all_to_all | solution.py:337
  36.3 290.5 %conditional.1 = (bf16[2048,1024]{1,0:T(8,128)(2,1)}, f32[128,512]{1,0:T(8,128)}) conditional(s32[]{:T(128)} %convert_element_type.39, (s32[32,128]{1,0:T(8,128)S(1)}, bf16[16,65536]{1,0:T(8,128)(2,1)}, s32[16,8,128]{2,1,0:T(8,128)S(1)}, s32[32]{0:T(128)}, bf16[32,64,128]{2,1,0:T(8,128)(2,1)}, /*index=5*/bf16[2048,1024]{1,0:T(8,128)(2,1)}, s32[]{:T(128)}, ...), branch_computations={%region_1.4_spmd, %region_4.7_spmd} | conditional | flops 1513478 | bytes 131691088 | solution.py:406
  36.4 8.5 %gather.3 = (bf16[30,2,8,128]{3,2,1,0:T(8,128)(2,1)}, bf16[30,2,8,128]{3,2,1,0:T(8,128)(2,1)}, bf16[30,2,8,128]{3,2,1,0:T(8,128)(2,1)}, bf16[30,2,8,128]{3,2,1,0...) custom-call(s32[2048]{0:T(1024)S(1)} %bitcast.28, ...), custom_call_target="tpu_custom_call" | custom-call | tf_op jit(solution)/shard_map/cond/branch_0_fun/gather/pallas_call | solution.py:191
  45.5 3.9 %collective-permute-start.11 = (bf16[30,2,8,128]{3,2,1,0:T(8,128)(2,1)}, bf16[30,2,8,128]{3,2,1,0:T(8,128)(2,1)S(1)}, u32[]{:S(2)}, u32[]{:S(2)}) collective-permute-start(bf16[30,2,8,128]{3,2,1,0:T(8,128)(2,1)} %get-tuple-element.47), channel_id=1, source_target_pairs={{0,5},{1,6},{2,7},{3,0},{4,1},{5,2},{6,3},{7,4},{8,13},{9,14},{10,... | collective-permute-start | bytes 368648 | tf_op jit(solution)/shard_map/cond/branch_0_fun/ppermute | solution.py:398
  49.4 1.2 collective-permute-start.12
  50.9 5.3 %gather.2 = (bf16[56,2,8,128]{3,2,1,0:T(8,128)(2,1)}, bf16[56,2,8,128]{3,2,1,0:T(8,128)(2,1)}, bf16[56,2,8,128]{3,2,1,0:T(8,128)(2,1)}, bf16[56,2,8,128]{3,2,1,0...) custom-call(s32[2048]{0:T(1024)S(1)} %bitcast.29, ...), custom_call_target="tpu_custom_call" | custom-call | tf_op jit(solution)/shard_map/cond/branch_0_fun/gather/pallas_call | solution.py:191
  56.3 1.2 collective-permute-start
  57.5 1.2 collective-permute-start.1
  58.7 5.8 %collective-permute-start.7 = (bf16[30,2,8,128]{3,2,1,0:T(8,128)(2,1)S(1)}, bf16[30,2,8,128]{3,2,1,0:T(8,128)(2,1)S(1)}, u32[]{:S(2)}, u32[]{:S(2)}) collective-permute-start(bf16[30,2,8,128]{3,2,1,0:T(8,128)(2,1)S(1)} %copy-done.42), channel_id=1, source_target_pairs={{0,1},{1,2},{2,3},{3,4},{4,5},{5,6},{6,7},{7,0},{8,9},{9,10},{10,1... | collective-permute-start | bytes 368648 | tf_op jit(solution)/shard_map/cond/branch_0_fun/ppermute | solution.py:398
  64.5 3.0 collective-permute-done.12.refs_14_
  67.5 2.1 collective-permute-start.8
  69.6 3.4 %collective-permute-start.9 = (bf16[30,2,8,128]{3,2,1,0:T(8,128)(2,1)S(1)}, bf16[30,2,8,128]{3,2,1,0:T(8,128)(2,1)S(1)}, u32[]{:S(2)}, u32[]{:S(2)}) collective-permute-start(bf16[30,2,8,128]{3,2,1,0:T(8,128)(2,1)S(1)} %copy-done.40), channel_id=1, source_target_pairs={{0,3},{1,4},{2,5},{3,6},{4,7},{5,0},{6,1},{7,2},{8,11},{9,12},{10,... | collective-permute-start | bytes 368648 | tf_op jit(solution)/shard_map/cond/branch_0_fun/ppermute | solution.py:398
  73.2 3.5 %collective-permute-start.2 = (bf16[56,2,8,128]{3,2,1,0:T(8,128)(2,1)}, bf16[56,2,8,128]{3,2,1,0:T(8,128)(2,1)S(1)}, u32[]{:S(2)}, u32[]{:S(2)}) collective-permute-start(bf16[56,2,8,128]{3,2,1,0:T(8,128)(2,1)} %get-tuple-element.37), channel_id=1, source_target_pairs={{0,3},{1,4},{2,5},{3,6},{4,7},{5,0},{6,1},{7,2},{8,11},{9,12},{10,... | collective-permute-start | bytes 688136 | tf_op jit(solution)/shard_map/cond/branch_0_fun/ppermute | solution.py:398
  76.7 1.4 collective-permute-done.8.refs_10_
  78.1 2.8 collective-permute-start.3
  81.8 3.5 %collective-permute-start.4 = (bf16[56,2,8,128]{3,2,1,0:T(8,128)(2,1)}, bf16[56,2,8,128]{3,2,1,0:T(8,128)(2,1)S(1)}, u32[]{:S(2)}, u32[]{:S(2)}) collective-permute-start(bf16[56,2,8,128]{3,2,1,0:T(8,128)(2,1)} %get-tuple-element.39), channel_id=1, source_target_pairs={{0,5},{1,6},{2,7},{3,0},{4,1},{5,2},{6,3},{7,4},{8,13},{9,14},{10,... | collective-permute-start | bytes 688136 | tf_op jit(solution)/shard_map/cond/branch_0_fun/ppermute | solution.py:398
  85.3 3.2 collective-permute-start.5
  88.5 3.0 collective-permute-start.6
  92.4 13.2 %collective-permute-done.3.refs_4_ = bf16[56,2,8,128]{3,2,1,0:T(8,128)(2,1)S(1)} collective-permute-done((bf16[56,2,8,128]{3,2,1,0:T(8,128)(2,1)}, bf16[56,2,8,128]{3,2,1,0:T(8,128)(2,1)S(1)}, u32[]{:S(2)}, u32[]{:S(2)}) %collective-permute-start.3) | collective-permute-done | bytes 229408 | tf_op jit(solution)/shard_map/cond/branch_0_fun/ppermute | solution.py:398
  105.6 9.8 %collective-permute-done.6.refs_7_ = bf16[56,2,8,128]{3,2,1,0:T(8,128)(2,1)S(1)} collective-permute-done((bf16[56,2,8,128]{3,2,1,0:T(8,128)(2,1)}, bf16[56,2,8,128]{3,2,1,0:T(8,128)(2,1)S(1)}, u32[]{:S(2)}, u32[]{:S(2)}) %collective-permute-start.6) | collective-permute-done | bytes 229408 | tf_op jit(solution)/shard_map/cond/branch_0_fun/ppermute | solution.py:398
  116.1 6.6 %pick.5 = bf16[32,8,2,8,128]{4,3,2,1,0:T(8,128)(2,1)} custom-call(s32[4096]{0:T(1024)S(1)} %bitcast.37, bf16[56,2,8,128]{3,2,1,0:T(8,128)(2,1)} %get-tuple-element.34.refs_0_, bf16[56,2,8,128]{3,2,1,0:T(8,128)(2,1)} %copy-done.6, bf16[56,2,8,128]{3,2,1,0:T(8,128)(2,1)} %copy-done.7, bf16[56,2,8,128]{3,2,1,0:T(8,128)(2,1)} %copy-done.8, ...), custom_call_target="tpu_custom_call" | custom-call | tf_op jit(solution)/shard_map/cond/branch_0_fun/pick/pallas_call | solution.py:215
  122.7 12.1 %all-to-all-start.1 = ((bf16[32,8,2,8,128]{4,3,2,1,0:T(8,128)(2,1)}), bf16[32,8,2,8,128]{4,3,2,1,0:T(8,128)(2,1)S(1)}, u32[]{:S(2)}, u32[]{:S(2)}) async-start(bf16[32,8,2,8,128]{4,3,2,1,0:T(8,128)(2,1)} %pick.5), calls=%async_computation.1 | async-start | bytes 2097152 | tf_op jit(solution)/shard_map/cond/branch_0_fun/all_to_all | solution.py:337
  135.3 3.7 %collective-permute-start.15 = (bf16[42,2,8,128]{3,2,1,0:T(8,128)(2,1)S(1)}, bf16[42,2,8,128]{3,2,1,0:T(8,128)(2,1)S(1)}, u32[]{:S(2)}, u32[]{:S(2)}) collective-permute-start(bf16[42,2,8,128]{3,2,1,0:T(8,128)(2,1)S(1)} %copy-done.38), channel_id=1, source_target_pairs={{0,2},{1,3},{2,4},{3,5},{4,6},{5,7},{6,0},{7,1},{8,10},{9,11},{10,... | collective-permute-start | bytes 516104 | tf_op jit(solution)/shard_map/cond/branch_0_fun/ppermute | solution.py:398
  139.0 2.6 collective-permute-start.16
  142.2 3.8 %collective-permute-start.18 = (bf16[42,2,8,128]{3,2,1,0:T(8,128)(2,1)S(1)}, bf16[42,2,8,128]{3,2,1,0:T(8,128)(2,1)S(1)}, u32[]{:S(2)}, u32[]{:S(2)}) collective-permute-start(bf16[42,2,8,128]{3,2,1,0:T(8,128)(2,1)S(1)} %copy-done.35), channel_id=1, source_target_pairs={{0,5},{1,6},{2,7},{3,0},{4,1},{5,2},{6,3},{7,4},{8,13},{9,14},{10,... | collective-permute-start | bytes 516104 | tf_op jit(solution)/shard_map/cond/branch_0_fun/ppermute | solution.py:398
  146.0 2.6 collective-permute-start.19
  148.6 1.2 collective-permute-done.15.refs_18_
  149.8 1.2 collective-permute-start.20
  151.0 12.4 %collective-permute-done.16.refs_19_ = bf16[42,2,8,128]{3,2,1,0:T(8,128)(2,1)S(1)} collective-permute-done((bf16[42,2,8,128]{3,2,1,0:T(8,128)(2,1)S(1)}, bf16[42,2,8,128]{3,2,1,0:T(8,128)(2,1)S(1)}, u32[]{:S(2)}, u32[]{:S(2)}) %collective-permute-start.16) | collective-permute-done | bytes 172064 | tf_op jit(solution)/shard_map/cond/branch_0_fun/ppermute | solution.py:398
  163.4 2.7 collective-permute-done.17.refs_20_
  166.1 6.5 %collective-permute-done.19.refs_22_ = bf16[42,2,8,128]{3,2,1,0:T(8,128)(2,1)S(1)} collective-permute-done((bf16[42,2,8,128]{3,2,1,0:T(8,128)(2,1)S(1)}, bf16[42,2,8,128]{3,2,1,0:T(8,128)(2,1)S(1)}, u32[]{:S(2)}, u32[]{:S(2)}) %collective-permute-start.19) | collective-permute-done | bytes 172064 | tf_op jit(solution)/shard_map/cond/branch_0_fun/ppermute | solution.py:398
  172.6 1.7 collective-permute-done.20.refs_23_
  175.0 7.4 %pick.6 = bf16[32,12,2,8,128]{4,3,2,1,0:T(8,128)(2,1)} custom-call(s32[4096]{0:T(1024)S(1)} %bitcast.38, bf16[56,2,8,128]{3,2,1,0:T(8,128)(2,1)} %get-tuple-element.34.refs_0_, bf16[56,2,8,128]{3,2,1,0:T(8,128)(2,1)} %copy-done.6, bf16[56,2,8,128]{3,2,1,0:T(8,128)(2,1)} %copy-done.7, bf16[56,2,8,128]{3,2,1,0:T(8,128)(2,1)} %copy-done.8, ...), custom_call_target="tpu_custom_call" | custom-call | tf_op jit(solution)/shard_map/cond/branch_0_fun/pick/pallas_call | solution.py:215
  182.4 8.7 %all-to-all-start.2 = ((bf16[32,12,2,8,128]{4,3,2,1,0:T(8,128)(2,1)}), bf16[32,12,2,8,128]{4,3,2,1,0:T(8,128)(2,1)S(1)}, u32[]{:S(2)}, u32[]{:S(2)}) async-start(bf16[32,12,2,8,128]{4,3,2,1,0:T(8,128)(2,1)} %pick.6), calls=%async_computation.2 | async-start | bytes 3145728 | tf_op jit(solution)/shard_map/cond/branch_0_fun/all_to_all | solution.py:337
  191.1 6.5 %pick.4 = bf16[32,12,2,8,128]{4,3,2,1,0:T(8,128)(2,1)} custom-call(s32[4096]{0:T(1024)S(1)} %bitcast.39, bf16[56,2,8,128]{3,2,1,0:T(8,128)(2,1)} %get-tuple-element.34.refs_0_, bf16[56,2,8,128]{3,2,1,0:T(8,128)(2,1)} %copy-done.6, bf16[56,2,8,128]{3,2,1,0:T(8,128)(2,1)} %copy-done.7, bf16[56,2,8,128]{3,2,1,0:T(8,128)(2,1)} %copy-done.8, ...), custom_call_target="tpu_custom_call" | custom-call | tf_op jit(solution)/shard_map/cond/branch_0_fun/pick/pallas_call | solution.py:215
  197.7 16.1 %all-to-all-done.2.refs_2_ = bf16[32,12,2,8,128]{4,3,2,1,0:T(8,128)(2,1)S(1)} async-done(((bf16[32,12,2,8,128]{4,3,2,1,0:T(8,128)(2,1)}), bf16[32,12,2,8,128]{4,3,2,1,0:T(8,128)(2,1)S(1)}, u32[]{:S(2)}, u32[]{:S(2)}) %all-to-all-start.2) | async-done | bytes 1572896 | tf_op jit(solution)/shard_map/cond/branch_0_fun/all_to_all | solution.py:337
  213.8 27.1 %all_to_all.54.refs_0_ = bf16[32,12,2,8,128]{4,3,2,1,0:T(8,128)(2,1)S(1)} all-to-all(bf16[32,12,2,8,128]{4,3,2,1,0:T(8,128)(2,1)} %pick.4), channel_id=1, replica_groups=mesh['tm'=32,'space'=8] {'tm'}, dimensions={0} | all-to-all | bytes 3145728 | tf_op jit(solution)/shard_map/cond/branch_0_fun/all_to_all | solution.py:337
  240.9 10.1 %project.2 = (bf16[2048,512]{1,0:T(8,128)(2,1)}, bf16[32,16,1024]{2,1,0:T(8,128)(2,1)S(1)}) custom-call(s32[32]{0:T(128)S(1)} %copy-done.31, bf16[32,12,2,8,128]{4,3,2,1,0:T(8,128)(2,1)S(1)} %all_to_all.54.refs_0_, bf16[32,8,2,8,128]{4,3,2,1,0:T(8,128)(2,1)S(1)} %all-to-all-done.1.refs_1_, bf16[32,12,2,8,128]{4,3,2,1,0:T(8,128)(2,1)S(1)} %all-to-all-done.2.refs_2_, ...), custom_call_target="tpu_custom_call" | custom-call | tf_op jit(solution)/shard_map/cond/branch_0_fun/project/pallas_call | solution.py:284
  251.0 20.3 %all_to_all.55 = bf16[32,16,1024]{2,1,0:T(8,128)(2,1)S(1)} all-to-all(bf16[32,16,1024]{2,1,0:T(8,128)(2,1)S(1)} %get-tuple-element.60), channel_id=1, replica_groups=mesh['tm'=32,'space'=8] {'tm'}, dimensions={0} | all-to-all | bytes 2097152 | tf_op jit(solution)/shard_map/cond/branch_0_fun/all_to_all | solution.py:337
  272.3 3.7 %all-to-all-start.4 = ((f32[8,16,1024]{2,1,0:T(8,128)}), f32[8,16,1024]{2,1,0:T(8,128)S(1)}, u32[]{:S(2)}, u32[]{:S(2)}) async-start(f32[8,16,1024]{2,1,0:T(8,128)} %broadcast_in_dim.22), calls=%async_computation.4 | async-start | bytes 1048576 | tf_op jit(solution)/shard_map/cond/branch_0_fun/all_to_all | solution.py:337
  276.0 18.0 %all-to-all-done.4 = f32[8,16,1024]{2,1,0:T(8,128)S(1)} async-done(((f32[8,16,1024]{2,1,0:T(8,128)}), f32[8,16,1024]{2,1,0:T(8,128)S(1)}, u32[]{:S(2)}, u32[]{:S(2)}) %all-to-all-start.4) | async-done | bytes 524320 | tf_op jit(solution)/shard_map/cond/branch_0_fun/all_to_all | solution.py:337
  295.2 4.1 %all-to-all-start.5 = ((bf16[32,16,1152]{2,1,0:T(8,128)(2,1)}), bf16[32,16,1152]{2,1,0:T(8,128)(2,1)S(1)}, u32[]{:S(2)}, u32[]{:S(2)}) async-start(bf16[32,16,1152]{2,1,0:T(8,128)(2,1)} %broadcast_in_dim.23), calls=%async_computation.5 | async-start | bytes 2359296 | tf_op jit(solution)/shard_map/cond/branch_0_fun/all_to_all | solution.py:337
  299.3 18.4 %all-to-all-done.5 = bf16[32,16,1152]{2,1,0:T(8,128)(2,1)S(1)} async-done(((bf16[32,16,1152]{2,1,0:T(8,128)(2,1)}), bf16[32,16,1152]{2,1,0:T(8,128)(2,1)S(1)}, u32[]{:S(2)}, u32[]{:S(2)}) %all-to-all-start.5) | async-done | bytes 1179680 | tf_op jit(solution)/shard_map/cond/branch_0_fun/all_to_all | solution.py:337
  318.7 8.0 %rotate.2 = bf16[2048,1024]{1,0:T(8,128)(2,1)} custom-call(bf16[2048,512]{1,0:T(8,128)(2,1)S(1)} %copy-done, bf16[512,1024]{1,0:T(8,128)(2,1)S(1)} %bitcast.26, bf16[2048,1024]{1,0:T(8,128)(2,1)} %get-tuple-element.59.refs_4_.basis_ref, f32[1,1024]{1,0:T(1,128)S(1)} %bitcast.41), custom_call_target="tpu_custom_call" | custom-call | tf_op jit(solution)/shard_map/cond/branch_0_fun/rotate/pallas_call | solution.py:319
  (111 shorter events, 10.6 us)
Async XLA Ops:
  2.1 15.5 %all-to-all-start.11 = ((s32[32,1,128]{2,1,0:T(1,128)}), s32[32,1,128]{2,1,0:T(1,128)S(1)}, u32[]{:S(2)}, u32[]{:S(2)}) async-start(s32[32,1,128]{2,1,0:T(1,128)} %broadcast_in_dim.34), calls=%async_computation.11 | async-start | bytes 32768 | tf_op jit(solution)/shard_map/all_to_all | solution.py:337
  19.9 15.1 %all-to-all-start.12 = ((s32[8,8,128]{2,1,0:T(8,128)}), s32[8,8,128]{2,1,0:T(8,128)S(1)}, u32[]{:S(2)}, u32[]{:S(2)}) async-start(s32[8,8,128]{2,1,0:T(8,128)} %get-tuple-element.77), calls=%async_computation.12 | async-start | bytes 65536 | tf_op jit(solution)/shard_map/all_to_all | solution.py:337
  36.3 138.0 %copy-start.27 = (s32[32,128]{1,0:T(8,128)}, s32[32,128]{1,0:T(8,128)S(1)}, u32[]{:S(2)}) copy-start(s32[32,128]{1,0:T(8,128)S(1)} %get-tuple-element.31) | copy-start | bytes 49156 | tf_op jit(solution)/shard_map/cond
  44.8 22.7 %copy-start.41 = (bf16[30,2,8,128]{3,2,1,0:T(8,128)(2,1)S(1)}, bf16[30,2,8,128]{3,2,1,0:T(8,128)(2,1)}, u32[]{:S(2)}) copy-start(bf16[30,2,8,128]{3,2,1,0:T(8,128)(2,1)} %get-tuple-element.44) | copy-start | bytes 368644 | tf_op jit(solution)/shard_map/cond
  44.8 24.8 %copy-start.40 = (bf16[30,2,8,128]{3,2,1,0:T(8,128)(2,1)S(1)}, bf16[30,2,8,128]{3,2,1,0:T(8,128)(2,1)}, u32[]{:S(2)}) copy-start(bf16[30,2,8,128]{3,2,1,0:T(8,128)(2,1)} %get-tuple-element.45) | copy-start | bytes 368644 | tf_op jit(solution)/shard_map/cond
  44.9 12.6 %collective-permute-start.10 = (bf16[30,2,8,128]{3,2,1,0:T(8,128)(2,1)}, bf16[30,2,8,128]{3,2,1,0:T(8,128)(2,1)S(1)}, u32[]{:S(2)}, u32[]{:S(2)}) collective-permute-start(bf16[30,2,8,128]{3,2,1,0:T(8,128)(2,1)} %get-tuple-element.46), channel_id=1, source_target_pairs={{0,4},{1,5},{2,6},{3,7},{4,0},{5,1},{6,2},{7,3},{8,12},{9,13},{10,... | collective-permute-start | bytes 368648 | tf_op jit(solution)/shard_map/cond/branch_0_fun/ppermute | solution.py:398
  45.5 13.2 %collective-permute-start.11 = (bf16[30,2,8,128]{3,2,1,0:T(8,128)(2,1)}, bf16[30,2,8,128]{3,2,1,0:T(8,128)(2,1)S(1)}, u32[]{:S(2)}, u32[]{:S(2)}) collective-permute-start(bf16[30,2,8,128]{3,2,1,0:T(8,128)(2,1)} %get-tuple-element.47), channel_id=1, source_target_pairs={{0,5},{1,6},{2,7},{3,0},{4,1},{5,2},{6,3},{7,4},{8,13},{9,14},{10,... | collective-permute-start | bytes 368648 | tf_op jit(solution)/shard_map/cond/branch_0_fun/ppermute | solution.py:398
  49.4 18.1 %collective-permute-start.12 = (bf16[30,2,8,128]{3,2,1,0:T(8,128)(2,1)}, bf16[30,2,8,128]{3,2,1,0:T(8,128)(2,1)S(1)}, u32[]{:S(2)}, u32[]{:S(2)}) collective-permute-start(bf16[30,2,8,128]{3,2,1,0:T(8,128)(2,1)} %get-tuple-element.48), channel_id=1, source_target_pairs={{0,6},{1,7},{2,0},{3,1},{4,2},{5,3},{6,4},{7,5},{8,14},{9,15},{10,... | collective-permute-start | bytes 368648 | tf_op jit(solution)/shard_map/cond/branch_0_fun/ppermute | solution.py:398
  50.6 19.0 %collective-permute-start.13 = (bf16[30,2,8,128]{3,2,1,0:T(8,128)(2,1)}, bf16[30,2,8,128]{3,2,1,0:T(8,128)(2,1)S(1)}, u32[]{:S(2)}, u32[]{:S(2)}) collective-permute-start(bf16[30,2,8,128]{3,2,1,0:T(8,128)(2,1)} %get-tuple-element.49), channel_id=1, source_target_pairs={{0,7},{1,0},{2,1},{3,2},{4,3},{5,4},{6,5},{7,6},{8,15},{9,8},{10,9... | collective-permute-start | bytes 368648 | tf_op jit(solution)/shard_map/cond/branch_0_fun/ppermute | solution.py:398
  56.3 29.0 %collective-permute-start = (bf16[56,2,8,128]{3,2,1,0:T(8,128)(2,1)}, bf16[56,2,8,128]{3,2,1,0:T(8,128)(2,1)S(1)}, u32[]{:S(2)}, u32[]{:S(2)}) collective-permute-start(bf16[56,2,8,128]{3,2,1,0:T(8,128)(2,1)} %get-tuple-element.35), channel_id=1, source_target_pairs={{0,1},{1,2},{2,3},{3,4},{4,5},{5,6},{6,7},{7,0},{8,9},{9,10},{10,1... | collective-permute-start | bytes 688136 | tf_op jit(solution)/shard_map/cond/branch_0_fun/ppermute | solution.py:398
  57.5 57.9 %copy-start.13 = (bf16[30,2,8,128]{3,2,1,0:T(8,128)(2,1)}, bf16[30,2,8,128]{3,2,1,0:T(8,128)(2,1)S(1)}, u32[]{:S(2)}) copy-start(bf16[30,2,8,128]{3,2,1,0:T(8,128)(2,1)S(1)} %collective-permute-done.10.refs_12_) | copy-start | bytes 368644 | tf_op jit(solution)/shard_map/cond
  57.5 31.0 %collective-permute-start.1 = (bf16[56,2,8,128]{3,2,1,0:T(8,128)(2,1)}, bf16[56,2,8,128]{3,2,1,0:T(8,128)(2,1)S(1)}, u32[]{:S(2)}, u32[]{:S(2)}) collective-permute-start(bf16[56,2,8,128]{3,2,1,0:T(8,128)(2,1)} %get-tuple-element.36), channel_id=1, source_target_pairs={{0,2},{1,3},{2,4},{3,5},{4,6},{5,7},{6,0},{7,1},{8,10},{9,11},{10,... | collective-permute-start | bytes 688136 | tf_op jit(solution)/shard_map/cond/branch_0_fun/ppermute | solution.py:398
  58.7 56.7 %copy-start.14 = (bf16[30,2,8,128]{3,2,1,0:T(8,128)(2,1)}, bf16[30,2,8,128]{3,2,1,0:T(8,128)(2,1)S(1)}, u32[]{:S(2)}) copy-start(bf16[30,2,8,128]{3,2,1,0:T(8,128)(2,1)S(1)} %collective-permute-done.11.refs_13_) | copy-start | bytes 368644 | tf_op jit(solution)/shard_map/cond
  58.7 14.5 %collective-permute-start.7 = (bf16[30,2,8,128]{3,2,1,0:T(8,128)(2,1)S(1)}, bf16[30,2,8,128]{3,2,1,0:T(8,128)(2,1)S(1)}, u32[]{:S(2)}, u32[]{:S(2)}) collective-permute-start(bf16[30,2,8,128]{3,2,1,0:T(8,128)(2,1)S(1)} %copy-done.42), channel_id=1, source_target_pairs={{0,1},{1,2},{2,3},{3,4},{4,5},{5,6},{6,7},{7,0},{8,9},{9,10},{10,1... | collective-permute-start | bytes 368648 | tf_op jit(solution)/shard_map/cond/branch_0_fun/ppermute | solution.py:398
  67.5 47.9 %copy-start.15 = (bf16[30,2,8,128]{3,2,1,0:T(8,128)(2,1)}, bf16[30,2,8,128]{3,2,1,0:T(8,128)(2,1)S(1)}, u32[]{:S(2)}) copy-start(bf16[30,2,8,128]{3,2,1,0:T(8,128)(2,1)S(1)} %collective-permute-done.12.refs_14_) | copy-start | bytes 368644 | tf_op jit(solution)/shard_map/cond
  67.5 10.6 %collective-permute-start.8 = (bf16[30,2,8,128]{3,2,1,0:T(8,128)(2,1)S(1)}, bf16[30,2,8,128]{3,2,1,0:T(8,128)(2,1)S(1)}, u32[]{:S(2)}, u32[]{:S(2)}) collective-permute-start(bf16[30,2,8,128]{3,2,1,0:T(8,128)(2,1)S(1)} %copy-done.41), channel_id=1, source_target_pairs={{0,2},{1,3},{2,4},{3,5},{4,6},{5,7},{6,0},{7,1},{8,10},{9,11},{10,... | collective-permute-start | bytes 368648 | tf_op jit(solution)/shard_map/cond/branch_0_fun/ppermute | solution.py:398
  69.6 45.8 %copy-start.16 = (bf16[30,2,8,128]{3,2,1,0:T(8,128)(2,1)}, bf16[30,2,8,128]{3,2,1,0:T(8,128)(2,1)S(1)}, u32[]{:S(2)}) copy-start(bf16[30,2,8,128]{3,2,1,0:T(8,128)(2,1)S(1)} %collective-permute-done.13.refs_15_) | copy-start | bytes 368644 | tf_op jit(solution)/shard_map/cond
  69.6 12.2 %collective-permute-start.9 = (bf16[30,2,8,128]{3,2,1,0:T(8,128)(2,1)S(1)}, bf16[30,2,8,128]{3,2,1,0:T(8,128)(2,1)S(1)}, u32[]{:S(2)}, u32[]{:S(2)}) collective-permute-start(bf16[30,2,8,128]{3,2,1,0:T(8,128)(2,1)S(1)} %copy-done.40), channel_id=1, source_target_pairs={{0,3},{1,4},{2,5},{3,6},{4,7},{5,0},{6,1},{7,2},{8,11},{9,12},{10,... | collective-permute-start | bytes 368648 | tf_op jit(solution)/shard_map/cond/branch_0_fun/ppermute | solution.py:398
  73.2 42.3 %copy-start.17 = (bf16[30,2,8,128]{3,2,1,0:T(8,128)(2,1)}, bf16[30,2,8,128]{3,2,1,0:T(8,128)(2,1)S(1)}, u32[]{:S(2)}) copy-start(bf16[30,2,8,128]{3,2,1,0:T(8,128)(2,1)S(1)} %collective-permute-done.7.refs_9_) | copy-start | bytes 368644 | tf_op jit(solution)/shard_map/cond
  73.2 19.2 %collective-permute-start.2 = (bf16[56,2,8,128]{3,2,1,0:T(8,128)(2,1)}, bf16[56,2,8,128]{3,2,1,0:T(8,128)(2,1)S(1)}, u32[]{:S(2)}, u32[]{:S(2)}) collective-permute-start(bf16[56,2,8,128]{3,2,1,0:T(8,128)(2,1)} %get-tuple-element.37), channel_id=1, source_target_pairs={{0,3},{1,4},{2,5},{3,6},{4,7},{5,0},{6,1},{7,2},{8,11},{9,12},{10,... | collective-permute-start | bytes 688136 | tf_op jit(solution)/shard_map/cond/branch_0_fun/ppermute | solution.py:398
  78.1 37.3 %copy-start.18 = (bf16[30,2,8,128]{3,2,1,0:T(8,128)(2,1)}, bf16[30,2,8,128]{3,2,1,0:T(8,128)(2,1)S(1)}, u32[]{:S(2)}) copy-start(bf16[30,2,8,128]{3,2,1,0:T(8,128)(2,1)S(1)} %collective-permute-done.8.refs_10_) | copy-start | bytes 368644 | tf_op jit(solution)/shard_map/cond
  78.1 27.5 %collective-permute-start.3 = (bf16[56,2,8,128]{3,2,1,0:T(8,128)(2,1)}, bf16[56,2,8,128]{3,2,1,0:T(8,128)(2,1)S(1)}, u32[]{:S(2)}, u32[]{:S(2)}) collective-permute-start(bf16[56,2,8,128]{3,2,1,0:T(8,128)(2,1)} %get-tuple-element.38), channel_id=1, source_target_pairs={{0,4},{1,5},{2,6},{3,7},{4,0},{5,1},{6,2},{7,3},{8,12},{9,13},{10,... | collective-permute-start | bytes 688136 | tf_op jit(solution)/shard_map/cond/branch_0_fun/ppermute | solution.py:398
  81.8 33.7 %copy-start.19 = (bf16[30,2,8,128]{3,2,1,0:T(8,128)(2,1)}, bf16[30,2,8,128]{3,2,1,0:T(8,128)(2,1)S(1)}, u32[]{:S(2)}) copy-start(bf16[30,2,8,128]{3,2,1,0:T(8,128)(2,1)S(1)} %collective-permute-done.9.refs_11_) | copy-start | bytes 368644 | tf_op jit(solution)/shard_map/cond
  81.8 23.8 %collective-permute-start.4 = (bf16[56,2,8,128]{3,2,1,0:T(8,128)(2,1)}, bf16[56,2,8,128]{3,2,1,0:T(8,128)(2,1)S(1)}, u32[]{:S(2)}, u32[]{:S(2)}) collective-permute-start(bf16[56,2,8,128]{3,2,1,0:T(8,128)(2,1)} %get-tuple-element.39), channel_id=1, source_target_pairs={{0,5},{1,6},{2,7},{3,0},{4,1},{5,2},{6,3},{7,4},{8,13},{9,14},{10,... | collective-permute-start | bytes 688136 | tf_op jit(solution)/shard_map/cond/branch_0_fun/ppermute | solution.py:398
  85.3 30.2 %copy-start.6 = (bf16[56,2,8,128]{3,2,1,0:T(8,128)(2,1)}, bf16[56,2,8,128]{3,2,1,0:T(8,128)(2,1)S(1)}, u32[]{:S(2)}) copy-start(bf16[56,2,8,128]{3,2,1,0:T(8,128)(2,1)S(1)} %collective-permute-done.refs_1_) | copy-start | bytes 688132 | tf_op jit(solution)/shard_map/cond
  85.3 20.3 %collective-permute-start.5 = (bf16[56,2,8,128]{3,2,1,0:T(8,128)(2,1)}, bf16[56,2,8,128]{3,2,1,0:T(8,128)(2,1)S(1)}, u32[]{:S(2)}, u32[]{:S(2)}) collective-permute-start(bf16[56,2,8,128]{3,2,1,0:T(8,128)(2,1)} %get-tuple-element.40), channel_id=1, source_target_pairs={{0,6},{1,7},{2,0},{3,1},{4,2},{5,3},{6,4},{7,5},{8,14},{9,15},{10,... | collective-permute-start | bytes 688136 | tf_op jit(solution)/shard_map/cond/branch_0_fun/ppermute | solution.py:398
  88.5 26.9 %copy-start.7 = (bf16[56,2,8,128]{3,2,1,0:T(8,128)(2,1)}, bf16[56,2,8,128]{3,2,1,0:T(8,128)(2,1)S(1)}, u32[]{:S(2)}) copy-start(bf16[56,2,8,128]{3,2,1,0:T(8,128)(2,1)S(1)} %collective-permute-done.1.refs_2_) | copy-start | bytes 688132 | tf_op jit(solution)/shard_map/cond
  88.5 26.9 %collective-permute-start.6 = (bf16[56,2,8,128]{3,2,1,0:T(8,128)(2,1)}, bf16[56,2,8,128]{3,2,1,0:T(8,128)(2,1)S(1)}, u32[]{:S(2)}, u32[]{:S(2)}) collective-permute-start(bf16[56,2,8,128]{3,2,1,0:T(8,128)(2,1)} %get-tuple-element.41), channel_id=1, source_target_pairs={{0,7},{1,0},{2,1},{3,2},{4,3},{5,4},{6,5},{7,6},{8,15},{9,8},{10,9... | collective-permute-start | bytes 688136 | tf_op jit(solution)/shard_map/cond/branch_0_fun/ppermute | solution.py:398
  92.4 23.1 %copy-start.8 = (bf16[56,2,8,128]{3,2,1,0:T(8,128)(2,1)}, bf16[56,2,8,128]{3,2,1,0:T(8,128)(2,1)S(1)}, u32[]{:S(2)}) copy-start(bf16[56,2,8,128]{3,2,1,0:T(8,128)(2,1)S(1)} %collective-permute-done.2.refs_3_) | copy-start | bytes 688132 | tf_op jit(solution)/shard_map/cond
  122.7 19.5 %copy-start.35 = (bf16[42,2,8,128]{3,2,1,0:T(8,128)(2,1)S(1)}, bf16[42,2,8,128]{3,2,1,0:T(8,128)(2,1)}, u32[]{:S(2)}) copy-start(bf16[42,2,8,128]{3,2,1,0:T(8,128)(2,1)} %get-tuple-element.55) | copy-start | bytes 516100 | tf_op jit(solution)/shard_map/cond
  122.7 23.3 %copy-start.34 = (bf16[42,2,8,128]{3,2,1,0:T(8,128)(2,1)S(1)}, bf16[42,2,8,128]{3,2,1,0:T(8,128)(2,1)}, u32[]{:S(2)}) copy-start(bf16[42,2,8,128]{3,2,1,0:T(8,128)(2,1)} %get-tuple-element.56) | copy-start | bytes 516100 | tf_op jit(solution)/shard_map/cond
  122.7 27.1 %copy-start.33 = (bf16[42,2,8,128]{3,2,1,0:T(8,128)(2,1)S(1)}, bf16[42,2,8,128]{3,2,1,0:T(8,128)(2,1)}, u32[]{:S(2)}) copy-start(bf16[42,2,8,128]{3,2,1,0:T(8,128)(2,1)} %get-tuple-element.57) | copy-start | bytes 516100 | tf_op jit(solution)/shard_map/cond
  122.7 59.7 %all-to-all-start.1 = ((bf16[32,8,2,8,128]{4,3,2,1,0:T(8,128)(2,1)}), bf16[32,8,2,8,128]{4,3,2,1,0:T(8,128)(2,1)S(1)}, u32[]{:S(2)}, u32[]{:S(2)}) async-start(bf16[32,8,2,8,128]{4,3,2,1,0:T(8,128)(2,1)} %pick.5), calls=%async_computation.1 | async-start | bytes 2097152 | tf_op jit(solution)/shard_map/cond/branch_0_fun/all_to_all | solution.py:337
  134.8 11.2 %collective-permute-start.14 = (bf16[42,2,8,128]{3,2,1,0:T(8,128)(2,1)S(1)}, bf16[42,2,8,128]{3,2,1,0:T(8,128)(2,1)S(1)}, u32[]{:S(2)}, u32[]{:S(2)}) collective-permute-start(bf16[42,2,8,128]{3,2,1,0:T(8,128)(2,1)S(1)} %copy-done.39), channel_id=1, source_target_pairs={{0,1},{1,2},{2,3},{3,4},{4,5},{5,6},{6,7},{7,0},{8,9},{9,10},{10,1... | collective-permute-start | bytes 516104 | tf_op jit(solution)/shard_map/cond/branch_0_fun/ppermute | solution.py:398
  135.3 14.5 %collective-permute-start.15 = (bf16[42,2,8,128]{3,2,1,0:T(8,128)(2,1)S(1)}, bf16[42,2,8,128]{3,2,1,0:T(8,128)(2,1)S(1)}, u32[]{:S(2)}, u32[]{:S(2)}) collective-permute-start(bf16[42,2,8,128]{3,2,1,0:T(8,128)(2,1)S(1)} %copy-done.38), channel_id=1, source_target_pairs={{0,2},{1,3},{2,4},{3,5},{4,6},{5,7},{6,0},{7,1},{8,10},{9,11},{10,... | collective-permute-start | bytes 516104 | tf_op jit(solution)/shard_map/cond/branch_0_fun/ppermute | solution.py:398
  139.0 24.4 %collective-permute-start.16 = (bf16[42,2,8,128]{3,2,1,0:T(8,128)(2,1)S(1)}, bf16[42,2,8,128]{3,2,1,0:T(8,128)(2,1)S(1)}, u32[]{:S(2)}, u32[]{:S(2)}) collective-permute-start(bf16[42,2,8,128]{3,2,1,0:T(8,128)(2,1)S(1)} %copy-done.37), channel_id=1, source_target_pairs={{0,3},{1,4},{2,5},{3,6},{4,7},{5,0},{6,1},{7,2},{8,11},{9,12},{10,... | collective-permute-start | bytes 516104 | tf_op jit(solution)/shard_map/cond/branch_0_fun/ppermute | solution.py:398
  141.7 24.4 %collective-permute-start.17 = (bf16[42,2,8,128]{3,2,1,0:T(8,128)(2,1)S(1)}, bf16[42,2,8,128]{3,2,1,0:T(8,128)(2,1)S(1)}, u32[]{:S(2)}, u32[]{:S(2)}) collective-permute-start(bf16[42,2,8,128]{3,2,1,0:T(8,128)(2,1)S(1)} %copy-done.36), channel_id=1, source_target_pairs={{0,4},{1,5},{2,6},{3,7},{4,0},{5,1},{6,2},{7,3},{8,12},{9,13},{10,... | collective-permute-start | bytes 516104 | tf_op jit(solution)/shard_map/cond/branch_0_fun/ppermute | solution.py:398
  142.2 23.9 %collective-permute-start.18 = (bf16[42,2,8,128]{3,2,1,0:T(8,128)(2,1)S(1)}, bf16[42,2,8,128]{3,2,1,0:T(8,128)(2,1)S(1)}, u32[]{:S(2)}, u32[]{:S(2)}) collective-permute-start(bf16[42,2,8,128]{3,2,1,0:T(8,128)(2,1)S(1)} %copy-done.35), channel_id=1, source_target_pairs={{0,5},{1,6},{2,7},{3,0},{4,1},{5,2},{6,3},{7,4},{8,13},{9,14},{10,... | collective-permute-start | bytes 516104 | tf_op jit(solution)/shard_map/cond/branch_0_fun/ppermute | solution.py:398
  146.0 28.3 %copy-start.20 = (bf16[42,2,8,128]{3,2,1,0:T(8,128)(2,1)}, bf16[42,2,8,128]{3,2,1,0:T(8,128)(2,1)S(1)}, u32[]{:S(2)}) copy-start(bf16[42,2,8,128]{3,2,1,0:T(8,128)(2,1)S(1)} %collective-permute-done.14.refs_17_) | copy-start | bytes 516100 | tf_op jit(solution)/shard_map/cond
  146.0 26.6 %collective-permute-start.19 = (bf16[42,2,8,128]{3,2,1,0:T(8,128)(2,1)S(1)}, bf16[42,2,8,128]{3,2,1,0:T(8,128)(2,1)S(1)}, u32[]{:S(2)}, u32[]{:S(2)}) collective-permute-start(bf16[42,2,8,128]{3,2,1,0:T(8,128)(2,1)S(1)} %copy-done.34), channel_id=1, source_target_pairs={{0,6},{1,7},{2,0},{3,1},{4,2},{5,3},{6,4},{7,5},{8,14},{9,15},{10,... | collective-permute-start | bytes 516104 | tf_op jit(solution)/shard_map/cond/branch_0_fun/ppermute | solution.py:398
  149.8 24.5 %copy-start.21 = (bf16[42,2,8,128]{3,2,1,0:T(8,128)(2,1)}, bf16[42,2,8,128]{3,2,1,0:T(8,128)(2,1)S(1)}, u32[]{:S(2)}) copy-start(bf16[42,2,8,128]{3,2,1,0:T(8,128)(2,1)S(1)} %collective-permute-done.15.refs_18_) | copy-start | bytes 516100 | tf_op jit(solution)/shard_map/cond
  149.8 24.5 %collective-permute-start.20 = (bf16[42,2,8,128]{3,2,1,0:T(8,128)(2,1)S(1)}, bf16[42,2,8,128]{3,2,1,0:T(8,128)(2,1)S(1)}, u32[]{:S(2)}, u32[]{:S(2)}) collective-permute-start(bf16[42,2,8,128]{3,2,1,0:T(8,128)(2,1)S(1)} %copy-done.33), channel_id=1, source_target_pairs={{0,7},{1,0},{2,1},{3,2},{4,3},{5,4},{6,5},{7,6},{8,15},{9,8},{10,9... | collective-permute-start | bytes 516104 | tf_op jit(solution)/shard_map/cond/branch_0_fun/ppermute | solution.py:398
  182.4 31.3 %all-to-all-start.2 = ((bf16[32,12,2,8,128]{4,3,2,1,0:T(8,128)(2,1)}), bf16[32,12,2,8,128]{4,3,2,1,0:T(8,128)(2,1)S(1)}, u32[]{:S(2)}, u32[]{:S(2)}) async-start(bf16[32,12,2,8,128]{4,3,2,1,0:T(8,128)(2,1)} %pick.6), calls=%async_computation.2 | async-start | bytes 3145728 | tf_op jit(solution)/shard_map/cond/branch_0_fun/all_to_all | solution.py:337
  197.6 43.2 %copy-start.4 = (bf16[32,64,128]{2,1,0:T(8,128)(2,1)S(1)}, bf16[32,64,128]{2,1,0:T(8,128)(2,1)}, u32[]{:S(2)}) copy-start(bf16[32,64,128]{2,1,0:T(8,128)(2,1)} %get-tuple-element.58.refs_3_) | copy-start | bytes 1572868 | tf_op jit(solution)/shard_map/cond
  197.6 43.2 %copy-start.31 = (s32[32]{0:T(128)S(1)}, s32[32]{0:T(128)}, u32[]{:S(2)}) copy-start(s32[32]{0:T(128)} %get-tuple-element.30.counts_ref) | copy-start | bytes 388 | tf_op jit(solution)/shard_map/cond
  272.3 21.7 %all-to-all-start.4 = ((f32[8,16,1024]{2,1,0:T(8,128)}), f32[8,16,1024]{2,1,0:T(8,128)S(1)}, u32[]{:S(2)}, u32[]{:S(2)}) async-start(f32[8,16,1024]{2,1,0:T(8,128)} %broadcast_in_dim.22), calls=%async_computation.4 | async-start | bytes 1048576 | tf_op jit(solution)/shard_map/cond/branch_0_fun/all_to_all | solution.py:337
  295.2 22.5 %all-to-all-start.5 = ((bf16[32,16,1152]{2,1,0:T(8,128)(2,1)}), bf16[32,16,1152]{2,1,0:T(8,128)(2,1)S(1)}, u32[]{:S(2)}, u32[]{:S(2)}) async-start(bf16[32,16,1152]{2,1,0:T(8,128)(2,1)} %broadcast_in_dim.23), calls=%async_computation.5 | async-start | bytes 2359296 | tf_op jit(solution)/shard_map/cond/branch_0_fun/all_to_all | solution.py:337
  299.3 19.5 %copy-start = (bf16[2048,512]{1,0:T(8,128)(2,1)S(1)}, bf16[2048,512]{1,0:T(8,128)(2,1)}, u32[]{:S(2)}) copy-start(bf16[2048,512]{1,0:T(8,128)(2,1)} %get-tuple-element.62.remapped_ref) | copy-start | bytes 6291460 | tf_op jit(solution)/shard_map/cond
  (17 other events, 177.0 us)
